TPU v7x, 32 devices: a whole 2x2x4 slice. The times are simulated.
32 devices in a mesh: groups: 2 (over y), row: 16 (over z, x, core).
Axes of the slice: x: 2, y: 2, z: 4, core: 2. Of those that a mesh axis runs over, the one named last changes fastest.
Arguments:
- walkers: bfloat16 [64, 1024, 256], P('groups', 'row'), parts along dimension 0, may hold values from -6 to 6
- cholesky: bfloat16 [1024, 1024, 1024], P('groups', 'row'), parts along dimension 0, may hold values from -0.03125 to 0.03125
- slab_index: int32 [4, 64], P('groups'), parts along dimension 0, may hold values from 0 to 511
- fields: bfloat16 [2, 64, 64], P(None, ('groups', 'row')), parts along dimension 1, may hold values from -5 to 5
- counts: int32 [32], P('groups'), parts along dimension 0, may hold values from 1 to 2, as said below
- sources: int32 [4, 32], P('groups'), parts along dimension 0, may hold values from 0 to 31, as said below
Outputs:
- branched: bfloat16 [64, 1024, 256], P('groups', 'row'), parts along dimension 0
There are 2 independent parts, one for each index of `groups`. A program takes and returns all parts, laid end to end along the dimension named above; each array names one. Nothing has to cross between parts.
Inputs may be any that keep to these rules, and one draw needn't show every extreme that they name: counts[d] walkers live in the first counts[d] of the 2 slots d * 2 ... ; some index has all 2 live. For a living slot j, sources[s, j] is a living slot; for any other slot it is j itself.
All inputs are finite; a program needn't handle non-finite values.
Results may differ from a plain program's by a relative error of at most 0.0086.
Values may be sent and summed in bfloat16 or wider, within the bound.
No kernel may reach another device: no remote copies, remote signals or barrier semaphores. Data moves between devices by JAX's collectives and lax.ppermute only.
A program may use at most 192 MiB of HBM per device.

v0:
```python
import jax
import jax.numpy as jnp
from jax import lax
from jax.sharding import PartitionSpec as P

SLAB = 64
STEPS = 2


def taylor_step(potential, initial):
    summed = initial.astype(jnp.float32)
    term_now = initial
    for degree in range(1, 5):
        product = jnp.dot(potential, term_now, preferred_element_type=jnp.float32) / degree
        summed = summed + product
        term_now = product.astype(jnp.bfloat16)
    return summed.astype(jnp.bfloat16)


def on_device(walkers, cholesky, slab_index, fields, counts, sources):
    local_rows = walkers.shape[1]
    orbitals = cholesky.shape[2]
    per_device = fields.shape[1]
    row_devices = lax.axis_size("row")
    slot_count = per_device * row_devices
    my_index = lax.axis_index("row")
    all_fields = lax.all_gather(fields, "row", axis=1, tiled=True)
    slot_ids = jnp.arange(slot_count, dtype=jnp.int32)
    owners = slot_ids // per_device
    within = slot_ids % per_device
    owner_counts = jnp.take(counts, owners)
    living = within < owner_counts
    before = jnp.cumsum(counts) - counts
    live_total = jnp.sum(counts)
    owner_before = jnp.take(before, owners)
    ordinal = jnp.where(
        living,
        owner_before + within,
        live_total + owners * per_device - owner_before + within - owner_counts,
    )
    position = ordinal % row_devices * per_device + ordinal // row_devices
    placed = jnp.zeros((slot_count,), jnp.int32).at[position].set(slot_ids)
    busy_slots = (live_total - my_index + row_devices - 1) // row_devices
    current = walkers
    for step_number in range(STEPS):
        chosen = jnp.take(cholesky, slab_index[step_number], axis=0).reshape(
            SLAB, local_rows * orbitals
        )
        ordered_fields = jnp.take(all_fields[step_number], placed, axis=0)
        potential_rows = (
            jnp.dot(ordered_fields, chosen, preferred_element_type=jnp.float32)
            .astype(jnp.bfloat16)
            .reshape(slot_count, local_rows, orbitals)
        )
        ordered = jnp.take(current, placed, axis=0)
        potentials, columns = (
            lax.all_to_all(potential_rows, "row", split_axis=0, concat_axis=1, tiled=True),
            lax.all_to_all(ordered, "row", split_axis=0, concat_axis=1, tiled=True),
        )

        def advance(walker, buffer):
            matrix = lax.dynamic_index_in_dim(potentials, walker, 0, keepdims=False)
            initial = lax.dynamic_index_in_dim(columns, walker, 0, keepdims=False)
            return lax.dynamic_update_index_in_dim(buffer, taylor_step(matrix, initial), walker, 0)

        advanced = lax.fori_loop(0, busy_slots, advance, jnp.zeros_like(columns))
        returned = lax.all_to_all(advanced, "row", split_axis=1, concat_axis=0, tiled=True)
        current = jnp.take(returned, jnp.take(position, sources[step_number]), axis=0)
    return current


def solution(mesh):
    in_specs = (
        P("groups", "row", None),
        P("groups", "row", None),
        P("groups", None),
        P(None, ("groups", "row"), None),
        P("groups"),
        P("groups", None),
    )
    out_specs = P("groups", "row", None)
    return jax.shard_map(
        on_device, mesh=mesh, in_specs=in_specs, out_specs=out_specs, check_vma=False
    )
```

profile of v0, /device:TPU:9, one launch (start us, length us, event | category | flops | bytes accessed | tf_op | source)
XLA Modules:
  0.0 391.6 jit_solution(3536680181950253770)
XLA Ops:
  0.0 0.8 copy.22
  0.9 0.1 reduce
  1.0 1.4 fusion.98
  2.3 1.4 gather_fusion
  3.7 0.7 gather_fusion.1
  4.4 0.6 compare_select_fusion.8
  5.1 0.7 scatter_custom_fusion
  5.8 0.6 gather_fusion.2
  6.4 1.1 broadcast_select_fusion.3
  7.6 6.5 %all-to-all-start = ((bf16[32,64,256]{2,1,0:T(8,128)(2,1)}), bf16[32,64,256]{2,1,0:T(8,128)(2,1)S(1)}, u32[]{:S(2)}, u32[]{:S(2)}) async-start(bf16[32,64,256]{2,1,0:T(8,128)(2,1)} %broadcast_select_fusion.3), calls=%async_computation | async-start | bytes 2097152 | tf_op jit(solution)/shard_map/all_to_all | solution.py:58
  14.2 7.6 %gather_fusion.4 = bf16[64,64,1024]{2,1,0:T(8,128)(2,1)} fusion(bf16[512,64,1024]{2,1,0:T(8,128)(2,1)} %param.21, s32[1024]{0:T(1024)S(1)} %pad_clamp_fusion.3), kind=kCustom, calls=%fused_computation.2.clone | custom fusion | bytes 16777472 | tf_op jit(solution)/shard_map/jit(_take)/gather | solution.py:46
  21.7 7.7 %gather_fusion.9 = bf16[64,64,1024]{2,1,0:T(8,128)(2,1)} fusion(bf16[512,64,1024]{2,1,0:T(8,128)(2,1)} %param.21, s32[1024]{0:T(1024)S(1)} %pad_clamp_fusion.1), kind=kCustom, calls=%fused_computation.7.clone | custom fusion | bytes 16777472 | tf_op jit(solution)/shard_map/jit(_take)/gather | solution.py:46
  29.4 11.8 %broadcast_select_fusion = (bf16[64,64,1024]{2,1,0:T(8,128)(2,1)}, bf16[64,64,1024]{2,1,0:T(8,128)(2,1)}) fusion(bf16[64,64,1024]{2,1,0:T(8,128)(2,1)} %gather_fusion.9, pred[64]{0:T(512)(128)(4,1)S(1)} %get-tuple-element.90, bf16[64,64,1024]{2,1,0:T(8,128)(2,1)} %gather_fusion.4, pred[64]{0:T(512)(128)(4,1)S(1)} %get-tuple-element.104), kind=kLoop, calls=%fused_computation.71 | loop fusion | flops 8388608 | bytes 33554560 | tf_op jit(solution)/shard_map/jit(_take)/select_n | solution.py:46
  41.2 11.9 %copy.38 = bf16[8,8,64,1024]{3,1,2,0:T(8,128)(2,1)} copy(bf16[8,8,64,1024]{3,2,1,0:T(8,128)(2,1)} %bitcast.149) | data formatting | bytes 16777216
  53.2 19.0 %all_gather.3 = bf16[2,32,64]{2,0,1:T(2,128)(2,1)S(1)} all-gather(bf16[2,2,64]{2,0,1:T(2,128)(2,1)S(1)} %copy.24), channel_id=1, replica_groups=mesh['groups'=2,'row'=16] {'row'}, dimensions={1}, use_global_device_ids=true | all-gather | bytes 8704 | tf_op jit(solution)/shard_map/all_gather | solution.py:27
  72.2 0.6 gather_fusion.3
  72.8 4.7 %convolution_convert_fusion.1 = bf16[32,65536]{1,0:T(8,128)(2,1)S(1)} fusion(bf16[64,65536]{1,0:T(8,128)(2,1)} %bitcast.150, bf16[32,64]{1,0:T(8,128)(2,1)S(1)} %gather_fusion.3, pred[32]{0:T(512)(128)(4,1)S(1)} %compare_and_fusion.2), kind=kOutput, calls=%fused_computation.70 | convolution fusion | flops 270534656 | bytes 12587040 | tf_op jit(solution)/shard_map/dot_general | solution.py:51
  77.5 4.3 %copy.39 = bf16[4,8,64,1024]{3,2,1,0:T(8,128)(2,1)} copy(bf16[4,8,64,1024]{3,1,2,0:T(8,128)(2,1)S(1)} %bitcast.154) | data formatting | bytes 8388608
  81.7 7.3 %all-to-all-start.1 = ((bf16[32,64,1024]{2,1,0:T(8,128)(2,1)}), bf16[32,64,1024]{2,1,0:T(8,128)(2,1)}, u32[]{:S(2)}, u32[]{:S(2)}) async-start(bf16[32,64,1024]{2,1,0:T(8,128)(2,1)} %bitcast.152), calls=%async_computation.1 | async-start | bytes 8388608 | tf_op jit(solution)/shard_map/all_to_all | solution.py:57
  89.7 0.1 copy.23
  89.8 89.5 %all-to-all-done.1 = bf16[32,64,1024]{2,1,0:T(8,128)(2,1)} async-done(((bf16[32,64,1024]{2,1,0:T(8,128)(2,1)}), bf16[32,64,1024]{2,1,0:T(8,128)(2,1)}, u32[]{:S(2)}, u32[]{:S(2)}) %all-to-all-start.1) | async-done | bytes 4194336 | tf_op jit(solution)/shard_map/all_to_all | solution.py:57
  179.3 4.8 %copy.26 = bf16[16,2,64,1024]{3,2,0,1:T(8,128)(2,1)} copy(bf16[16,2,64,1024]{3,2,1,0:T(8,128)(2,1)} %bitcast.14) | data formatting | bytes 8388608 | tf_op jit(solution)/shard_map/all_to_all | solution.py:57
  184.1 0.1 broadcast.69.clone
  184.2 5.1 %while.20 = (s32[]{:T(128)}, bf16[2,1024,256]{2,1,0:T(8,128)(2,1)S(1)}, s32[]{:T(128)}, bf16[2,1024,256]{2,1,0:T(8,128)(2,1)S(1)}, bf16[2,1024,1024]{2,1,0:T(8,128)(2,1)}, /*index=5*/s32[]{:T(128)}, s32[]{:T(128)}, s32[]{:T(128)}) while((s32[]{:T(128)}, bf16[2,1024,256]{2,1,0:T(8,128)(2,1)S(1)}, s32[]{:T(128)}, ...), condition=%wide.region_4.9_spmd, body=%wide.region_3.8_spmd.sunk | while | flops 2150629376 | bytes 36178072 | solution.py:66
  184.2 2.5 fusion.133
  186.7 0.3 copy-done.3
  187.0 0.7 fusion.134
  187.8 0.7 fusion.135
  188.5 0.8 fusion.136
  189.3 2.0 copy.27
  191.4 7.0 %all-to-all-start.2 = ((bf16[2,1024,256]{2,0,1:T(2,128)(2,1)}), bf16[2,1024,256]{2,0,1:T(2,128)(2,1)S(1)}, u32[]{:S(2)}, u32[]{:S(2)}) async-start(bf16[2,1024,256]{2,0,1:T(2,128)(2,1)} %copy.27), calls=%async_computation.2 | async-start | bytes 2097152 | tf_op jit(solution)/shard_map/all_to_all | solution.py:67
  198.4 11.9 %copy.40 = bf16[8,8,64,1024]{3,1,2,0:T(8,128)(2,1)} copy(bf16[8,8,64,1024]{3,2,1,0:T(8,128)(2,1)} %bitcast.148) | data formatting | bytes 16777216
  210.3 0.6 gather_fusion.8
  210.9 4.7 %convolution_convert_fusion = bf16[32,65536]{1,0:T(8,128)(2,1)S(1)} fusion(bf16[64,65536]{1,0:T(8,128)(2,1)} %bitcast.151, bf16[32,64]{1,0:T(8,128)(2,1)S(1)} %gather_fusion.8, pred[32]{0:T(512)(128)(4,1)S(1)} %compare_and_fusion.2), kind=kOutput, calls=%fused_computation.69 | convolution fusion | flops 270534656 | bytes 12587040 | tf_op jit(solution)/shard_map/dot_general | solution.py:51
  215.6 4.3 %copy.41 = bf16[4,8,64,1024]{3,2,1,0:T(8,128)(2,1)} copy(bf16[4,8,64,1024]{3,1,2,0:T(8,128)(2,1)S(1)} %bitcast.155) | data formatting | bytes 8388608
  219.9 3.4 all-to-all-done.2
  223.3 4.9 %all-to-all-start.4 = ((bf16[32,64,1024]{2,1,0:T(8,128)(2,1)}), bf16[32,64,1024]{2,1,0:T(8,128)(2,1)}, u32[]{:S(2)}, u32[]{:S(2)}) async-start(bf16[32,64,1024]{2,1,0:T(8,128)(2,1)} %bitcast.153), calls=%async_computation.4 | async-start | bytes 8388608 | tf_op jit(solution)/shard_map/all_to_all | solution.py:57
  228.2 0.7 gather_fusion.5
  228.9 0.7 gather_fusion.10
  229.7 0.1 copy.28
  229.8 0.1 copy.29
  229.9 0.6 gather_fusion.6
  230.6 0.2 broadcast_select_fusion.5
  230.7 0.6 gather_fusion.7
  231.4 1.1 broadcast_select_fusion.4
  232.5 85.9 %all-to-all-done.4 = bf16[32,64,1024]{2,1,0:T(8,128)(2,1)} async-done(((bf16[32,64,1024]{2,1,0:T(8,128)(2,1)}), bf16[32,64,1024]{2,1,0:T(8,128)(2,1)}, u32[]{:S(2)}, u32[]{:S(2)}) %all-to-all-start.4) | async-done | bytes 4194336 | tf_op jit(solution)/shard_map/all_to_all | solution.py:57
  318.4 7.0 %all-to-all-start.3 = ((bf16[32,64,256]{2,1,0:T(8,128)(2,1)}), bf16[32,64,256]{2,1,0:T(8,128)(2,1)S(1)}, u32[]{:S(2)}, u32[]{:S(2)}) async-start(bf16[32,64,256]{2,1,0:T(8,128)(2,1)} %broadcast_select_fusion.4), calls=%async_computation.3 | async-start | bytes 2097152 | tf_op jit(solution)/shard_map/all_to_all | solution.py:58
  325.5 4.9 %copy.32 = bf16[16,2,64,1024]{3,2,0,1:T(8,128)(2,1)} copy(bf16[16,2,64,1024]{3,2,1,0:T(8,128)(2,1)} %bitcast.25) | data formatting | bytes 8388608 | tf_op jit(solution)/shard_map/all_to_all | solution.py:57
  330.3 20.1 %all-to-all-done.3 = bf16[32,64,256]{2,1,0:T(8,128)(2,1)S(1)} async-done(((bf16[32,64,256]{2,1,0:T(8,128)(2,1)}), bf16[32,64,256]{2,1,0:T(8,128)(2,1)S(1)}, u32[]{:S(2)}, u32[]{:S(2)}) %all-to-all-start.3) | async-done | bytes 1048608 | tf_op jit(solution)/shard_map/all_to_all | solution.py:58
  350.4 0.1 copy.30
  350.5 0.1 broadcast.69
  350.5 5.4 %while.21 = (s32[]{:T(128)}, bf16[2,1024,256]{2,1,0:T(8,128)(2,1)S(1)}, s32[]{:T(128)}, bf16[2,1024,256]{2,1,0:T(8,128)(2,1)S(1)}, bf16[2,1024,1024]{2,1,0:T(8,128)(2,1)}, /*index=5*/s32[]{:T(128)}, s32[]{:T(128)}, s32[]{:T(128)}) while((s32[]{:T(128)}, bf16[2,1024,256]{2,1,0:T(8,128)(2,1)S(1)}, s32[]{:T(128)}, ...), condition=%wide.region_6.12_spmd, body=%wide.region_5.11_spmd.sunk | while | flops 2150629376 | bytes 36178072 | solution.py:66
  350.8 2.5 fusion.145
  353.3 0.3 copy-done.2
  353.6 0.7 fusion.146
  354.4 0.7 fusion.147
  355.1 0.8 fusion.148
  355.9 2.0 copy.33
  358.0 6.6 %all-to-all-start.5 = ((bf16[2,1024,256]{2,0,1:T(2,128)(2,1)}), bf16[2,1024,256]{2,0,1:T(2,128)(2,1)S(1)}, u32[]{:S(2)}, u32[]{:S(2)}) async-start(bf16[2,1024,256]{2,0,1:T(2,128)(2,1)} %copy.33), calls=%async_computation.5 | async-start | bytes 2097152 | tf_op jit(solution)/shard_map/all_to_all | solution.py:67
  364.6 24.9 %all-to-all-done.5 = bf16[2,1024,256]{2,0,1:T(2,128)(2,1)S(1)} async-done(((bf16[2,1024,256]{2,0,1:T(2,128)(2,1)}), bf16[2,1024,256]{2,0,1:T(2,128)(2,1)S(1)}, u32[]{:S(2)}, u32[]{:S(2)}) %all-to-all-start.5) | async-done | bytes 1048608 | tf_op jit(solution)/shard_map/all_to_all | solution.py:67
  389.6 0.1 copy.34
  389.7 0.1 copy.35
  389.8 0.6 gather_fusion.11
  390.4 1.1 broadcast_select_fusion.2
  (31 shorter events, 0.2 us)
Async XLA Ops:
  0.0 5.8 %copy-start = (bf16[32,64,256]{2,1,0:T(8,128)(2,1)S(1)}, bf16[32,64,256]{2,1,0:T(8,128)(2,1)}, u32[]{:S(2)}) copy-start(bf16[32,64,256]{2,1,0:T(8,128)(2,1)} %param.20) | copy-start | bytes 3145732
  0.0 14.1 %copy-start.5 = (s32[2,64]{1,0:T(2,128)S(1)}, s32[2,64]{1,0:T(2,128)}, u32[]{:S(2)}) copy-start(s32[2,64]{1,0:T(2,128)} %param.22) | copy-start | bytes 1540
  7.6 74.2 %all-to-all-start = ((bf16[32,64,256]{2,1,0:T(8,128)(2,1)}), bf16[32,64,256]{2,1,0:T(8,128)(2,1)S(1)}, u32[]{:S(2)}, u32[]{:S(2)}) async-start(bf16[32,64,256]{2,1,0:T(8,128)(2,1)} %broadcast_select_fusion.3), calls=%async_computation | async-start | bytes 2097152 | tf_op jit(solution)/shard_map/all_to_all | solution.py:58
  41.2 11.9 %copy-start.6 = (bf16[2,2,64]{2,1,0:T(2,128)(2,1)S(1)}, bf16[2,2,64]{2,1,0:T(2,128)(2,1)}, u32[]{:S(2)}) copy-start(bf16[2,2,64]{2,1,0:T(2,128)(2,1)} %param.23) | copy-start | bytes 1540
  81.7 97.6 %all-to-all-start.1 = ((bf16[32,64,1024]{2,1,0:T(8,128)(2,1)}), bf16[32,64,1024]{2,1,0:T(8,128)(2,1)}, u32[]{:S(2)}, u32[]{:S(2)}) async-start(bf16[32,64,1024]{2,1,0:T(8,128)(2,1)} %bitcast.152), calls=%async_computation.1 | async-start | bytes 8388608 | tf_op jit(solution)/shard_map/all_to_all | solution.py:57
  184.2 2.8 copy-start.3
  191.4 31.9 %all-to-all-start.2 = ((bf16[2,1024,256]{2,0,1:T(2,128)(2,1)}), bf16[2,1024,256]{2,0,1:T(2,128)(2,1)S(1)}, u32[]{:S(2)}, u32[]{:S(2)}) async-start(bf16[2,1024,256]{2,0,1:T(2,128)(2,1)} %copy.27), calls=%async_computation.2 | async-start | bytes 2097152 | tf_op jit(solution)/shard_map/all_to_all | solution.py:67
  223.3 4.9 %copy-start.4 = (s32[2,32]{1,0:T(2,128)S(1)}, s32[2,32]{1,0:T(2,128)}, u32[]{:S(2)}) copy-start(s32[2,32]{1,0:T(2,128)} %param.25) | copy-start | bytes 772
  223.3 95.1 %all-to-all-start.4 = ((bf16[32,64,1024]{2,1,0:T(8,128)(2,1)}), bf16[32,64,1024]{2,1,0:T(8,128)(2,1)}, u32[]{:S(2)}, u32[]{:S(2)}) async-start(bf16[32,64,1024]{2,1,0:T(8,128)(2,1)} %bitcast.153), calls=%async_computation.4 | async-start | bytes 8388608 | tf_op jit(solution)/shard_map/all_to_all | solution.py:57
  318.4 32.0 %all-to-all-start.3 = ((bf16[32,64,256]{2,1,0:T(8,128)(2,1)}), bf16[32,64,256]{2,1,0:T(8,128)(2,1)S(1)}, u32[]{:S(2)}, u32[]{:S(2)}) async-start(bf16[32,64,256]{2,1,0:T(8,128)(2,1)} %broadcast_select_fusion.4), calls=%async_computation.3 | async-start | bytes 2097152 | tf_op jit(solution)/shard_map/all_to_all | solution.py:58
  350.8 2.8 copy-start.2
  358.0 31.6 %all-to-all-start.5 = ((bf16[2,1024,256]{2,0,1:T(2,128)(2,1)}), bf16[2,1024,256]{2,0,1:T(2,128)(2,1)S(1)}, u32[]{:S(2)}, u32[]{:S(2)}) async-start(bf16[2,1024,256]{2,0,1:T(2,128)(2,1)} %copy.33), calls=%async_computation.5 | async-start | bytes 2097152 | tf_op jit(solution)/shard_map/all_to_all | solution.py:67
  364.6 27.0 %copy-start.1 = (bf16[32,64,256]{2,1,0:T(8,128)(2,1)S(1)}, bf16[32,64,256]{2,1,0:T(8,128)(2,1)}, u32[]{:S(2)}) copy-start(bf16[32,64,256]{2,1,0:T(8,128)(2,1)} %param.20) | copy-start | bytes 3145732
where the time goes:
time: 392 us
  waiting for transfers between devices  224 us (57%)
  local copies, waits for them, and re-layouts  71.6 us (18%)
  starting transfers between devices  39.5 us (10%)
  blocking collectives  19 us (5%)
  matrix products  18.8 us (5%)
  other arithmetic  17.6 us (4%)
    all_to_all x2, waiting for transfers between devices, on_device(): lax.all_to_all(potential_rows, 'row', split_axis=0, concat_axis=1, tiled=...  175 us
    unnamed x15, local copies, waits for them, and re-layouts  32.4 us
    all_to_all x2, waiting for transfers between devices, on_device(): lax.all_to_all(advanced, 'row', split_axis=1, concat_axis=0, tiled=True)  28.4 us
    all_to_all x2, waiting for transfers between devices, on_device(): lax.all_to_all(ordered, 'row', split_axis=0, concat_axis=1, tiled=True)  20.1 us
    all_gather x1, blocking collectives, on_device(): all_fields = lax.all_gather(fields, 'row', axis=1, tiled=True)  19 us
    gather x2, local copies, waits for them, and re-layouts, on_device(): jnp.take(cholesky, slab_index[step_number], axis=0)  15.3 us
    all_to_all x2, starting transfers between devices, on_device(): lax.all_to_all(advanced, 'row', split_axis=1, concat_axis=0, tiled=True)  13.7 us
    all_to_all x2, starting transfers between devices, on_device(): lax.all_to_all(ordered, 'row', split_axis=0, concat_axis=1, tiled=True)  13.6 us
  transfers between devices with their start and end apart: 6, of which 5 were waited for; matrix products, arithmetic and copies ran while one was open for 20% of the time, Pallas kernels for 0%

commit v1 on v0

v1 whole, which is shorter than its diff:
```python
import functools

import jax
import jax.numpy as jnp
from jax import lax
from jax.experimental import pallas as pl
from jax.experimental.pallas import tpu as pltpu
from jax.sharding import PartitionSpec as P

ORDER = 4
ROWS = 16
SMEM = pl.BlockSpec(memory_space=pltpu.SMEM)
VMEM = pl.BlockSpec(memory_space=pltpu.VMEM)
ANY = pl.BlockSpec(memory_space=pl.ANY)


def plan_kernel(per_device, counts, sources, first, second, place, total, order):
    slots = place.shape[0]

    def clear(slot, carry):
        order[slot] = -1
        first[slot] = 0
        second[slot] = 0
        return carry

    lax.fori_loop(0, slots, clear, 0)

    def alive(slot):
        return slot % per_device < counts[slot // per_device]

    def mark(slot, carry):
        @pl.when(alive(slot))
        def _():
            order[sources[1, slot]] = 0

        return carry

    lax.fori_loop(0, slots, mark, 0)

    def number(slot, found):
        kept = order[slot] >= 0

        @pl.when(kept)
        def _():
            order[slot] = found
            first[found] = sources[0, slot]
            second[found] = slot

        return found + kept.astype(jnp.int32)

    total[0] = lax.fori_loop(0, slots, number, jnp.int32(0))

    def look(slot, carry):
        place[slot] = jnp.where(alive(slot), order[sources[1, slot]], -1)
        return carry

    lax.fori_loop(0, slots, look, 0)


def plan(counts, sources, per_device):
    slots = sources.shape[1]
    vector = jax.ShapeDtypeStruct((slots,), jnp.int32)
    return pl.pallas_call(
        functools.partial(plan_kernel, per_device),
        out_shape=(vector, vector, vector, jax.ShapeDtypeStruct((1,), jnp.int32)),
        in_specs=[SMEM, SMEM],
        out_specs=(SMEM, SMEM, SMEM, SMEM),
        scratch_shapes=[pltpu.SMEM((slots,), jnp.int32)],
    )(counts, sources)


def pick_kernel(first, base, walkers, picked, semaphore):
    for chain in range(picked.shape[0]):
        pltpu.make_async_copy(
            walkers.at[first[base[0] + chain]], picked.at[chain], semaphore
        ).start()
    pltpu.make_async_copy(picked, picked, semaphore).wait()


def pick(walkers, first, base, chains):
    shape = (chains,) + walkers.shape[1:]
    return pl.pallas_call(
        pick_kernel,
        out_shape=jax.ShapeDtypeStruct(shape, walkers.dtype),
        in_specs=[SMEM, SMEM, ANY],
        out_specs=VMEM,
        scratch_shapes=[pltpu.SemaphoreType.DMA],
    )(first, base, walkers)


def potential_kernel(
    chains, step, chosen, base, slab, fields, cholesky, out, blocks, left, semaphores
):
    vectors = blocks.shape[1]
    block = pl.program_id(0)

    def fetch(block, slot):
        def one(vector, carry):
            pltpu.make_async_copy(
                cholesky.at[slab[step, vector], pl.ds(block * ROWS, ROWS), :],
                blocks.at[slot, vector],
                semaphores.at[slot],
            ).start()
            return carry

        lax.fori_loop(0, vectors, one, 0, unroll=8)

    @pl.when(block == 0)
    def _():
        fetch(0, 0)
        slots = fields.shape[0]
        row = lax.broadcasted_iota(jnp.int32, (chains * ROWS, slots), 0) // ROWS
        wanted = jnp.zeros((chains * ROWS, slots), jnp.int32)
        for chain in range(chains):
            wanted = jnp.where(row == chain, chosen[base[0] + chain], wanted)
        column = lax.broadcasted_iota(jnp.int32, (chains * ROWS, slots), 1)
        rows_of = (wanted == column).astype(jnp.float32).astype(jnp.bfloat16)
        repeated = jnp.dot(
            rows_of, fields[...], preferred_element_type=jnp.float32
        ).astype(jnp.bfloat16)
        spread = (
            lax.broadcasted_iota(jnp.int32, (vectors, vectors * ROWS), 0)
            == lax.broadcasted_iota(jnp.int32, (vectors, vectors * ROWS), 1) // ROWS
        )
        wide = jnp.dot(
            repeated,
            spread.astype(jnp.float32).astype(jnp.bfloat16),
            preferred_element_type=jnp.float32,
        )
        same = (
            lax.broadcasted_iota(jnp.int32, wide.shape, 0) % ROWS
            == lax.broadcasted_iota(jnp.int32, wide.shape, 1) % ROWS
        )
        left[...] = jnp.where(same, wide, 0.0).astype(jnp.bfloat16)

    @pl.when(block + 1 < pl.num_programs(0))
    def _():
        fetch(block + 1, (block + 1) % 2)

    slot = block % 2
    pltpu.make_async_copy(blocks.at[slot], blocks.at[slot], semaphores.at[slot]).wait()
    orbitals = out.shape[2]
    right = blocks[slot].reshape(vectors * ROWS, orbitals)
    product = jnp.dot(left[...], right, preferred_element_type=jnp.float32)
    out[...] = product.astype(jnp.bfloat16).reshape(chains, ROWS, orbitals)


def potential_rows(cholesky, slab, fields, chosen, base, step, chains):
    local_rows, orbitals = cholesky.shape[1:]
    vectors = slab.shape[1]
    if local_rows % ROWS:
        members = lax.dynamic_slice_in_dim(chosen, base[0], chains)
        return (
            jnp.dot(
                jnp.take(fields, members, axis=0, mode="clip"),
                jnp.take(cholesky, slab[step], axis=0, mode="clip").reshape(vectors, -1),
                preferred_element_type=jnp.float32,
            )
            .astype(jnp.bfloat16)
            .reshape(chains, local_rows, orbitals)
        )
    return pl.pallas_call(
        functools.partial(potential_kernel, chains, step),
        out_shape=jax.ShapeDtypeStruct((chains, local_rows, orbitals), jnp.bfloat16),
        grid=(local_rows // ROWS,),
        in_specs=[SMEM, SMEM, SMEM, VMEM, ANY],
        out_specs=pl.BlockSpec((chains, ROWS, orbitals), lambda block: (0, block, 0)),
        scratch_shapes=[
            pltpu.VMEM((2, vectors, ROWS, orbitals), jnp.bfloat16),
            pltpu.VMEM((chains * ROWS, vectors * ROWS), jnp.bfloat16),
            pltpu.SemaphoreType.DMA((2,)),
        ],
        cost_estimate=pl.CostEstimate(
            flops=2 * chains * ROWS * vectors * local_rows * orbitals,
            bytes_accessed=2 * (vectors + chains) * local_rows * orbitals,
            transcendentals=0,
        ),
        compiler_params=pltpu.CompilerParams(vmem_limit_bytes=32 << 20),
    )(chosen, base, slab, fields, cholesky)


def taylor_kernel(matrix, initial, out, summed, term):
    tile = min(256, matrix.shape[0])
    for degree in range(1, ORDER + 1):
        source = initial if degree == 1 else term.at[degree % 2]
        for start in range(0, matrix.shape[0], tile):
            rows = slice(start, start + tile)
            product = jnp.dot(
                matrix[rows, :], source[...], preferred_element_type=jnp.float32
            ) * (1.0 / degree)
            before = initial[rows, :].astype(jnp.float32) if degree == 1 else summed[rows, :]
            if degree == ORDER:
                out[rows, :] = (before + product).astype(jnp.bfloat16)
            else:
                summed[rows, :] = before + product
                term[(degree + 1) % 2, rows, :] = product.astype(jnp.bfloat16)


def taylor(matrix, initial):
    rows, columns = initial.shape
    return pl.pallas_call(
        taylor_kernel,
        out_shape=jax.ShapeDtypeStruct(initial.shape, jnp.bfloat16),
        in_specs=[VMEM, VMEM],
        out_specs=VMEM,
        scratch_shapes=[
            pltpu.VMEM((rows, columns), jnp.float32),
            pltpu.VMEM((2, rows, columns), jnp.bfloat16),
        ],
        cost_estimate=pl.CostEstimate(
            flops=2 * ORDER * rows * rows * columns,
            bytes_accessed=2 * rows * (rows + 2 * columns),
            transcendentals=0,
        ),
        compiler_params=pltpu.CompilerParams(vmem_limit_bytes=32 << 20),
    )(matrix, initial)


def exchange(array):
    return lax.all_to_all(array, "row", split_axis=0, concat_axis=0, tiled=True)


def on_device(walkers, cholesky, slab_index, fields, counts, sources):
    local_rows, columns = walkers.shape[1:]
    orbitals = cholesky.shape[2]
    steps, per_device, vectors = fields.shape
    devices = lax.axis_size("row")
    slots = per_device * devices
    first, second, place, total = plan(counts, sources, per_device)
    sent = jnp.broadcast_to(
        fields.reshape(1, steps * per_device, vectors), (devices, steps * per_device, vectors)
    )
    all_fields = (
        exchange(sent)
        .reshape(devices, steps, per_device, vectors)
        .swapaxes(0, 1)
        .reshape(steps, slots, vectors)
    )

    def one_pass(base):
        initial = exchange(pick(walkers, first, base, devices))
        early = exchange(
            potential_rows(cholesky, slab_index, all_fields[0], first, base, 0, devices)
        )
        late = exchange(
            potential_rows(cholesky, slab_index, all_fields[1], second, base, 1, devices)
        )
        current = initial.reshape(orbitals, columns)
        for matrix in (early, late):
            current = taylor(matrix.reshape(orbitals, orbitals), current)
        return exchange(current.reshape(devices, local_rows, columns))

    def select(returned, base):
        own = place - base[0]
        hit = jnp.logical_and(own >= 0, own < devices)
        return hit[:, None, None], jnp.take(returned, own, axis=0, mode="clip")

    base = jnp.zeros((1,), jnp.int32)
    hit, rows = select(one_pass(base), base)
    branched = jnp.where(hit, rows, jnp.zeros_like(rows))

    def another(number, branched):
        base = jnp.full((1,), number * devices, jnp.int32)
        hit, rows = select(one_pass(base), base)
        return jnp.where(hit, rows, branched)

    return lax.fori_loop(1, (total[0] + devices - 1) // devices, another, branched)


def solution(mesh):
    in_specs = (
        P("groups", "row", None),
        P("groups", "row", None),
        P("groups", None),
        P(None, ("groups", "row"), None),
        P("groups"),
        P("groups", None),
    )
    out_specs = P("groups", "row", None)
    return jax.shard_map(
        on_device, mesh=mesh, in_specs=in_specs, out_specs=out_specs, check_vma=False
    )
```

time: 392 us -> 165 us (0.42)
  waiting for transfers between devices: 224 us -> 103 us
  local copies, waits for them, and re-layouts: 71.6 us -> 2.13 us
  Pallas kernels: 0 us -> 26.7 us
  blocking collectives: 19 us -> 0 us
  matrix products: 18.8 us -> 0 us
  other arithmetic: 17.6 us -> 1.12 us
  starting transfers between devices: 39.5 us -> 29.1 us
    all_to_all x6 -> x5, waiting for transfers between devices: 224 us -> 103 us  [exchange(): return lax.all_to_all(array, 'row', split_axis=0, concat_axis=0, tiled=True)]
    unnamed x15 -> x4, local copies, waits for them, and re-layouts: 32.4 us -> 0.77 us
    pallas_call x0 -> x6, Pallas kernels: none -> 26.7 us  [the longest x2 14.3 us: potential_rows(): pl.pallas_call(functools.partial(potential_kernel, chains, step), out_sha...]
    gather x12 -> x1, local copies, waits for them, and re-layouts: 22.4 us -> 0.61 us  [select(): return (hit[:, None, None], jnp.take(returned, own, axis=0, mode='clip'))]
    all_gather x1 -> x0, blocking collectives: 19 us -> none  [on_device(): all_fields = lax.all_gather(fields, 'row', axis=1, tiled=True)]
    dot_general x10 -> x0, matrix products: 18.8 us -> none  [the longest x8 9.4 us: taylor_step(): jnp.dot(potential, term_now, preferred_element_type=jnp.float32) / degree]
    select_n x9 -> x1, other arithmetic: 16 us -> 1.11 us  [on_device(): branched = jnp.where(hit, rows, jnp.zeros_like(rows))]
    all_to_all x6 -> x5, starting transfers between devices: 39.5 us -> 29.1 us  [exchange(): return lax.all_to_all(array, 'row', split_axis=0, concat_axis=0, tiled=True)]
  transfers between devices with their start and end apart: 6 -> 5, of which waited for: 5 -> 4; matrix products, arithmetic and copies ran while one was open for 20% -> 0% of each run, Pallas kernels for 0% -> 13%
where the time goes in v1:
time: 165 us; the launch traced here: 163 us
  waiting for transfers between devices  103 us (62%)
  starting transfers between devices  29.1 us (18%)
  Pallas kernels  26.7 us (16%)
  local copies, waits for them, and re-layouts  2.13 us (1%)
    all_to_all x5, waiting for transfers between devices, exchange(): return lax.all_to_all(array, 'row', split_axis=0, concat_axis=0, tiled=True)  103 us
    all_to_all x5, starting transfers between devices, exchange(): return lax.all_to_all(array, 'row', split_axis=0, concat_axis=0, tiled=True)  29.1 us
    pallas_call x2, Pallas kernels, potential_rows(): pl.pallas_call(functools.partial(potential_kernel, chains, step), out_sha...  14.3 us
    pallas_call x2, Pallas kernels, taylor(): pl.pallas_call(taylor_kernel, out_shape=jax.ShapeDtypeStruct(initial.shap...  7.2 us
  transfers between devices with their start and end apart: 5, of which 4 were waited for; matrix products, arithmetic and copies ran while one was open for 0% of the time, Pallas kernels for 13%

profile of v1, /device:TPU:9, one launch (start us, length us, event | category | flops | bytes accessed | tf_op | source)
XLA Modules:
  0.0 162.8 jit_solution(2511063712991169659)
XLA Ops:
  0.0 0.0 copy-start.2
  0.0 0.7 broadcast_in_dim.39
  0.7 0.7 reshape.78
  1.4 6.5 %all-to-all-start.4 = ((bf16[16,2,128]{2,1,0:T(2,128)(2,1)}), bf16[16,2,128]{2,1,0:T(2,128)(2,1)S(1)}, u32[]{:S(2)}, u32[]{:S(2)}) async-start(bf16[16,2,128]{2,1,0:T(2,128)(2,1)} %reshape.78), calls=%async_computation.4 | async-start | bytes 16384 | tf_op jit(solution)/shard_map/all_to_all | solution.py:220
  7.9 2.8 %shard_map.64 = (s32[32]{0:T(128)S(1)}, s32[32]{0:T(128)S(1)}, s32[32]{0:T(128)S(1)}, s32[1]{0:T(128)}) custom-call(s32[16]{0:T(128)} %counts.1, s32[2,32]{1,0:T(2,128)} %sources.1), custom_call_target="tpu_custom_call" | custom-call | tf_op jit(solution)/shard_map/pallas_call | solution.py:63
  10.8 2.3 %shard_map.67 = bf16[16,64,256]{2,1,0:T(8,128)(2,1)} custom-call(s32[32]{0:T(128)S(1)} %get-tuple-element.171.chosen.first, s32[1]{0:T(128)} %constant.29.clone.1.base, bf16[32,64,256]{2,1,0:T(8,128)(2,1)} %walkers.1), custom_call_target="tpu_custom_call" | custom-call | tf_op jit(solution)/shard_map/pallas_call | solution.py:82
  13.1 0.0 all-to-all-done.4
  13.2 6.0 %all-to-all-start.7 = ((bf16[16,64,256]{2,1,0:T(8,128)(2,1)}), bf16[16,64,256]{2,1,0:T(8,128)(2,1)S(1)}, u32[]{:S(2)}, u32[]{:S(2)}) async-start(bf16[16,64,256]{2,1,0:T(8,128)(2,1)} %shard_map.67), calls=%async_computation.7 | async-start | bytes 1048576 | tf_op jit(solution)/shard_map/all_to_all | solution.py:220
  19.2 0.1 reshape.79
  19.3 0.0 copy-done.2
  19.3 7.2 %shard_map.66 = bf16[16,64,1024]{2,1,0:T(8,128)(2,1)} custom-call(s32[32]{0:T(128)S(1)} %get-tuple-element.171.chosen.first, s32[1]{0:T(128)} %constant.29.clone.1.base, s32[2,64]{1,0:T(2,128)S(1)} %copy-done.2, bf16[32,64]{1,0:T(8,128)(2,1)S(1)} %bitcast.38, bf16[512,64,1024]{2,1,0:T(8,128)(2,1)} %cholesky.3), custom_call_target="tpu_custom_call" | custom-call | flops 2147483648 | bytes 10485760 | tf_op jit(solution)/shard_map/pallas_call | solution.py:162
  26.5 6.8 %all-to-all-done.7 = bf16[16,64,256]{2,1,0:T(8,128)(2,1)S(1)} async-done(((bf16[16,64,256]{2,1,0:T(8,128)(2,1)}), bf16[16,64,256]{2,1,0:T(8,128)(2,1)S(1)}, u32[]{:S(2)}, u32[]{:S(2)}) %all-to-all-start.7) | async-done | bytes 524320 | tf_op jit(solution)/shard_map/all_to_all | solution.py:220
  33.3 4.3 %all-to-all-start.6 = ((bf16[16,64,1024]{2,1,0:T(8,128)(2,1)}), bf16[16,64,1024]{2,1,0:T(8,128)(2,1)S(1)}, u32[]{:S(2)}, u32[]{:S(2)}) async-start(bf16[16,64,1024]{2,1,0:T(8,128)(2,1)} %shard_map.66), calls=%async_computation.6 | async-start | bytes 4194304 | tf_op jit(solution)/shard_map/all_to_all | solution.py:220
  37.6 7.1 %shard_map.65 = bf16[16,64,1024]{2,1,0:T(8,128)(2,1)} custom-call(s32[32]{0:T(128)S(1)} %get-tuple-element.168.chosen, s32[1]{0:T(128)} %constant.29.clone.1.base, s32[2,64]{1,0:T(2,128)S(1)} %copy-done.2, bf16[32,64]{1,0:T(8,128)(2,1)S(1)} %bitcast.37, bf16[512,64,1024]{2,1,0:T(8,128)(2,1)} %cholesky.3), custom_call_target="tpu_custom_call" | custom-call | flops 2147483648 | bytes 10485760 | tf_op jit(solution)/shard_map/pallas_call | solution.py:162
  44.7 39.0 %all-to-all-done.6 = bf16[16,64,1024]{2,1,0:T(8,128)(2,1)S(1)} async-done(((bf16[16,64,1024]{2,1,0:T(8,128)(2,1)}), bf16[16,64,1024]{2,1,0:T(8,128)(2,1)S(1)}, u32[]{:S(2)}, u32[]{:S(2)}) %all-to-all-start.6) | async-done | bytes 2097184 | tf_op jit(solution)/shard_map/all_to_all | solution.py:220
  83.7 6.1 %all-to-all-start.5 = ((bf16[16,64,1024]{2,1,0:T(8,128)(2,1)}), bf16[16,64,1024]{2,1,0:T(8,128)(2,1)}, u32[]{:S(2)}, u32[]{:S(2)}) async-start(bf16[16,64,1024]{2,1,0:T(8,128)(2,1)} %shard_map.65), calls=%async_computation.5 | async-start | bytes 4194304 | tf_op jit(solution)/shard_map/all_to_all | solution.py:220
  89.8 2.4 %shard_map.68.initial = bf16[1024,256]{1,0:T(8,128)(2,1)S(1)} custom-call(bf16[1024,1024]{1,0:T(8,128)(2,1)S(1)} %bitcast.35, bf16[1024,256]{1,0:T(8,128)(2,1)S(1)} %bitcast.36), custom_call_target="tpu_custom_call" | custom-call | flops 2147483648 | bytes 3145728 | tf_op jit(solution)/shard_map/pallas_call | solution.py:201
  92.3 43.8 %all-to-all-done.5 = bf16[16,64,1024]{2,1,0:T(8,128)(2,1)} async-done(((bf16[16,64,1024]{2,1,0:T(8,128)(2,1)}), bf16[16,64,1024]{2,1,0:T(8,128)(2,1)}, u32[]{:S(2)}, u32[]{:S(2)}) %all-to-all-start.5) | async-done | bytes 2097184 | tf_op jit(solution)/shard_map/all_to_all | solution.py:220
  136.0 4.8 %shard_map.69 = bf16[1024,256]{1,0:T(8,128)(2,1)} custom-call(bf16[1024,1024]{1,0:T(8,128)(2,1)} %bitcast.11.matrix, bf16[1024,256]{1,0:T(8,128)(2,1)S(1)} %shard_map.68.initial), custom_call_target="tpu_custom_call" | custom-call | flops 2147483648 | bytes 3145728 | tf_op jit(solution)/shard_map/pallas_call | solution.py:201
  140.8 6.1 %all-to-all-start.8 = ((bf16[16,64,256]{2,1,0:T(8,128)(2,1)}), bf16[16,64,256]{2,1,0:T(8,128)(2,1)S(1)}, u32[]{:S(2)}, u32[]{:S(2)}) async-start(bf16[16,64,256]{2,1,0:T(8,128)(2,1)} %bitcast.16), calls=%async_computation.8 | async-start | bytes 1048576 | tf_op jit(solution)/shard_map/all_to_all | solution.py:220
  147.6 13.4 %all-to-all-done.8 = bf16[16,64,256]{2,1,0:T(8,128)(2,1)S(1)} async-done(((bf16[16,64,256]{2,1,0:T(8,128)(2,1)}), bf16[16,64,256]{2,1,0:T(8,128)(2,1)S(1)}, u32[]{:S(2)}, u32[]{:S(2)}) %all-to-all-start.8) | async-done | bytes 524320 | tf_op jit(solution)/shard_map/all_to_all | solution.py:220
  161.0 0.6 gather_fusion.1
  161.6 1.1 broadcast_select_fusion.1
  (8 shorter events, 0.1 us)
Async XLA Ops:
  0.0 19.3 %copy-start.2 = (s32[2,64]{1,0:T(2,128)S(1)}, s32[2,64]{1,0:T(2,128)}, u32[]{:S(2)}) copy-start(s32[2,64]{1,0:T(2,128)} %slab.3) | copy-start | bytes 1540
  1.4 11.8 %all-to-all-start.4 = ((bf16[16,2,128]{2,1,0:T(2,128)(2,1)}), bf16[16,2,128]{2,1,0:T(2,128)(2,1)S(1)}, u32[]{:S(2)}, u32[]{:S(2)}) async-start(bf16[16,2,128]{2,1,0:T(2,128)(2,1)} %reshape.78), calls=%async_computation.4 | async-start | bytes 16384 | tf_op jit(solution)/shard_map/all_to_all | solution.py:220
  13.2 20.2 %all-to-all-start.7 = ((bf16[16,64,256]{2,1,0:T(8,128)(2,1)}), bf16[16,64,256]{2,1,0:T(8,128)(2,1)S(1)}, u32[]{:S(2)}, u32[]{:S(2)}) async-start(bf16[16,64,256]{2,1,0:T(8,128)(2,1)} %shard_map.67), calls=%async_computation.7 | async-start | bytes 1048576 | tf_op jit(solution)/shard_map/all_to_all | solution.py:220
  33.3 50.4 %all-to-all-start.6 = ((bf16[16,64,1024]{2,1,0:T(8,128)(2,1)}), bf16[16,64,1024]{2,1,0:T(8,128)(2,1)S(1)}, u32[]{:S(2)}, u32[]{:S(2)}) async-start(bf16[16,64,1024]{2,1,0:T(8,128)(2,1)} %shard_map.66), calls=%async_computation.6 | async-start | bytes 4194304 | tf_op jit(solution)/shard_map/all_to_all | solution.py:220
  83.7 52.3 %all-to-all-start.5 = ((bf16[16,64,1024]{2,1,0:T(8,128)(2,1)}), bf16[16,64,1024]{2,1,0:T(8,128)(2,1)}, u32[]{:S(2)}, u32[]{:S(2)}) async-start(bf16[16,64,1024]{2,1,0:T(8,128)(2,1)} %shard_map.65), calls=%async_computation.5 | async-start | bytes 4194304 | tf_op jit(solution)/shard_map/all_to_all | solution.py:220
  140.8 20.2 %all-to-all-start.8 = ((bf16[16,64,256]{2,1,0:T(8,128)(2,1)}), bf16[16,64,256]{2,1,0:T(8,128)(2,1)S(1)}, u32[]{:S(2)}, u32[]{:S(2)}) async-start(bf16[16,64,256]{2,1,0:T(8,128)(2,1)} %bitcast.16), calls=%async_computation.8 | async-start | bytes 1048576 | tf_op jit(solution)/shard_map/all_to_all | solution.py:220

commit v2 on v0

v2 whole, which is shorter than its diff:
```python
import functools

import jax
import jax.numpy as jnp
from jax import lax
from jax.experimental import pallas as pl
from jax.experimental.pallas import tpu as pltpu
from jax.sharding import PartitionSpec as P


ORDER = 4
ROWS = 16
SMEM = pl.BlockSpec(memory_space=pltpu.SMEM)
VMEM = pl.BlockSpec(memory_space=pltpu.VMEM)
ANY = pl.BlockSpec(memory_space=pl.ANY)


def params(mebibytes=40):
    return pltpu.CompilerParams(vmem_limit_bytes=mebibytes << 20)


def plan_kernel(per_device, counts, sources, lists, place, total, order):
    slots = place.shape[0]

    def clear(slot, carry):
        order[slot] = -1
        lists[0, slot] = 0
        lists[1, slot] = 0
        return carry

    lax.fori_loop(0, slots, clear, 0)

    def alive(slot):
        return slot % per_device < counts[slot // per_device]

    def mark(slot, carry):
        @pl.when(alive(slot))
        def _():
            order[sources[1, slot]] = 0

        return carry

    lax.fori_loop(0, slots, mark, 0)

    def number(slot, found):
        kept = order[slot] >= 0

        @pl.when(kept)
        def _():
            order[slot] = found
            lists[0, found] = sources[0, slot]
            lists[1, found] = slot

        return found + kept.astype(jnp.int32)

    total[0] = lax.fori_loop(0, slots, number, jnp.int32(0))

    def look(slot, carry):
        place[slot] = jnp.where(alive(slot), order[sources[1, slot]], -1)
        return carry

    lax.fori_loop(0, slots, look, 0)


def plan(counts, sources, per_device):
    slots = sources.shape[1]
    vector = jax.ShapeDtypeStruct((slots,), jnp.int32)
    return pl.pallas_call(
        functools.partial(plan_kernel, per_device),
        out_shape=(
            jax.ShapeDtypeStruct((2, slots), jnp.int32),
            vector,
            jax.ShapeDtypeStruct((1,), jnp.int32),
        ),
        in_specs=[SMEM, SMEM],
        out_specs=(SMEM, SMEM, SMEM),
        scratch_shapes=[pltpu.SMEM((slots,), jnp.int32)],
    )(counts, sources)


def target_of(small, step, chips, device):
    chip, core = device // 2, device % 2
    if small and core:
        return chip % 2, chips + chip // 2
    return step, chip + core * chips


def potential_kernel(targets, spread, per_device, pieces, walked, me, lists, base, slab, *refs):
    fields, refs = refs[:pieces], refs[pieces:]
    cholesky, refs = refs[0], refs[1:]
    walkers, refs = (refs[0], refs[1:]) if walked else (None, refs)
    scratch = refs[-4 - walked :]
    blocks, left, held, semaphores = scratch[:4]
    picked = scratch[4] if walked else None
    outs = refs[: -4 - walked]
    steps = sorted({step for step, _ in targets})
    vectors = blocks.shape[1]
    halves = semaphores.shape[0] - 1
    half_rows = blocks.shape[2] // halves
    orbitals = blocks.shape[3]
    devices = held.shape[0]
    block = pl.program_id(0)

    def slot_of(number):
        step, chain = targets[number]
        if spread:
            chain = (me[0] // 2) ^ chain
        return lists[step, base[0] + chain]

    @pl.when(block == 0)
    def _():
        for half in range(halves):
            rows = pl.ds(half * half_rows, half_rows)
            for which, step in enumerate(steps):

                def one(vector, carry, rows=rows, half=half, which=which, step=step):
                    pltpu.make_async_copy(
                        cholesky.at[slab[step, vector], rows, :],
                        blocks.at[which, vector, rows, :],
                        semaphores.at[half],
                    ).start()
                    return carry

                lax.fori_loop(0, vectors, one, 0, unroll=8)
        if walked:
            for number in range(len(targets)):
                pltpu.make_async_copy(
                    walkers.at[slot_of(number)], picked.at[number], semaphores.at[halves]
                ).start()
        part = devices // pieces
        for piece in range(pieces):
            held[piece * part : (piece + 1) * part, :] = fields[piece][...].astype(jnp.float32)
        widen = (
            lax.broadcasted_iota(jnp.int32, (vectors, vectors * ROWS), 0)
            == lax.broadcasted_iota(jnp.int32, (vectors, vectors * ROWS), 1) // ROWS
        )
        widen = widen.astype(jnp.float32).astype(jnp.bfloat16)
        start = 0
        for step in steps:
            members = [number for number, target in enumerate(targets) if target[0] == step]
            shape = (len(members) * ROWS, devices)
            row = lax.broadcasted_iota(jnp.int32, shape, 0) // ROWS
            column = lax.broadcasted_iota(jnp.int32, shape, 1)
            wanted = jnp.zeros(shape, jnp.int32)
            for place, number in enumerate(members):
                slot = slot_of(number)
                there = ((slot // per_device) ^ me[0]) * per_device + slot % per_device
                wanted = jnp.where(row == place, there, wanted)
            repeated = jnp.zeros((shape[0], vectors), jnp.float32)
            for within in range(per_device):
                rows_of = (wanted == column * per_device + within).astype(jnp.float32)
                first = (step * per_device + within) * vectors
                repeated = repeated + jnp.dot(
                    rows_of.astype(jnp.bfloat16),
                    held[:, first : first + vectors].astype(jnp.bfloat16),
                    preferred_element_type=jnp.float32,
                )
            wide = jnp.dot(
                repeated.astype(jnp.bfloat16), widen, preferred_element_type=jnp.float32
            )
            same = (
                lax.broadcasted_iota(jnp.int32, wide.shape, 0) % ROWS
                == lax.broadcasted_iota(jnp.int32, wide.shape, 1) % ROWS
            )
            left[start : start + shape[0], :] = jnp.where(same, wide, 0.0).astype(jnp.bfloat16)
            start += shape[0]
        if walked:
            pltpu.make_async_copy(picked, picked, semaphores.at[halves]).wait()

    for half in range(halves):

        @pl.when(block == half * (half_rows // ROWS))
        def _():
            view = blocks.at[:, :, pl.ds(half * half_rows, half_rows), :]
            pltpu.make_async_copy(view, view, semaphores.at[half]).wait()

    rows = pl.ds(block * ROWS, ROWS)
    start = 0
    for which, step in enumerate(steps):
        members = [number for number, target in enumerate(targets) if target[0] == step]
        right = blocks[which, :, rows, :].reshape(vectors * ROWS, orbitals)
        end = start + len(members) * ROWS
        product = jnp.dot(
            left[start:end, :], right, preferred_element_type=jnp.float32
        ).astype(jnp.bfloat16)
        start = end
        for place, number in enumerate(members):
            out = outs[number] if spread else outs[0].at[number]
            out[:, :orbitals] = product[place * ROWS : (place + 1) * ROWS]
            if walked:
                out[:, orbitals:] = picked[number, rows, :]


def potential_rows(
    cholesky, slab, fields, walkers, lists, me, base, targets, spread, per_device, devices
):
    local_rows, orbitals = cholesky.shape[1:]
    vectors = slab.shape[1]
    count = len({step for step, _ in targets})
    walked = walkers is not None
    width = orbitals + (walkers.shape[2] if walked else 0)
    halves = 2 if local_rows % (2 * ROWS) == 0 else 1
    scratch = [
        pltpu.VMEM((count, vectors, local_rows, orbitals), jnp.bfloat16),
        pltpu.VMEM((len(targets) * ROWS, vectors * ROWS), jnp.bfloat16),
        pltpu.VMEM((devices, fields[0].shape[1]), jnp.float32),
        pltpu.SemaphoreType.DMA((halves + 1,)),
    ]
    if walked:
        scratch.append(pltpu.VMEM((len(targets),) + walkers.shape[1:], jnp.bfloat16))
    if spread:
        shapes = [jax.ShapeDtypeStruct((local_rows, width), jnp.bfloat16)] * len(targets)
        specs = [pl.BlockSpec((ROWS, width), lambda block: (block, 0))] * len(targets)
    else:
        shapes = jax.ShapeDtypeStruct((len(targets), local_rows, width), jnp.bfloat16)
        specs = pl.BlockSpec((len(targets), ROWS, width), lambda block: (0, block, 0))
    return pl.pallas_call(
        functools.partial(
            potential_kernel, targets, spread, per_device, len(fields), walked
        ),
        out_shape=shapes,
        grid=(local_rows // ROWS,),
        in_specs=[SMEM] * 4 + [VMEM] * len(fields) + [ANY] * (1 + walked),
        out_specs=specs,
        scratch_shapes=scratch,
        cost_estimate=pl.CostEstimate(
            flops=2 * len(targets) * ROWS * vectors * local_rows * orbitals,
            bytes_accessed=2 * (count * vectors + len(targets)) * local_rows * orbitals,
            transcendentals=0,
        ),
        compiler_params=params(),
    )(me, lists, base, slab, *fields, cholesky, *((walkers,) if walked else ()))


def taylor_kernel(mode, chips, me, joint, *refs):
    parts, refs = (refs[:chips], refs[chips:]) if mode == "small" else ((), refs)
    across, refs = (refs[: chips], refs[chips:]) if mode == "small" else ((), refs)
    starts, refs = refs[: {"first": 0, "large": 1, "small": 2}[mode]], refs[
        {"first": 0, "large": 1, "small": 2}[mode] :
    ]
    out, matrix, begun, summed, term, semaphores, ready = refs
    devices, local = joint.shape[:2]
    rows, columns = summed.shape
    tiles = devices // 4
    tile = rows // tiles

    def view(number):
        return matrix.at[pl.ds(pl.multiple_of(number * tile, tile), tile), :]

    def copy_joint(number):
        for device in range(4):
            pltpu.make_async_copy(
                joint.at[4 * number + device, :, pl.ds(0, rows)],
                matrix.at[pl.ds(pl.multiple_of((4 * number + device) * local, local), local), :],
                semaphores.at[number],
            ).start()

    def copy_begun(source):
        pltpu.make_async_copy(source, begun, ready).start()

    if mode == "first":
        for device in range(devices):
            pltpu.make_async_copy(
                joint.at[device, :, pl.ds(rows, columns)],
                begun.at[pl.ds(device * local, local), :],
                ready,
            ).start()
    if mode == "large":
        copy_begun(starts[0])
    if mode == "small":
        own = me[0] % 2 == 0

        @pl.when(own)
        def _():
            copy_begun(starts[0])
            for chip in range(chips):
                for core in range(2):
                    device = me[0] ^ (2 * chip + core)
                    pltpu.make_async_copy(
                        across[chip] if core else parts[chip],
                        matrix.at[pl.ds(pl.multiple_of(device * local, local), local), :],
                        semaphores.at[device // 4],
                    ).start()

        @pl.when(jnp.logical_not(own))
        def _():
            copy_begun(starts[1])
            for number in range(tiles):
                copy_joint(number)
    else:
        for number in range(tiles):
            copy_joint(number)
    pltpu.make_async_copy(begun, begun, ready).wait()
    for degree in range(1, ORDER + 1):
        for number in range(tiles):
            span = slice(number * tile, (number + 1) * tile)
            if degree == 1:
                pltpu.make_async_copy(view(number), view(number), semaphores.at[number]).wait()
                source = begun[...]
                before = begun[span, :].astype(jnp.float32)
            else:
                source = term[degree % 2]
                before = summed[span, :]
            product = jnp.dot(
                matrix[span, :], source, preferred_element_type=jnp.float32
            ) * (1.0 / degree)
            if degree < ORDER:
                summed[span, :] = before + product
                term[(degree + 1) % 2, span, :] = product.astype(jnp.bfloat16)
            else:
                out[span, :] = (before + product).astype(jnp.bfloat16)


def taylor(mode, me, joint, parts, across, starts, columns):
    devices, local = joint.shape[:2]
    rows = devices * local
    chips = devices // 2
    return pl.pallas_call(
        functools.partial(taylor_kernel, mode, chips),
        out_shape=jax.ShapeDtypeStruct((rows, columns), jnp.bfloat16),
        in_specs=[SMEM] + [ANY] * (1 + len(parts) + len(across) + len(starts)),
        out_specs=VMEM,
        scratch_shapes=[
            pltpu.VMEM((rows, rows), jnp.bfloat16),
            pltpu.VMEM((rows, columns), jnp.bfloat16),
            pltpu.VMEM((rows, columns), jnp.float32),
            pltpu.VMEM((2, rows, columns), jnp.bfloat16),
            pltpu.SemaphoreType.DMA((devices // 4,)),
            pltpu.SemaphoreType.DMA,
        ],
        cost_estimate=pl.CostEstimate(
            flops=2 * ORDER * rows * rows * columns,
            bytes_accessed=2 * rows * (rows + 3 * columns),
            transcendentals=0,
        ),
        compiler_params=params(),
    )(me, joint, *parts, *across, *starts)


def select_kernel(small, kept, place, base, returned, *refs):
    out = refs[-1]
    chips = returned.shape[0] // 2
    capacity = chips * 3 // 2 if small else chips * 2

    def one(slot, carry):
        chain = place[slot] - base[0]
        hit = jnp.logical_and(chain >= 0, chain < capacity)
        chain = jnp.clip(chain, 0, capacity - 1)
        other = 2 * (chain - chips)
        owner = jnp.where(chain < chips, 2 * chain, 2 * other + 3 if small else other + 1)

        @pl.when(hit)
        def _():
            out[slot] = returned[owner]

        @pl.when(jnp.logical_not(hit))
        def _():
            out[slot] = refs[0][slot] if kept else jnp.zeros(out.shape[1:], out.dtype)

        return carry

    lax.fori_loop(0, out.shape[0], one, 0)


def select(place, base, returned, before, small):
    kept = before is not None
    slots = place.shape[0]
    return pl.pallas_call(
        functools.partial(select_kernel, small, kept),
        out_shape=jax.ShapeDtypeStruct((slots,) + returned.shape[1:], returned.dtype),
        in_specs=[SMEM] * 2 + [VMEM] * (1 + kept),
        out_specs=VMEM,
        compiler_params=params(),
    )(place, base, returned, *((before,) if kept else ()))


def swap(array, distance, devices, senders=lambda device: True):
    pairs = [(d, d ^ distance) for d in range(devices) if senders(d)]
    return lax.ppermute(array, "row", pairs)


def share_fields(fields, devices):
    rows, distance = fields.reshape(1, -1), 1
    while distance * 4 < devices:
        rows = jnp.concatenate([rows, swap(rows, distance, devices)])
        distance *= 2
    return [rows] + [swap(rows, far, devices) for far in range(distance, devices, distance)]


def by_chips(walkers, cholesky, slab_index, fields, counts, sources):
    local_rows, columns = walkers.shape[1:]
    per_device = fields.shape[1]
    devices = lax.axis_size("row")
    chips = devices // 2
    me = lax.axis_index("row").reshape(1).astype(jnp.int32)
    lists, place, total = plan(counts, sources, per_device)
    pieces = share_fields(fields, devices)

    def one_pass(small, base, before):
        def rows_of(targets, spread, moved):
            return potential_rows(
                cholesky, slab_index, pieces, moved, lists, me, base, targets, spread,
                per_device, devices,
            )

        def all_targets(step):
            return tuple(target_of(small, step, chips, d) for d in range(devices))

        rows = rows_of(all_targets(0), False, walkers)
        joint = exchange(rows)
        if small:
            late = rows_of(tuple((1, m) for m in range(chips)), True, None)
            parts = [late[0]] + [
                swap(late[m], 2 * m, devices, lambda d: d % 2 == 0)
                for m in range(1, chips)
            ]
            across = [swap(late[m], 2 * m + 1, devices, lambda d: d % 2 == 1) for m in range(chips)]
            current = taylor("first", me, joint, [], [], [], columns)
            moved = swap(current, 2, devices, lambda d: d % 4 == 1)
            advanced = taylor("small", me, joint, parts, across, [current, moved], columns)
        else:
            rows = rows_of(all_targets(1), False, None)
            late = exchange(rows)
            current = taylor("first", me, joint, [], [], [], columns)
            advanced = taylor("large", me, late, [], [], [current], columns)
        returned = exchange(advanced.reshape(devices, local_rows, columns))
        return select(place, base, returned, before, small)

    def small():
        return one_pass(True, jnp.zeros((1,), jnp.int32), None)

    def large():
        def another(turn, before):
            return one_pass(False, jnp.full((1,), turn * devices, jnp.int32), before)

        turns = (total[0] + devices - 1) // devices
        return lax.fori_loop(0, turns, another, jnp.zeros_like(walkers))

    return lax.cond(total[0] <= chips * 3 // 2, small, large)


def exchange(array):
    return lax.all_to_all(array, "row", split_axis=0, concat_axis=0, tiled=True)


def taylor_step(potential, initial):
    summed = initial.astype(jnp.float32)
    term_now = initial
    for degree in range(1, ORDER + 1):
        product = jnp.dot(potential, term_now, preferred_element_type=jnp.float32) / degree
        summed = summed + product
        term_now = product.astype(jnp.bfloat16)
    return summed.astype(jnp.bfloat16)


def by_all_to_alls(walkers, cholesky, slab_index, fields, counts, sources):
    local_rows, columns = walkers.shape[1:]
    orbitals = cholesky.shape[2]
    per_device = fields.shape[1]
    devices = lax.axis_size("row")
    (first, second), place, total = plan(counts, sources, per_device)
    all_fields = lax.all_gather(fields, "row", axis=1, tiled=True)

    def rows_of(chosen, step, base):
        members = lax.dynamic_slice_in_dim(chosen, base, devices)
        vectors = jnp.take(cholesky, slab_index[step], axis=0, mode="clip")
        rows = jnp.dot(
            jnp.take(all_fields[step], members, axis=0, mode="clip"),
            vectors.reshape(vectors.shape[0], -1),
            preferred_element_type=jnp.float32,
        )
        return rows.astype(jnp.bfloat16).reshape(devices, local_rows, orbitals)

    def another(turn, before):
        base = turn * devices
        members = lax.dynamic_slice_in_dim(first, base, devices)
        current = exchange(jnp.take(walkers, members, axis=0, mode="clip"))
        current = current.reshape(orbitals, columns)
        for step, chosen in enumerate((first, second)):
            matrix = exchange(rows_of(chosen, step, base))
            current = taylor_step(matrix.reshape(orbitals, orbitals), current)
        returned = exchange(current.reshape(devices, local_rows, columns))
        own = place - base
        hit = jnp.logical_and(own >= 0, own < devices)
        rows = jnp.take(returned, own, axis=0, mode="clip")
        return jnp.where(hit[:, None, None], rows, before)

    turns = (total[0] + devices - 1) // devices
    return lax.fori_loop(0, turns, another, jnp.zeros_like(walkers))


def on_device(walkers, cholesky, slab_index, fields, counts, sources):
    devices = lax.axis_size("row")
    power = devices & (devices - 1) == 0
    if power and 8 <= devices <= 32 and cholesky.shape[1] % ROWS == 0 and walkers.shape[2] % 128 == 0:
        route = by_chips
    else:
        route = by_all_to_alls
    return route(walkers, cholesky, slab_index, fields, counts, sources)


def solution(mesh):
    in_specs = (
        P("groups", "row", None),
        P("groups", "row", None),
        P("groups", None),
        P(None, ("groups", "row"), None),
        P("groups"),
        P("groups", None),
    )
    out_specs = P("groups", "row", None)
    return jax.shard_map(
        on_device, mesh=mesh, in_specs=in_specs, out_specs=out_specs, check_vma=False
    )
```

time: 392 us -> 163 us (0.42)
  waiting for transfers between devices: 224 us -> 48.6 us
  local copies, waits for them, and re-layouts: 71.6 us -> 2.71 us
  Pallas kernels: 0 us -> 30.4 us
  matrix products: 18.8 us -> 0 us
  other arithmetic: 17.6 us -> 0.02 us
  starting transfers between devices: 39.5 us -> 55.7 us
    all_to_all x6 -> x1, waiting for transfers between devices: 224 us -> 39.1 us  [exchange(): return lax.all_to_all(array, 'row', split_axis=0, concat_axis=0, tiled=True)]
    ppermute x0 -> x21, starting transfers between devices: none -> 46.6 us  [swap(): return lax.ppermute(array, 'row', pairs)]
    unnamed x15 -> x0, local copies, waits for them, and re-layouts: 32.4 us -> none
    pallas_call x0 -> x6, Pallas kernels: none -> 30.4 us  [the longest x2 17.6 us: potential_rows(): pl.pallas_call(functools.partial(potential_kernel, targets, spread, per_d...]
    all_to_all x6 -> x1, starting transfers between devices: 39.5 us -> 9.16 us  [exchange(): return lax.all_to_all(array, 'row', split_axis=0, concat_axis=0, tiled=True)]
    all_to_all x0 -> x1, blocking collectives: none -> 22.9 us  [exchange(): return lax.all_to_all(array, 'row', split_axis=0, concat_axis=0, tiled=True)]
    gather x12 -> x0, local copies, waits for them, and re-layouts: 22.4 us -> none  [the longest x2 15.3 us: on_device(): jnp.take(cholesky, slab_index[step_number], axis=0)]
    all_gather x1 -> x0, blocking collectives: 19 us -> none  [on_device(): all_fields = lax.all_gather(fields, 'row', axis=1, tiled=True)]
  transfers between devices with their start and end apart: 6 -> 22, of which waited for: 5 -> 8; matrix products, arithmetic and copies ran while one was open for 20% -> 0% of each run, Pallas kernels for 0% -> 8%
where the time goes in v2:
time: 163 us; the launch traced here: 161 us
  starting transfers between devices  55.7 us (34%)
  waiting for transfers between devices  48.6 us (30%)
  Pallas kernels  30.4 us (19%)
  blocking collectives  22.9 us (14%)
  local copies, waits for them, and re-layouts  2.71 us (2%)
    ppermute x21, starting transfers between devices, swap(): return lax.ppermute(array, 'row', pairs)  46.6 us
    all_to_all x1, waiting for transfers between devices, exchange(): return lax.all_to_all(array, 'row', split_axis=0, concat_axis=0, tiled=True)  39.1 us
    all_to_all x1, blocking collectives, exchange(): return lax.all_to_all(array, 'row', split_axis=0, concat_axis=0, tiled=True)  22.9 us
    pallas_call x2, Pallas kernels, potential_rows(): pl.pallas_call(functools.partial(potential_kernel, targets, spread, per_d...  17.6 us
    ppermute x21, waiting for transfers between devices, swap(): return lax.ppermute(array, 'row', pairs)  9.47 us
    all_to_all x1, starting transfers between devices, exchange(): return lax.all_to_all(array, 'row', split_axis=0, concat_axis=0, tiled=True)  9.16 us
    pallas_call x2, Pallas kernels, taylor(): pl.pallas_call(functools.partial(taylor_kernel, mode, chips), out_shape=j...  7.63 us
  transfers between devices with their start and end apart: 22, of which 8 were waited for; matrix products, arithmetic and copies ran while one was open for 0% of the time, Pallas kernels for 8%

profile of v2, /device:TPU:9, one launch (start us, length us, event | category | flops | bytes accessed | tf_op | source)
XLA Modules:
  0.0 161.4 jit_solution(18385258683931112330)
XLA Ops:
  0.0 0.8 reshape.19
  0.8 0.7 collective-permute-start.16
  1.4 0.8 collective-permute-done.16
  2.3 1.2 collective-permute-start.17
  3.5 1.2 collective-permute-done.17
  4.7 0.1 collective-permute-start.18
  4.8 2.5 %collective-permute-start.19 = (bf16[4,256]{1,0:T(4,128)(2,1)S(1)}, bf16[4,256]{1,0:T(4,128)(2,1)S(1)}, u32[]{:S(2)}, u32[]{:S(2)}) collective-permute-start(bf16[4,256]{1,0:T(4,128)(2,1)S(1)} %pad_maximum_fusion), channel_id=1, source_target_pairs={{0,8},{1,9},{2,10},{3,11},{4,12},{5,13},{6,14},{7,15},{8,0},{9,1},... | collective-permute-start | bytes 6152 | tf_op jit(solution)/shard_map/ppermute | solution.py:379
  7.3 0.2 collective-permute-start.20
  7.4 3.0 %shard_map.66 = (s32[2,32]{1,0:T(2,128)S(1)}, s32[32]{0:T(128)S(1)}, s32[1]{0:T(128)}) custom-call(s32[16]{0:T(128)} %counts.1, s32[2,32]{1,0:T(2,128)} %sources.1), custom_call_target="tpu_custom_call" | custom-call | tf_op jit(solution)/shard_map/pallas_call | solution.py:68
  11.1 0.0 collective-permute-done.18
  11.1 0.0 collective-permute-done.19
  11.1 0.0 collective-permute-done.20
  11.1 150.3 %conditional.1 = (bf16[32,64,256]{2,1,0:T(8,128)(2,1)}) conditional(s32[]{:T(128)} %bitcast.4, (s32[1]{0:T(128)}, s32[1]{0:T(128)}, s32[2,32]{1,0:T(2,128)S(1)}, s32[2,64]{1,0:T(2,128)}, bf16[4,256]{1,0:T(4,128)(2,1)S(1)}, /*index=5*/bf16[4,256]{1,0:T(4,128)(2,1)S(1)}, bf16[4,256]{1,0:T(4,128)(2,1)S(1)}, bf16[4,256]{1,0:T(4,128)(2,1)S(1)}, ...), branch_computations={%region_0.3_spmd, %region_3.4_spmd} | conditional | flops 8589934592 | bytes 57675684 | solution.py:439
  11.1 0.0 copy-start.9
  11.1 11.5 %branch_1_fun.5 = bf16[16,64,1280]{2,1,0:T(8,128)(2,1)} custom-call(s32[1]{0:T(128)} %get-tuple-element.130.me, s32[2,32]{1,0:T(2,128)S(1)} %get-tuple-element.131.lists, s32[1]{0:T(128)} %constant.34.clone.base, s32[2,64]{1,0:T(2,128)} %get-tuple-element.132.slab, bf16[4,256]{1,0:T(4,128)(2,1)S(1)} %get-tuple-element.133.refs_0_, ...), custom_call_target="tpu_custom_call" | custom-call | flops 2147483648 | bytes 18874368 | tf_op jit(solution)/shard_map/cond/branch_1_fun/pallas_call | solution.py:217
  22.6 0.0 copy-done.9
  22.6 0.0 copy-start.8
  22.6 9.2 %all-to-all-start = ((bf16[16,64,1280]{2,1,0:T(8,128)(2,1)}), bf16[16,64,1280]{2,1,0:T(8,128)(2,1)S(1)}, u32[]{:S(2)}, u32[]{:S(2)}) async-start(bf16[16,64,1280]{2,1,0:T(8,128)(2,1)} %branch_1_fun.5), calls=%async_computation | async-start | bytes 5242880 | tf_op jit(solution)/shard_map/cond/branch_1_fun/all_to_all | solution.py:443
  31.8 0.0 copy-done.8
  31.8 6.1 %branch_1_fun.6 = (bf16[64,1024]{1,0:T(8,128)(2,1)S(1)}, bf16[64,1024]{1,0:T(8,128)(2,1)S(1)}, bf16[64,1024]{1,0:T(8,128)(2,1)S(1)}, bf16[64,1024]{1,0:T(8,128)(...) custom-call(s32[1]{0:T(128)} %get-tuple-element.130.me, ...), custom_call_target="tpu_custom_call" | custom-call | flops 1073741824 | bytes 9437184 | tf_op jit(solution)/shard_map/cond/branch_1_fun/pallas_call | solution.py:217
  38.0 0.0 copy-start
  38.0 0.6 copy-done
  38.6 0.6 copy-done.2
  39.3 0.6 copy-done.4
  39.9 0.7 collective-permute-start
  40.6 0.7 collective-permute-start.1
  41.2 8.1 %collective-permute-start.10 = (bf16[64,1024]{1,0:T(8,128)(2,1)}, bf16[64,1024]{1,0:T(8,128)(2,1)S(1)}, u32[]{:S(2)}, u32[]{:S(2)}) collective-permute-start(bf16[64,1024]{1,0:T(8,128)(2,1)} %get-tuple-element.142), channel_id=1, source_target_pairs={{1,6},{3,4},{5,2},{7,0},{9,14},{11,12},{13,10},{15,8},{17,22},{19,... | collective-permute-start | bytes 393224 | tf_op jit(solution)/shard_map/cond/branch_1_fun/ppermute | solution.py:379
  49.3 39.1 %all-to-all-done.joint = bf16[16,64,1280]{2,1,0:T(8,128)(2,1)S(1)} async-done(((bf16[16,64,1280]{2,1,0:T(8,128)(2,1)}), bf16[16,64,1280]{2,1,0:T(8,128)(2,1)S(1)}, u32[]{:S(2)}, u32[]{:S(2)}) %all-to-all-start) | async-done | bytes 2621472 | tf_op jit(solution)/shard_map/cond/branch_1_fun/all_to_all | solution.py:443
  88.4 3.8 %branch_1_fun.7.refs_16_ = bf16[1024,256]{1,0:T(8,128)(2,1)S(1)} custom-call(s32[1]{0:T(128)} %get-tuple-element.130.me, bf16[16,64,1280]{2,1,0:T(8,128)(2,1)S(1)} %all-to-all-done.joint), custom_call_target="tpu_custom_call" | custom-call | flops 2147483648 | bytes 3670016 | tf_op jit(solution)/shard_map/cond/branch_1_fun/pallas_call | solution.py:318
  92.2 5.2 %collective-permute-start.15 = (bf16[1024,256]{1,0:T(8,128)(2,1)S(1)}, bf16[1024,256]{1,0:T(8,128)(2,1)S(1)}, u32[]{:S(2)}, u32[]{:S(2)}) collective-permute-start(bf16[1024,256]{1,0:T(8,128)(2,1)S(1)} %branch_1_fun.7.refs_16_), channel_id=1, source_target_pairs={{1,3},{5,7},{9,11},{13,15},{17,19},{21,23},{25,27},{29,31}} | collective-permute-start | bytes 1572872 | tf_op jit(solution)/shard_map/cond/branch_1_fun/ppermute | solution.py:379
  97.4 0.0 copy-done.5
  97.4 1.3 collective-permute-start.11
  98.7 0.0 collective-permute-done.refs_1_
  98.7 0.0 copy-done.3
  98.7 1.5 collective-permute-start.12
  100.3 0.0 collective-permute-done.1.refs_2_
  100.3 0.0 copy-done.1
  100.3 1.3 collective-permute-start.13
  101.6 0.0 collective-permute-done.10.refs_11_
  101.6 1.3 collective-permute-start.14
  102.9 3.3 %collective-permute-done.11.refs_12_ = bf16[64,1024]{1,0:T(8,128)(2,1)S(1)} collective-permute-done((bf16[64,1024]{1,0:T(8,128)(2,1)S(1)}, bf16[64,1024]{1,0:T(8,128)(2,1)S(1)}, u32[]{:S(2)}, u32[]{:S(2)}) %collective-permute-start.11) | collective-permute-done | bytes 131104 | tf_op jit(solution)/shard_map/cond/branch_1_fun/ppermute | solution.py:379
  106.2 0.7 collective-permute-start.2
  106.9 0.7 collective-permute-done.12.refs_13_
  107.6 0.7 collective-permute-start.3
  108.3 0.7 collective-permute-done.13.refs_14_
  109.0 0.7 collective-permute-start.4
  109.7 0.7 collective-permute-done.14.refs_15_
  110.4 0.7 collective-permute-start.5
  111.1 0.0 collective-permute-done.2.refs_3_
  111.1 0.7 collective-permute-start.6
  111.8 0.0 collective-permute-done.3.refs_4_
  111.8 15.2 %collective-permute-start.8 = (bf16[64,1024]{1,0:T(8,128)(2,1)S(1)}, bf16[64,1024]{1,0:T(8,128)(2,1)S(1)}, u32[]{:S(2)}, u32[]{:S(2)}) collective-permute-start(bf16[64,1024]{1,0:T(8,128)(2,1)S(1)} %get-tuple-element.140), channel_id=1, source_target_pairs={{1,2},{3,0},{5,6},{7,4},{9,10},{11,8},{13,14},{15,12},{17,18},{19,... | collective-permute-start | bytes 393224 | tf_op jit(solution)/shard_map/cond/branch_1_fun/ppermute | solution.py:379
  127.0 0.0 collective-permute-done.4.refs_5_
  127.0 1.3 collective-permute-start.7
  128.3 0.0 collective-permute-done.5.refs_6_
  128.3 2.2 %collective-permute-start.9 = (bf16[64,1024]{1,0:T(8,128)(2,1)S(1)}, bf16[64,1024]{1,0:T(8,128)(2,1)S(1)}, u32[]{:S(2)}, u32[]{:S(2)}) collective-permute-start(bf16[64,1024]{1,0:T(8,128)(2,1)S(1)} %get-tuple-element.141), channel_id=1, source_target_pairs={{1,4},{3,6},{5,0},{7,2},{9,12},{11,14},{13,8},{15,10},{17,20},{19,... | collective-permute-start | bytes 393224 | tf_op jit(solution)/shard_map/cond/branch_1_fun/ppermute | solution.py:379
  130.5 0.0 collective-permute-done.6.refs_7_
  130.5 0.0 collective-permute-done.7.refs_8_
  130.6 0.0 collective-permute-done.8.refs_9_
  130.6 1.9 %collective-permute-done.9.refs_10_ = bf16[64,1024]{1,0:T(8,128)(2,1)S(1)} collective-permute-done((bf16[64,1024]{1,0:T(8,128)(2,1)S(1)}, bf16[64,1024]{1,0:T(8,128)(2,1)S(1)}, u32[]{:S(2)}, u32[]{:S(2)}) %collective-permute-start.9) | collective-permute-done | bytes 131104 | tf_op jit(solution)/shard_map/cond/branch_1_fun/ppermute | solution.py:379
  132.5 0.0 collective-permute-done.15.refs_17_
  132.5 3.8 %branch_1_fun.8 = bf16[1024,256]{1,0:T(8,128)(2,1)S(1)} custom-call(s32[1]{0:T(128)} %get-tuple-element.130.me, bf16[16,64,1280]{2,1,0:T(8,128)(2,1)S(1)} %all-to-all-done.joint, bf16[64,1024]{1,0:T(8,128)(2,1)S(1)} %get-tuple-element.139.refs_0_, bf16[64,1024]{1,0:T(8,128)(2,1)S(1)} %collective-permute-done.refs_1_, ...), custom_call_target="tpu_custom_call" | custom-call | flops 2147483648 | bytes 3670016 | tf_op jit(solution)/shard_map/cond/branch_1_fun/pallas_call | solution.py:318
  136.3 22.9 %all_to_all.26.returned = bf16[16,64,256]{2,1,0:T(8,128)(2,1)S(1)} all-to-all(bf16[16,64,256]{2,1,0:T(8,128)(2,1)S(1)} %bitcast.10), channel_id=1, replica_groups=mesh['groups'=2,'row'=16] {'row'}, dimensions={0} | all-to-all | bytes 1048576 | tf_op jit(solution)/shard_map/cond/branch_1_fun/all_to_all | solution.py:443
  159.2 2.2 %branch_1_fun.9 = bf16[32,64,256]{2,1,0:T(8,128)(2,1)} custom-call(s32[32]{0:T(128)S(1)} %copy-done.10, s32[1]{0:T(128)} %constant.34.clone.base, bf16[16,64,256]{2,1,0:T(8,128)(2,1)S(1)} %all_to_all.26.returned), custom_call_target="tpu_custom_call" | custom-call | tf_op jit(solution)/shard_map/cond/branch_1_fun/pallas_call | solution.py:368
  (9 shorter events, 0.0 us)
Async XLA Ops:
  0.8 1.5 collective-permute-start.16
  2.3 2.4 %collective-permute-start.17 = (bf16[2,256]{1,0:T(2,128)(2,1)S(1)}, bf16[2,256]{1,0:T(2,128)(2,1)S(1)}, u32[]{:S(2)}, u32[]{:S(2)}) collective-permute-start(bf16[2,256]{1,0:T(2,128)(2,1)S(1)} %pad_maximum_fusion.1), channel_id=1, source_target_pairs={{0,2},{1,3},{2,0},{3,1},{4,6},{5,7},{6,4},{7,5},{8,10},{9,11},{10,... | collective-permute-start | bytes 3080 | tf_op jit(solution)/shard_map/ppermute | solution.py:379
  4.7 6.3 %collective-permute-start.18 = (bf16[4,256]{1,0:T(4,128)(2,1)S(1)}, bf16[4,256]{1,0:T(4,128)(2,1)S(1)}, u32[]{:S(2)}, u32[]{:S(2)}) collective-permute-start(bf16[4,256]{1,0:T(4,128)(2,1)S(1)} %pad_maximum_fusion), channel_id=1, source_target_pairs={{0,4},{1,5},{2,6},{3,7},{4,0},{5,1},{6,2},{7,3},{8,12},{9,13},{10,... | collective-permute-start | bytes 6152 | tf_op jit(solution)/shard_map/ppermute | solution.py:379
  4.8 6.3 %collective-permute-start.19 = (bf16[4,256]{1,0:T(4,128)(2,1)S(1)}, bf16[4,256]{1,0:T(4,128)(2,1)S(1)}, u32[]{:S(2)}, u32[]{:S(2)}) collective-permute-start(bf16[4,256]{1,0:T(4,128)(2,1)S(1)} %pad_maximum_fusion), channel_id=1, source_target_pairs={{0,8},{1,9},{2,10},{3,11},{4,12},{5,13},{6,14},{7,15},{8,0},{9,1},... | collective-permute-start | bytes 6152 | tf_op jit(solution)/shard_map/ppermute | solution.py:379
  7.3 3.8 %collective-permute-start.20 = (bf16[4,256]{1,0:T(4,128)(2,1)S(1)}, bf16[4,256]{1,0:T(4,128)(2,1)S(1)}, u32[]{:S(2)}, u32[]{:S(2)}) collective-permute-start(bf16[4,256]{1,0:T(4,128)(2,1)S(1)} %pad_maximum_fusion), channel_id=1, source_target_pairs={{0,12},{1,13},{2,14},{3,15},{4,8},{5,9},{6,10},{7,11},{8,4},{9,5},... | collective-permute-start | bytes 6152 | tf_op jit(solution)/shard_map/ppermute | solution.py:379
  11.1 11.5 %copy-start.9 = (s32[32]{0:T(128)}, s32[32]{0:T(128)S(1)}, u32[]{:S(2)}) copy-start(s32[32]{0:T(128)S(1)} %get-tuple-element.129.place) | copy-start | bytes 388 | tf_op jit(solution)/shard_map/cond
  22.6 9.2 %copy-start.8 = (s32[2,64]{1,0:T(2,128)S(1)}, s32[2,64]{1,0:T(2,128)}, u32[]{:S(2)}) copy-start(s32[2,64]{1,0:T(2,128)} %get-tuple-element.132.slab) | copy-start | bytes 1540 | tf_op jit(solution)/shard_map/cond
  22.6 65.8 %all-to-all-start = ((bf16[16,64,1280]{2,1,0:T(8,128)(2,1)}), bf16[16,64,1280]{2,1,0:T(8,128)(2,1)S(1)}, u32[]{:S(2)}, u32[]{:S(2)}) async-start(bf16[16,64,1280]{2,1,0:T(8,128)(2,1)} %branch_1_fun.5), calls=%async_computation | async-start | bytes 5242880 | tf_op jit(solution)/shard_map/cond/branch_1_fun/all_to_all | solution.py:443
  38.0 0.6 copy-start
  38.6 0.6 copy-start.2
  39.2 0.6 copy-start.4
  39.9 58.8 %collective-permute-start = (bf16[64,1024]{1,0:T(8,128)(2,1)S(1)}, bf16[64,1024]{1,0:T(8,128)(2,1)S(1)}, u32[]{:S(2)}, u32[]{:S(2)}) collective-permute-start(bf16[64,1024]{1,0:T(8,128)(2,1)S(1)} %get-tuple-element.140), channel_id=1, source_target_pairs={{0,2},{2,0},{4,6},{6,4},{8,10},{10,8},{12,14},{14,12},{16,18},{18,... | collective-permute-start | bytes 393224 | tf_op jit(solution)/shard_map/cond/branch_1_fun/ppermute | solution.py:379
  40.6 59.7 %collective-permute-start.1 = (bf16[64,1024]{1,0:T(8,128)(2,1)S(1)}, bf16[64,1024]{1,0:T(8,128)(2,1)S(1)}, u32[]{:S(2)}, u32[]{:S(2)}) collective-permute-start(bf16[64,1024]{1,0:T(8,128)(2,1)S(1)} %get-tuple-element.141), channel_id=1, source_target_pairs={{0,4},{2,6},{4,0},{6,2},{8,12},{10,14},{12,8},{14,10},{16,20},{18,... | collective-permute-start | bytes 393224 | tf_op jit(solution)/shard_map/cond/branch_1_fun/ppermute | solution.py:379
  41.2 60.4 %collective-permute-start.10 = (bf16[64,1024]{1,0:T(8,128)(2,1)}, bf16[64,1024]{1,0:T(8,128)(2,1)S(1)}, u32[]{:S(2)}, u32[]{:S(2)}) collective-permute-start(bf16[64,1024]{1,0:T(8,128)(2,1)} %get-tuple-element.142), channel_id=1, source_target_pairs={{1,6},{3,4},{5,2},{7,0},{9,14},{11,12},{13,10},{15,8},{17,22},{19,... | collective-permute-start | bytes 393224 | tf_op jit(solution)/shard_map/cond/branch_1_fun/ppermute | solution.py:379
  88.4 9.0 %copy-start.5 = (bf16[64,1024]{1,0:T(8,128)(2,1)S(1)}, bf16[64,1024]{1,0:T(8,128)(2,1)}, u32[]{:S(2)}) copy-start(bf16[64,1024]{1,0:T(8,128)(2,1)} %copy-done.4) | copy-start | bytes 393220 | tf_op jit(solution)/shard_map/cond
  88.4 10.3 %copy-start.3 = (bf16[64,1024]{1,0:T(8,128)(2,1)S(1)}, bf16[64,1024]{1,0:T(8,128)(2,1)}, u32[]{:S(2)}) copy-start(bf16[64,1024]{1,0:T(8,128)(2,1)} %copy-done.2) | copy-start | bytes 393220 | tf_op jit(solution)/shard_map/cond
  88.4 11.9 %copy-start.1 = (bf16[64,1024]{1,0:T(8,128)(2,1)S(1)}, bf16[64,1024]{1,0:T(8,128)(2,1)}, u32[]{:S(2)}) copy-start(bf16[64,1024]{1,0:T(8,128)(2,1)} %copy-done) | copy-start | bytes 393220 | tf_op jit(solution)/shard_map/cond
  92.2 40.2 %collective-permute-start.15 = (bf16[1024,256]{1,0:T(8,128)(2,1)S(1)}, bf16[1024,256]{1,0:T(8,128)(2,1)S(1)}, u32[]{:S(2)}, u32[]{:S(2)}) collective-permute-start(bf16[1024,256]{1,0:T(8,128)(2,1)S(1)} %branch_1_fun.7.refs_16_), channel_id=1, source_target_pairs={{1,3},{5,7},{9,11},{13,15},{17,19},{21,23},{25,27},{29,31}} | collective-permute-start | bytes 1572872 | tf_op jit(solution)/shard_map/cond/branch_1_fun/ppermute | solution.py:379
  97.4 8.8 %collective-permute-start.11 = (bf16[64,1024]{1,0:T(8,128)(2,1)S(1)}, bf16[64,1024]{1,0:T(8,128)(2,1)S(1)}, u32[]{:S(2)}, u32[]{:S(2)}) collective-permute-start(bf16[64,1024]{1,0:T(8,128)(2,1)S(1)} %copy-done.5), channel_id=1, source_target_pairs={{1,8},{3,10},{5,12},{7,14},{9,0},{11,2},{13,4},{15,6},{17,24},{19,... | collective-permute-start | bytes 393224 | tf_op jit(solution)/shard_map/cond/branch_1_fun/ppermute | solution.py:379
  98.7 8.9 %collective-permute-start.12 = (bf16[64,1024]{1,0:T(8,128)(2,1)S(1)}, bf16[64,1024]{1,0:T(8,128)(2,1)S(1)}, u32[]{:S(2)}, u32[]{:S(2)}) collective-permute-start(bf16[64,1024]{1,0:T(8,128)(2,1)S(1)} %copy-done.3), channel_id=1, source_target_pairs={{1,10},{3,8},{5,14},{7,12},{9,2},{11,0},{13,6},{15,4},{17,26},{19,... | collective-permute-start | bytes 393224 | tf_op jit(solution)/shard_map/cond/branch_1_fun/ppermute | solution.py:379
  100.3 8.7 %collective-permute-start.13 = (bf16[64,1024]{1,0:T(8,128)(2,1)S(1)}, bf16[64,1024]{1,0:T(8,128)(2,1)S(1)}, u32[]{:S(2)}, u32[]{:S(2)}) collective-permute-start(bf16[64,1024]{1,0:T(8,128)(2,1)S(1)} %copy-done.1), channel_id=1, source_target_pairs={{1,12},{3,14},{5,8},{7,10},{9,4},{11,6},{13,0},{15,2},{17,28},{19,... | collective-permute-start | bytes 393224 | tf_op jit(solution)/shard_map/cond/branch_1_fun/ppermute | solution.py:379
  101.6 8.8 %collective-permute-start.14 = (bf16[64,1024]{1,0:T(8,128)(2,1)S(1)}, bf16[64,1024]{1,0:T(8,128)(2,1)S(1)}, u32[]{:S(2)}, u32[]{:S(2)}) collective-permute-start(bf16[64,1024]{1,0:T(8,128)(2,1)S(1)} %get-tuple-element.146), channel_id=1, source_target_pairs={{1,14},{3,12},{5,10},{7,8},{9,6},{11,4},{13,2},{15,0},{17,30},{19,... | collective-permute-start | bytes 393224 | tf_op jit(solution)/shard_map/cond/branch_1_fun/ppermute | solution.py:379
  106.2 4.9 %collective-permute-start.2 = (bf16[64,1024]{1,0:T(8,128)(2,1)}, bf16[64,1024]{1,0:T(8,128)(2,1)S(1)}, u32[]{:S(2)}, u32[]{:S(2)}) collective-permute-start(bf16[64,1024]{1,0:T(8,128)(2,1)} %get-tuple-element.142), channel_id=1, source_target_pairs={{0,6},{2,4},{4,2},{6,0},{8,14},{10,12},{12,10},{14,8},{16,22},{18,... | collective-permute-start | bytes 393224 | tf_op jit(solution)/shard_map/cond/branch_1_fun/ppermute | solution.py:379
  107.6 4.2 %collective-permute-start.3 = (bf16[64,1024]{1,0:T(8,128)(2,1)S(1)}, bf16[64,1024]{1,0:T(8,128)(2,1)S(1)}, u32[]{:S(2)}, u32[]{:S(2)}) collective-permute-start(bf16[64,1024]{1,0:T(8,128)(2,1)S(1)} %copy-done.5), channel_id=1, source_target_pairs={{0,8},{2,10},{4,12},{6,14},{8,0},{10,2},{12,4},{14,6},{16,24},{18,... | collective-permute-start | bytes 393224 | tf_op jit(solution)/shard_map/cond/branch_1_fun/ppermute | solution.py:379
  109.0 18.0 %collective-permute-start.4 = (bf16[64,1024]{1,0:T(8,128)(2,1)S(1)}, bf16[64,1024]{1,0:T(8,128)(2,1)S(1)}, u32[]{:S(2)}, u32[]{:S(2)}) collective-permute-start(bf16[64,1024]{1,0:T(8,128)(2,1)S(1)} %copy-done.3), channel_id=1, source_target_pairs={{0,10},{2,8},{4,14},{6,12},{8,2},{10,0},{12,6},{14,4},{16,26},{18,... | collective-permute-start | bytes 393224 | tf_op jit(solution)/shard_map/cond/branch_1_fun/ppermute | solution.py:379
  110.4 17.9 %collective-permute-start.5 = (bf16[64,1024]{1,0:T(8,128)(2,1)S(1)}, bf16[64,1024]{1,0:T(8,128)(2,1)S(1)}, u32[]{:S(2)}, u32[]{:S(2)}) collective-permute-start(bf16[64,1024]{1,0:T(8,128)(2,1)S(1)} %copy-done.1), channel_id=1, source_target_pairs={{0,12},{2,14},{4,8},{6,10},{8,4},{10,6},{12,0},{14,2},{16,28},{18,... | collective-permute-start | bytes 393224 | tf_op jit(solution)/shard_map/cond/branch_1_fun/ppermute | solution.py:379
  111.1 19.4 %collective-permute-start.6 = (bf16[64,1024]{1,0:T(8,128)(2,1)S(1)}, bf16[64,1024]{1,0:T(8,128)(2,1)S(1)}, u32[]{:S(2)}, u32[]{:S(2)}) collective-permute-start(bf16[64,1024]{1,0:T(8,128)(2,1)S(1)} %get-tuple-element.146), channel_id=1, source_target_pairs={{0,14},{2,12},{4,10},{6,8},{8,6},{10,4},{12,2},{14,0},{16,30},{18,... | collective-permute-start | bytes 393224 | tf_op jit(solution)/shard_map/cond/branch_1_fun/ppermute | solution.py:379
  111.8 18.8 %collective-permute-start.8 = (bf16[64,1024]{1,0:T(8,128)(2,1)S(1)}, bf16[64,1024]{1,0:T(8,128)(2,1)S(1)}, u32[]{:S(2)}, u32[]{:S(2)}) collective-permute-start(bf16[64,1024]{1,0:T(8,128)(2,1)S(1)} %get-tuple-element.140), channel_id=1, source_target_pairs={{1,2},{3,0},{5,6},{7,4},{9,10},{11,8},{13,14},{15,12},{17,18},{19,... | collective-permute-start | bytes 393224 | tf_op jit(solution)/shard_map/cond/branch_1_fun/ppermute | solution.py:379
  127.0 32.2 %copy-start.10 = (s32[32]{0:T(128)S(1)}, s32[32]{0:T(128)}, u32[]{:S(2)}) copy-start(s32[32]{0:T(128)} %copy-done.9) | copy-start | bytes 388 | tf_op jit(solution)/shard_map/cond
  127.0 3.5 %collective-permute-start.7 = (bf16[64,1024]{1,0:T(8,128)(2,1)S(1)}, bf16[64,1024]{1,0:T(8,128)(2,1)S(1)}, u32[]{:S(2)}, u32[]{:S(2)}) collective-permute-start(bf16[64,1024]{1,0:T(8,128)(2,1)S(1)} %get-tuple-element.139.refs_0_), channel_id=1, source_target_pairs={{1,0},{3,2},{5,4},{7,6},{9,8},{11,10},{13,12},{15,14},{17,16},{19,... | collective-permute-start | bytes 393224 | tf_op jit(solution)/shard_map/cond/branch_1_fun/ppermute | solution.py:379
  128.3 4.1 %collective-permute-start.9 = (bf16[64,1024]{1,0:T(8,128)(2,1)S(1)}, bf16[64,1024]{1,0:T(8,128)(2,1)S(1)}, u32[]{:S(2)}, u32[]{:S(2)}) collective-permute-start(bf16[64,1024]{1,0:T(8,128)(2,1)S(1)} %get-tuple-element.141), channel_id=1, source_target_pairs={{1,4},{3,6},{5,0},{7,2},{9,12},{11,14},{13,8},{15,10},{17,20},{19,... | collective-permute-start | bytes 393224 | tf_op jit(solution)/shard_map/cond/branch_1_fun/ppermute | solution.py:379

commit v3 on v2

--- a/solution.py
+++ b/solution.py
@@ -19,11 +19,15 @@
     return pltpu.CompilerParams(vmem_limit_bytes=mebibytes << 20)
 
 
-def plan_kernel(per_device, counts, sources, lists, place, total, order):
-    slots = place.shape[0]
+def plan_kernel(
+    per_device, counts, sources, lists, place, jobs, owned, total, order, lead, twin, owner
+):
+    slots, devices = place.shape[0], counts.shape[0]
+    chips = devices // 2
 
     def clear(slot, carry):
         order[slot] = -1
+        lead[slot] = -1
         lists[0, slot] = 0
         lists[1, slot] = 0
         return carry
@@ -43,49 +47,114 @@
     lax.fori_loop(0, slots, mark, 0)
 
     def number(slot, found):
+        count, twins = found
         kept = order[slot] >= 0
+        start = sources[0, slot]
+        other = lead[start]
+        paired = jnp.logical_and(kept, other >= 0)
 
         @pl.when(kept)
         def _():
-            order[slot] = found
-            lists[0, found] = sources[0, slot]
-            lists[1, found] = slot
-
-        return found + kept.astype(jnp.int32)
-
-    total[0] = lax.fori_loop(0, slots, number, jnp.int32(0))
+            order[slot] = count
+            lists[0, count] = start
+            lists[1, count] = slot
+
+        @pl.when(paired)
+        def _():
+            twin[other] = count
+            twin[count] = -2
+            lead[start] = -1
+
+        @pl.when(jnp.logical_and(kept, other < 0))
+        def _():
+            twin[count] = -1
+            lead[start] = count
+
+        return count + kept.astype(jnp.int32), twins + paired.astype(jnp.int32)
+
+    count, twins = lax.fori_loop(0, slots, number, (jnp.int32(0), jnp.int32(0)))
+    total[0] = count
+    leads, pair = count - twins, (twins + 1) // 2
+    fits = leads - chips <= jnp.maximum(chips // 2 - pair, 0)
+    total[1] = fits.astype(jnp.int32)
+
+    def empty(device, carry):
+        for row in range(4):
+            jobs[row, device] = 0
+        return carry
+
+    lax.fori_loop(0, devices, empty, 0)
+
+    @pl.when(fits)
+    def _():
+        def assign(chain, taken):
+            with_twin, without, more = taken
+            other = twin[chain]
+            leading = other > -2
+            doubled = other >= 0
+            single = other == -1
+            chip = jnp.where(doubled, with_twin, without)
+            inside = jnp.logical_and(leading, chip < chips)
+            outside = jnp.logical_and(single, chip >= chips)
+
+            @pl.when(inside)
+            def _():
+                jobs[1, 2 * chip] = lists[0, chain]
+                jobs[2, chip] = lists[1, chain]
+                owner[chain] = 2 * chip
+
+            @pl.when(doubled)
+            def _():
+                jobs[0, 2 * chip + 1] = 1
+                jobs[1, 2 * chip + 1] = lists[1, other]
+                jobs[3, chip] = 1
+                owner[other] = 2 * chip + 1
+
+            @pl.when(outside)
+            def _():
+                jobs[1, 4 * more + 1] = lists[0, chain]
+                jobs[0, 4 * more + 3] = 1
+                jobs[1, 4 * more + 3] = lists[1, chain]
+                owner[chain] = 4 * more + 3
+
+            return (
+                with_twin + doubled.astype(jnp.int32),
+                without + jnp.logical_and(single, inside).astype(jnp.int32),
+                more + outside.astype(jnp.int32),
+            )
+
+        lax.fori_loop(0, count, assign, (jnp.int32(0), twins, pair))
 
     def look(slot, carry):
-        place[slot] = jnp.where(alive(slot), order[sources[1, slot]], -1)
+        chain = jnp.where(alive(slot), order[sources[1, slot]], -1)
+        place[slot] = chain
+        owned[slot] = jnp.where(
+            jnp.logical_and(chain >= 0, fits), owner[jnp.maximum(chain, 0)], -1
+        )
         return carry
 
     lax.fori_loop(0, slots, look, 0)
 
 
 def plan(counts, sources, per_device):
-    slots = sources.shape[1]
+    slots, devices = sources.shape[1], counts.shape[0]
     vector = jax.ShapeDtypeStruct((slots,), jnp.int32)
     return pl.pallas_call(
         functools.partial(plan_kernel, per_device),
         out_shape=(
             jax.ShapeDtypeStruct((2, slots), jnp.int32),
             vector,
-            jax.ShapeDtypeStruct((1,), jnp.int32),
+            jax.ShapeDtypeStruct((4, devices), jnp.int32),
+            vector,
+            jax.ShapeDtypeStruct((2,), jnp.int32),
         ),
         in_specs=[SMEM, SMEM],
-        out_specs=(SMEM, SMEM, SMEM),
-        scratch_shapes=[pltpu.SMEM((slots,), jnp.int32)],
+        out_specs=(SMEM,) * 5,
+        scratch_shapes=[pltpu.SMEM((slots,), jnp.int32)] * 4,
     )(counts, sources)
 
 
-def target_of(small, step, chips, device):
-    chip, core = device // 2, device % 2
-    if small and core:
-        return chip % 2, chips + chip // 2
-    return step, chip + core * chips
-
-
-def potential_kernel(targets, spread, per_device, pieces, walked, me, lists, base, slab, *refs):
+def potential_kernel(kind, step, per_device, pieces, walked, me, jobs, base, slab, *refs):
     fields, refs = refs[:pieces], refs[pieces:]
     cholesky, refs = refs[0], refs[1:]
     walkers, refs = (refs[0], refs[1:]) if walked else (None, refs)
@@ -93,7 +162,7 @@
     blocks, left, held, semaphores = scratch[:4]
     picked = scratch[4] if walked else None
     outs = refs[: -4 - walked]
-    steps = sorted({step for step, _ in targets})
+    steps = (0, 1) if kind == "mixed" else (step,)
     vectors = blocks.shape[1]
     halves = semaphores.shape[0] - 1
     half_rows = blocks.shape[2] // halves
@@ -101,11 +170,16 @@
     devices = held.shape[0]
     block = pl.program_id(0)
 
+    members = {0: range(devices), 1: range(1, devices, 2)}
+    if kind != "mixed":
+        members = {step: range(devices if kind == "all" else devices // 2)}
+
     def slot_of(number):
-        step, chain = targets[number]
-        if spread:
-            chain = (me[0] // 2) ^ chain
-        return lists[step, base[0] + chain]
+        if kind == "all":
+            return jobs[step, base[0] + number // 2 + number % 2 * (devices // 2)]
+        if kind == "mixed":
+            return jobs[1, number]
+        return jobs[2, (me[0] // 2) ^ number]
 
     @pl.when(block == 0)
     def _():
@@ -123,7 +197,7 @@
 
                 lax.fori_loop(0, vectors, one, 0, unroll=8)
         if walked:
-            for number in range(len(targets)):
+            for number in range(devices):
                 pltpu.make_async_copy(
                     walkers.at[slot_of(number)], picked.at[number], semaphores.at[halves]
                 ).start()
@@ -136,20 +210,21 @@
         )
         widen = widen.astype(jnp.float32).astype(jnp.bfloat16)
         start = 0
-        for step in steps:
-            members = [number for number, target in enumerate(targets) if target[0] == step]
-            shape = (len(members) * ROWS, devices)
+        for now in steps:
+            shape = (len(members[now]) * ROWS, devices)
             row = lax.broadcasted_iota(jnp.int32, shape, 0) // ROWS
             column = lax.broadcasted_iota(jnp.int32, shape, 1)
             wanted = jnp.zeros(shape, jnp.int32)
-            for place, number in enumerate(members):
+            for place, number in enumerate(members[now]):
                 slot = slot_of(number)
                 there = ((slot // per_device) ^ me[0]) * per_device + slot % per_device
+                if kind == "mixed":
+                    there = jnp.where(jobs[0, number] == now, there, -1)
                 wanted = jnp.where(row == place, there, wanted)
             repeated = jnp.zeros((shape[0], vectors), jnp.float32)
             for within in range(per_device):
                 rows_of = (wanted == column * per_device + within).astype(jnp.float32)
-                first = (step * per_device + within) * vectors
+                first = (now * per_device + within) * vectors
                 repeated = repeated + jnp.dot(
                     rows_of.astype(jnp.bfloat16),
                     held[:, first : first + vectors].astype(jnp.bfloat16),
@@ -175,48 +250,55 @@
             pltpu.make_async_copy(view, view, semaphores.at[half]).wait()
 
     rows = pl.ds(block * ROWS, ROWS)
-    start = 0
-    for which, step in enumerate(steps):
-        members = [number for number, target in enumerate(targets) if target[0] == step]
+
+    def product(which, first, count):
         right = blocks[which, :, rows, :].reshape(vectors * ROWS, orbitals)
-        end = start + len(members) * ROWS
-        product = jnp.dot(
-            left[start:end, :], right, preferred_element_type=jnp.float32
-        ).astype(jnp.bfloat16)
-        start = end
-        for place, number in enumerate(members):
-            out = outs[number] if spread else outs[0].at[number]
-            out[:, :orbitals] = product[place * ROWS : (place + 1) * ROWS]
-            if walked:
-                out[:, orbitals:] = picked[number, rows, :]
+        return jnp.dot(
+            left[first : first + count * ROWS, :], right, preferred_element_type=jnp.float32
+        )
+
+    count = len(members[steps[0]])
+    made = product(0, 0, count)
+    if kind == "mixed":
+        second = product(1, count * ROWS, len(members[1]))
+    for number in range(count):
+        value = made[number * ROWS : (number + 1) * ROWS]
+        if kind == "mixed" and number % 2:
+            value = value + second[number // 2 * ROWS : (number // 2 + 1) * ROWS]
+        out = outs[number] if kind == "chips" else outs[0].at[number]
+        out[:, :orbitals] = value.astype(jnp.bfloat16)
+        if walked:
+            out[:, orbitals:] = picked[number, rows, :]
 
 
 def potential_rows(
-    cholesky, slab, fields, walkers, lists, me, base, targets, spread, per_device, devices
+    cholesky, slab, fields, walkers, jobs, me, base, kind, step, per_device, devices
 ):
     local_rows, orbitals = cholesky.shape[1:]
     vectors = slab.shape[1]
-    count = len({step for step, _ in targets})
+    count = 2 if kind == "mixed" else 1
+    targets = devices // 2 if kind == "chips" else devices
+    made = targets + (devices // 2 if kind == "mixed" else 0)
     walked = walkers is not None
     width = orbitals + (walkers.shape[2] if walked else 0)
     halves = 2 if local_rows % (2 * ROWS) == 0 else 1
     scratch = [
         pltpu.VMEM((count, vectors, local_rows, orbitals), jnp.bfloat16),
-        pltpu.VMEM((len(targets) * ROWS, vectors * ROWS), jnp.bfloat16),
+        pltpu.VMEM((made * ROWS, vectors * ROWS), jnp.bfloat16),
         pltpu.VMEM((devices, fields[0].shape[1]), jnp.float32),
         pltpu.SemaphoreType.DMA((halves + 1,)),
     ]
     if walked:
-        scratch.append(pltpu.VMEM((len(targets),) + walkers.shape[1:], jnp.bfloat16))
-    if spread:
-        shapes = [jax.ShapeDtypeStruct((local_rows, width), jnp.bfloat16)] * len(targets)
-        specs = [pl.BlockSpec((ROWS, width), lambda block: (block, 0))] * len(targets)
+        scratch.append(pltpu.VMEM((targets,) + walkers.shape[1:], jnp.bfloat16))
+    if kind == "chips":
+        shapes = [jax.ShapeDtypeStruct((local_rows, width), jnp.bfloat16)] * targets
+        specs = [pl.BlockSpec((ROWS, width), lambda block: (block, 0))] * targets
     else:
-        shapes = jax.ShapeDtypeStruct((len(targets), local_rows, width), jnp.bfloat16)
-        specs = pl.BlockSpec((len(targets), ROWS, width), lambda block: (0, block, 0))
+        shapes = jax.ShapeDtypeStruct((targets, local_rows, width), jnp.bfloat16)
+        specs = pl.BlockSpec((targets, ROWS, width), lambda block: (0, block, 0))
     return pl.pallas_call(
         functools.partial(
-            potential_kernel, targets, spread, per_device, len(fields), walked
+            potential_kernel, kind, step, per_device, len(fields), walked
         ),
         out_shape=shapes,
         grid=(local_rows // ROWS,),
@@ -224,20 +306,19 @@
         out_specs=specs,
         scratch_shapes=scratch,
         cost_estimate=pl.CostEstimate(
-            flops=2 * len(targets) * ROWS * vectors * local_rows * orbitals,
-            bytes_accessed=2 * (count * vectors + len(targets)) * local_rows * orbitals,
+            flops=2 * made * ROWS * vectors * local_rows * orbitals,
+            bytes_accessed=2 * (count * vectors + targets) * local_rows * orbitals,
             transcendentals=0,
         ),
         compiler_params=params(),
-    )(me, lists, base, slab, *fields, cholesky, *((walkers,) if walked else ()))
-
-
-def taylor_kernel(mode, chips, me, joint, *refs):
+    )(me, jobs, base, slab, *fields, cholesky, *((walkers,) if walked else ()))
+
+
+def taylor_kernel(mode, chips, me, jobs, joint, *refs):
     parts, refs = (refs[:chips], refs[chips:]) if mode == "small" else ((), refs)
     across, refs = (refs[: chips], refs[chips:]) if mode == "small" else ((), refs)
-    starts, refs = refs[: {"first": 0, "large": 1, "small": 2}[mode]], refs[
-        {"first": 0, "large": 1, "small": 2}[mode] :
-    ]
+    count = {"first": 0, "large": 1, "small": 3}[mode]
+    starts, refs = refs[:count], refs[count:]
     out, matrix, begun, summed, term, semaphores, ready = refs
     devices, local = joint.shape[:2]
     rows, columns = summed.shape
@@ -284,7 +365,9 @@
 
         @pl.when(jnp.logical_not(own))
         def _():
-            copy_begun(starts[1])
+            twin = jobs[3, me[0] // 2] == 1
+            pl.when(twin)(lambda: copy_begun(starts[1]))
+            pl.when(jnp.logical_not(twin))(lambda: copy_begun(starts[2]))
             for number in range(tiles):
                 copy_joint(number)
     else:
@@ -311,14 +394,14 @@
                 out[span, :] = (before + product).astype(jnp.bfloat16)
 
 
-def taylor(mode, me, joint, parts, across, starts, columns):
+def taylor(mode, me, jobs, joint, parts, across, starts, columns):
     devices, local = joint.shape[:2]
     rows = devices * local
     chips = devices // 2
     return pl.pallas_call(
         functools.partial(taylor_kernel, mode, chips),
         out_shape=jax.ShapeDtypeStruct((rows, columns), jnp.bfloat16),
-        in_specs=[SMEM] + [ANY] * (1 + len(parts) + len(across) + len(starts)),
+        in_specs=[SMEM] * 2 + [ANY] * (1 + len(parts) + len(across) + len(starts)),
         out_specs=VMEM,
         scratch_shapes=[
             pltpu.VMEM((rows, rows), jnp.bfloat16),
@@ -334,20 +417,19 @@
             transcendentals=0,
         ),
         compiler_params=params(),
-    )(me, joint, *parts, *across, *starts)
+    )(me, jobs, joint, *parts, *across, *starts)
 
 
 def select_kernel(small, kept, place, base, returned, *refs):
     out = refs[-1]
-    chips = returned.shape[0] // 2
-    capacity = chips * 3 // 2 if small else chips * 2
+    devices = returned.shape[0]
 
     def one(slot, carry):
         chain = place[slot] - base[0]
-        hit = jnp.logical_and(chain >= 0, chain < capacity)
-        chain = jnp.clip(chain, 0, capacity - 1)
-        other = 2 * (chain - chips)
-        owner = jnp.where(chain < chips, 2 * chain, 2 * other + 3 if small else other + 1)
+        hit = jnp.logical_and(chain >= 0, chain < devices)
+        owner = jnp.clip(chain, 0, devices - 1)
+        if not small:
+            owner = owner % (devices // 2) * 2 + owner // (devices // 2)
 
         @pl.when(hit)
         def _():
@@ -364,10 +446,10 @@
 
 def select(place, base, returned, before, small):
     kept = before is not None
-    slots = place.shape[0]
+    shape = place.shape + returned.shape[1:]
     return pl.pallas_call(
         functools.partial(select_kernel, small, kept),
-        out_shape=jax.ShapeDtypeStruct((slots,) + returned.shape[1:], returned.dtype),
+        out_shape=jax.ShapeDtypeStruct(shape, returned.dtype),
         in_specs=[SMEM] * 2 + [VMEM] * (1 + kept),
         out_specs=VMEM,
         compiler_params=params(),
@@ -393,38 +475,37 @@
     devices = lax.axis_size("row")
     chips = devices // 2
     me = lax.axis_index("row").reshape(1).astype(jnp.int32)
-    lists, place, total = plan(counts, sources, per_device)
+    lists, place, jobs, owned, total = plan(counts, sources, per_device)
     pieces = share_fields(fields, devices)
 
     def one_pass(small, base, before):
-        def rows_of(targets, spread, moved):
+        def rows_of(kind, step, moved):
             return potential_rows(
-                cholesky, slab_index, pieces, moved, lists, me, base, targets, spread,
-                per_device, devices,
+                cholesky, slab_index, pieces, moved, lists if kind == "all" else jobs, me,
+                base, kind, step, per_device, devices,
             )
 
-        def all_targets(step):
-            return tuple(target_of(small, step, chips, d) for d in range(devices))
-
-        rows = rows_of(all_targets(0), False, walkers)
+        rows = rows_of("mixed" if small else "all", 0, walkers)
         joint = exchange(rows)
         if small:
-            late = rows_of(tuple((1, m) for m in range(chips)), True, None)
+            late = rows_of("chips", 1, None)
             parts = [late[0]] + [
                 swap(late[m], 2 * m, devices, lambda d: d % 2 == 0)
                 for m in range(1, chips)
             ]
             across = [swap(late[m], 2 * m + 1, devices, lambda d: d % 2 == 1) for m in range(chips)]
-            current = taylor("first", me, joint, [], [], [], columns)
+            current = taylor("first", me, jobs, joint, [], [], [], columns)
+            twin = swap(current, 1, devices, lambda d: d % 2 == 0)
             moved = swap(current, 2, devices, lambda d: d % 4 == 1)
-            advanced = taylor("small", me, joint, parts, across, [current, moved], columns)
+            starts = [current, twin, moved]
+            advanced = taylor("small", me, jobs, joint, parts, across, starts, columns)
         else:
-            rows = rows_of(all_targets(1), False, None)
+            rows = rows_of("all", 1, None)
             late = exchange(rows)
-            current = taylor("first", me, joint, [], [], [], columns)
-            advanced = taylor("large", me, late, [], [], [current], columns)
+            current = taylor("first", me, jobs, joint, [], [], [], columns)
+            advanced = taylor("large", me, jobs, late, [], [], [current], columns)
         returned = exchange(advanced.reshape(devices, local_rows, columns))
-        return select(place, base, returned, before, small)
+        return select(owned if small else place, base, returned, before, small)
 
     def small():
         return one_pass(True, jnp.zeros((1,), jnp.int32), None)
@@ -436,7 +517,7 @@
         turns = (total[0] + devices - 1) // devices
         return lax.fori_loop(0, turns, another, jnp.zeros_like(walkers))
 
-    return lax.cond(total[0] <= chips * 3 // 2, small, large)
+    return lax.cond(total[1] == 1, small, large)
 
 
 def exchange(array):
@@ -458,7 +539,7 @@
     orbitals = cholesky.shape[2]
     per_device = fields.shape[1]
     devices = lax.axis_size("row")
-    (first, second), place, total = plan(counts, sources, per_device)
+    (first, second), place, _, _, total = plan(counts, sources, per_device)
     all_fields = lax.all_gather(fields, "row", axis=1, tiled=True)
 
     def rows_of(chosen, step, base):

time: 163 us -> 166 us (1.018)
  starting transfers between devices: 55.7 us -> 62.9 us
  waiting for transfers between devices: 48.6 us -> 43 us
  Pallas kernels: 30.4 us -> 33 us
    ppermute x21 -> x22, starting transfers between devices: 46.6 us -> 53.8 us  [swap(): return lax.ppermute(array, 'row', pairs)]
    ppermute x21 -> x22, waiting for transfers between devices: 9.47 us -> 4.54 us  [swap(): return lax.ppermute(array, 'row', pairs)]
  transfers between devices with their start and end apart: 22 -> 23, of which waited for: 8 -> 5; matrix products, arithmetic and copies ran while one was open for 0% -> 0% of each run, Pallas kernels for 8% -> 9%
where the time goes in v3:
time: 166 us; the launch traced here: 164 us
  starting transfers between devices  62.9 us (38%)
  waiting for transfers between devices  43 us (26%)
  Pallas kernels  33 us (20%)
  blocking collectives  22.3 us (13%)
  local copies, waits for them, and re-layouts  2.02 us (1%)
    ppermute x22, starting transfers between devices, swap(): return lax.ppermute(array, 'row', pairs)  53.8 us
    all_to_all x1, waiting for transfers between devices, exchange(): return lax.all_to_all(array, 'row', split_axis=0, concat_axis=0, tiled=True)  38.5 us
    all_to_all x1, blocking collectives, exchange(): return lax.all_to_all(array, 'row', split_axis=0, concat_axis=0, tiled=True)  22.3 us
    pallas_call x2, Pallas kernels, potential_rows(): pl.pallas_call(functools.partial(potential_kernel, kind, step, per_device...  18.1 us
    all_to_all x1, starting transfers between devices, exchange(): return lax.all_to_all(array, 'row', split_axis=0, concat_axis=0, tiled=True)  9.17 us
    pallas_call x2, Pallas kernels, taylor(): pl.pallas_call(functools.partial(taylor_kernel, mode, chips), out_shape=j...  9.08 us
    ppermute x22, waiting for transfers between devices, swap(): return lax.ppermute(array, 'row', pairs)  4.54 us
    pallas_call x1, Pallas kernels, plan(): pl.pallas_call(functools.partial(plan_kernel, per_device), out_shape=(jax...  3.71 us
  transfers between devices with their start and end apart: 23, of which 5 were waited for; matrix products, arithmetic and copies ran while one was open for 0% of the time, Pallas kernels for 9%

profile of v3, /device:TPU:9, one launch (start us, length us, event | category | flops | bytes accessed | tf_op | source)
XLA Modules:
  0.0 164.4 jit_solution(2249020091529097997)
XLA Ops:
  0.0 0.8 reshape.19
  0.8 0.7 collective-permute-start.17
  1.4 0.8 collective-permute-done.17
  2.3 1.2 collective-permute-start.18
  3.5 1.2 collective-permute-done.18
  4.7 0.1 collective-permute-start.19
  4.8 2.5 %collective-permute-start.20 = (bf16[4,256]{1,0:T(4,128)(2,1)S(1)}, bf16[4,256]{1,0:T(4,128)(2,1)S(1)}, u32[]{:S(2)}, u32[]{:S(2)}) collective-permute-start(bf16[4,256]{1,0:T(4,128)(2,1)S(1)} %pad_maximum_fusion), channel_id=1, source_target_pairs={{0,8},{1,9},{2,10},{3,11},{4,12},{5,13},{6,14},{7,15},{8,0},{9,1},... | collective-permute-start | bytes 6152 | tf_op jit(solution)/shard_map/ppermute | solution.py:461
  7.3 0.2 collective-permute-start.21
  7.4 3.7 %shard_map.66 = (s32[2,32]{1,0:T(2,128)}, s32[32]{0:T(128)}, s32[4,16]{1,0:T(4,128)S(1)}, s32[32]{0:T(128)}, s32[2]{0:T(128)S(1)}) custom-call(s32[16]{0:T(128)} %counts.1, s32[2,32]{1,0:T(2,128)} %sources.1), custom_call_target="tpu_custom_call" | custom-call | tf_op jit(solution)/shard_map/pallas_call | solution.py:142
  11.2 0.6 slice.6
  12.4 0.0 collective-permute-done.19
  12.4 0.0 collective-permute-done.20
  12.4 0.0 collective-permute-done.21
  12.4 151.9 %conditional.1 = (bf16[32,64,256]{2,1,0:T(8,128)(2,1)}) conditional(s32[]{:T(128)} %bitcast.4, (s32[2]{0:T(128)S(1)}, s32[1]{0:T(128)}, s32[2,32]{1,0:T(2,128)}, s32[2,64]{1,0:T(2,128)}, bf16[4,256]{1,0:T(4,128)(2,1)S(1)}, /*index=5*/bf16[4,256]{1,0:T(4,128)(2,1)S(1)}, bf16[4,256]{1,0:T(4,128)(2,1)S(1)}, bf16[4,256]{1,0:T(4,128)(2,1)S(1)}, ...), branch_computations={%region_0.3_spmd, %region_3.4_spmd} | conditional | flops 8589934592 | bytes 57677176 | solution.py:520
  12.4 0.0 copy-start.7
  12.4 11.9 %branch_1_fun.5 = bf16[16,64,1280]{2,1,0:T(8,128)(2,1)} custom-call(s32[1]{0:T(128)} %get-tuple-element.138.me, s32[4,16]{1,0:T(4,128)S(1)} %get-tuple-element.139.jobs, s32[1]{0:T(128)} %constant.34.clone.base, s32[2,64]{1,0:T(2,128)} %get-tuple-element.140.slab, bf16[4,256]{1,0:T(4,128)(2,1)S(1)} %get-tuple-element.141.refs_0_, ...), custom_call_target="tpu_custom_call" | custom-call | flops 3221225472 | bytes 18874368 | tf_op jit(solution)/shard_map/cond/branch_1_fun/pallas_call | solution.py:299
  24.3 0.0 copy-start.4
  24.3 9.2 %all-to-all-start = ((bf16[16,64,1280]{2,1,0:T(8,128)(2,1)}), bf16[16,64,1280]{2,1,0:T(8,128)(2,1)S(1)}, u32[]{:S(2)}, u32[]{:S(2)}) async-start(bf16[16,64,1280]{2,1,0:T(8,128)(2,1)} %branch_1_fun.5), calls=%async_computation | async-start | bytes 5242880 | tf_op jit(solution)/shard_map/cond/branch_1_fun/all_to_all | solution.py:524
  33.5 0.0 copy-done.7
  33.5 0.0 copy-done.4
  33.5 6.2 %branch_1_fun.6 = (bf16[64,1024]{1,0:T(8,128)(2,1)S(1)}, bf16[64,1024]{1,0:T(8,128)(2,1)S(1)}, bf16[64,1024]{1,0:T(8,128)(2,1)S(1)}, bf16[64,1024]{1,0:T(8,128)(...) custom-call(s32[1]{0:T(128)} %get-tuple-element.138.me, ...), custom_call_target="tpu_custom_call" | custom-call | flops 1073741824 | bytes 9437184 | tf_op jit(solution)/shard_map/cond/branch_1_fun/pallas_call | solution.py:299
  39.7 0.0 copy-start
  39.7 0.7 copy-done
  40.4 0.7 collective-permute-start
  41.0 0.7 collective-permute-start.1
  41.7 7.9 %collective-permute-start.10 = (bf16[64,1024]{1,0:T(8,128)(2,1)}, bf16[64,1024]{1,0:T(8,128)(2,1)S(1)}, u32[]{:S(2)}, u32[]{:S(2)}) collective-permute-start(bf16[64,1024]{1,0:T(8,128)(2,1)} %get-tuple-element.150), channel_id=1, source_target_pairs={{1,6},{3,4},{5,2},{7,0},{9,14},{11,12},{13,10},{15,8},{17,22},{19,... | collective-permute-start | bytes 393224 | tf_op jit(solution)/shard_map/cond/branch_1_fun/ppermute | solution.py:461
  49.6 2.2 %collective-permute-start.11 = (bf16[64,1024]{1,0:T(8,128)(2,1)}, bf16[64,1024]{1,0:T(8,128)(2,1)S(1)}, u32[]{:S(2)}, u32[]{:S(2)}) collective-permute-start(bf16[64,1024]{1,0:T(8,128)(2,1)} %get-tuple-element.151), channel_id=1, source_target_pairs={{1,8},{3,10},{5,12},{7,14},{9,0},{11,2},{13,4},{15,6},{17,24},{19,... | collective-permute-start | bytes 393224 | tf_op jit(solution)/shard_map/cond/branch_1_fun/ppermute | solution.py:461
  51.8 1.9 %collective-permute-start.12 = (bf16[64,1024]{1,0:T(8,128)(2,1)}, bf16[64,1024]{1,0:T(8,128)(2,1)}, u32[]{:S(2)}, u32[]{:S(2)}) collective-permute-start(bf16[64,1024]{1,0:T(8,128)(2,1)} %get-tuple-element.152), channel_id=1, source_target_pairs={{1,10},{3,8},{5,14},{7,12},{9,2},{11,0},{13,6},{15,4},{17,26},{19,... | collective-permute-start | bytes 393224 | tf_op jit(solution)/shard_map/cond/branch_1_fun/ppermute | solution.py:461
  53.8 0.0 collective-permute-done.refs_1_
  53.8 2.1 %collective-permute-start.13 = (bf16[64,1024]{1,0:T(8,128)(2,1)}, bf16[64,1024]{1,0:T(8,128)(2,1)}, u32[]{:S(2)}, u32[]{:S(2)}) collective-permute-start(bf16[64,1024]{1,0:T(8,128)(2,1)} %get-tuple-element.153), channel_id=1, source_target_pairs={{1,12},{3,14},{5,8},{7,10},{9,4},{11,6},{13,0},{15,2},{17,28},{19,... | collective-permute-start | bytes 393224 | tf_op jit(solution)/shard_map/cond/branch_1_fun/ppermute | solution.py:461
  55.8 38.5 %all-to-all-done.joint = bf16[16,64,1280]{2,1,0:T(8,128)(2,1)S(1)} async-done(((bf16[16,64,1280]{2,1,0:T(8,128)(2,1)}), bf16[16,64,1280]{2,1,0:T(8,128)(2,1)S(1)}, u32[]{:S(2)}, u32[]{:S(2)}) %all-to-all-start) | async-done | bytes 2621472 | tf_op jit(solution)/shard_map/cond/branch_1_fun/all_to_all | solution.py:524
  94.3 4.6 %branch_1_fun.7.refs_16_ = bf16[1024,256]{1,0:T(8,128)(2,1)S(1)} custom-call(s32[1]{0:T(128)} %get-tuple-element.138.me, s32[4,16]{1,0:T(4,128)} %copy-done.7, bf16[16,64,1280]{2,1,0:T(8,128)(2,1)S(1)} %all-to-all-done.joint), custom_call_target="tpu_custom_call" | custom-call | flops 2147483648 | bytes 3670016 | tf_op jit(solution)/shard_map/cond/branch_1_fun/pallas_call | solution.py:401
  98.9 0.0 collective-permute-done.1.refs_2_
  99.0 1.3 collective-permute-start.15
  100.3 0.0 collective-permute-done.10.refs_11_
  100.3 5.7 %collective-permute-start.16 = (bf16[1024,256]{1,0:T(8,128)(2,1)S(1)}, bf16[1024,256]{1,0:T(8,128)(2,1)S(1)}, u32[]{:S(2)}, u32[]{:S(2)}) collective-permute-start(bf16[1024,256]{1,0:T(8,128)(2,1)S(1)} %branch_1_fun.7.refs_16_), channel_id=1, source_target_pairs={{1,3},{5,7},{9,11},{13,15},{17,19},{21,23},{25,27},{29,31}} | collective-permute-start | bytes 1572872 | tf_op jit(solution)/shard_map/cond/branch_1_fun/ppermute | solution.py:461
  106.0 0.0 collective-permute-done.11.refs_12_
  106.0 0.0 copy-done.1
  106.0 1.3 collective-permute-start.14
  107.3 0.0 collective-permute-done.12.refs_13_
  107.3 0.7 collective-permute-start.2
  108.0 0.0 collective-permute-done.13.refs_14_
  108.0 0.7 collective-permute-start.3
  108.7 0.6 collective-permute-done.14.refs_15_
  109.3 0.7 collective-permute-start.4
  109.9 0.0 collective-permute-done.2.refs_3_
  109.9 0.7 collective-permute-start.5
  110.6 0.0 collective-permute-done.3.refs_4_
  110.6 0.7 collective-permute-start.6
  111.3 0.0 collective-permute-done.4.refs_5_
  111.3 15.8 %collective-permute-start.8 = (bf16[64,1024]{1,0:T(8,128)(2,1)S(1)}, bf16[64,1024]{1,0:T(8,128)(2,1)S(1)}, u32[]{:S(2)}, u32[]{:S(2)}) collective-permute-start(bf16[64,1024]{1,0:T(8,128)(2,1)S(1)} %get-tuple-element.148), channel_id=1, source_target_pairs={{1,2},{3,0},{5,6},{7,4},{9,10},{11,8},{13,14},{15,12},{17,18},{19,... | collective-permute-start | bytes 393224 | tf_op jit(solution)/shard_map/cond/branch_1_fun/ppermute | solution.py:461
  127.1 0.0 collective-permute-done.5.refs_6_
  127.1 1.3 collective-permute-start.7
  128.5 0.0 collective-permute-done.6.refs_7_
  128.5 5.0 %collective-permute-start.9 = (bf16[64,1024]{1,0:T(8,128)(2,1)S(1)}, bf16[64,1024]{1,0:T(8,128)(2,1)S(1)}, u32[]{:S(2)}, u32[]{:S(2)}) collective-permute-start(bf16[64,1024]{1,0:T(8,128)(2,1)S(1)} %get-tuple-element.149), channel_id=1, source_target_pairs={{1,4},{3,6},{5,0},{7,2},{9,12},{11,14},{13,8},{15,10},{17,20},{19,... | collective-permute-start | bytes 393224 | tf_op jit(solution)/shard_map/cond/branch_1_fun/ppermute | solution.py:461
  133.5 0.0 collective-permute-done.7.refs_8_
  133.5 0.0 collective-permute-done.8.refs_9_
  133.5 1.9 %collective-permute-done.9.refs_10_ = bf16[64,1024]{1,0:T(8,128)(2,1)S(1)} collective-permute-done((bf16[64,1024]{1,0:T(8,128)(2,1)S(1)}, bf16[64,1024]{1,0:T(8,128)(2,1)S(1)}, u32[]{:S(2)}, u32[]{:S(2)}) %collective-permute-start.9) | collective-permute-done | bytes 131104 | tf_op jit(solution)/shard_map/cond/branch_1_fun/ppermute | solution.py:461
  135.4 0.0 collective-permute-done.15.refs_17_
  135.4 0.0 collective-permute-done.16.refs_18_
  135.4 4.5 %branch_1_fun.8 = bf16[1024,256]{1,0:T(8,128)(2,1)S(1)} custom-call(s32[1]{0:T(128)} %get-tuple-element.138.me, s32[4,16]{1,0:T(4,128)S(1)} %copy-done.8, bf16[16,64,1280]{2,1,0:T(8,128)(2,1)S(1)} %all-to-all-done.joint, bf16[64,1024]{1,0:T(8,128)(2,1)S(1)} %get-tuple-element.147.refs_0_, bf16[64,1024]{1,0:T(8,128)(2,1)S(1)} %collective-permute-done.refs_1_, ...), custom_call_target="tpu_custom_call" | custom-call | flops 2147483648 | bytes 3670016 | tf_op jit(solution)/shard_map/cond/branch_1_fun/pallas_call | solution.py:401
  139.9 22.3 %all_to_all.26.returned = bf16[16,64,256]{2,1,0:T(8,128)(2,1)S(1)} all-to-all(bf16[16,64,256]{2,1,0:T(8,128)(2,1)S(1)} %bitcast.11), channel_id=1, replica_groups=mesh['groups'=2,'row'=16] {'row'}, dimensions={0} | all-to-all | bytes 1048576 | tf_op jit(solution)/shard_map/cond/branch_1_fun/all_to_all | solution.py:524
  162.2 0.0 copy-done.9
  162.2 2.2 %branch_1_fun.9 = bf16[32,64,256]{2,1,0:T(8,128)(2,1)} custom-call(s32[32]{0:T(128)S(1)} %copy-done.9, s32[1]{0:T(128)} %constant.34.clone.base, bf16[16,64,256]{2,1,0:T(8,128)(2,1)S(1)} %all_to_all.26.returned), custom_call_target="tpu_custom_call" | custom-call | tf_op jit(solution)/shard_map/cond/branch_1_fun/pallas_call | solution.py:450
  (6 shorter events, 0.0 us)
Async XLA Ops:
  0.8 1.5 collective-permute-start.17
  2.3 2.4 %collective-permute-start.18 = (bf16[2,256]{1,0:T(2,128)(2,1)S(1)}, bf16[2,256]{1,0:T(2,128)(2,1)S(1)}, u32[]{:S(2)}, u32[]{:S(2)}) collective-permute-start(bf16[2,256]{1,0:T(2,128)(2,1)S(1)} %pad_maximum_fusion.1), channel_id=1, source_target_pairs={{0,2},{1,3},{2,0},{3,1},{4,6},{5,7},{6,4},{7,5},{8,10},{9,11},{10,... | collective-permute-start | bytes 3080 | tf_op jit(solution)/shard_map/ppermute | solution.py:461
  4.7 7.7 %collective-permute-start.19 = (bf16[4,256]{1,0:T(4,128)(2,1)S(1)}, bf16[4,256]{1,0:T(4,128)(2,1)S(1)}, u32[]{:S(2)}, u32[]{:S(2)}) collective-permute-start(bf16[4,256]{1,0:T(4,128)(2,1)S(1)} %pad_maximum_fusion), channel_id=1, source_target_pairs={{0,4},{1,5},{2,6},{3,7},{4,0},{5,1},{6,2},{7,3},{8,12},{9,13},{10,... | collective-permute-start | bytes 6152 | tf_op jit(solution)/shard_map/ppermute | solution.py:461
  4.8 7.6 %collective-permute-start.20 = (bf16[4,256]{1,0:T(4,128)(2,1)S(1)}, bf16[4,256]{1,0:T(4,128)(2,1)S(1)}, u32[]{:S(2)}, u32[]{:S(2)}) collective-permute-start(bf16[4,256]{1,0:T(4,128)(2,1)S(1)} %pad_maximum_fusion), channel_id=1, source_target_pairs={{0,8},{1,9},{2,10},{3,11},{4,12},{5,13},{6,14},{7,15},{8,0},{9,1},... | collective-permute-start | bytes 6152 | tf_op jit(solution)/shard_map/ppermute | solution.py:461
  7.3 5.1 %collective-permute-start.21 = (bf16[4,256]{1,0:T(4,128)(2,1)S(1)}, bf16[4,256]{1,0:T(4,128)(2,1)S(1)}, u32[]{:S(2)}, u32[]{:S(2)}) collective-permute-start(bf16[4,256]{1,0:T(4,128)(2,1)S(1)} %pad_maximum_fusion), channel_id=1, source_target_pairs={{0,12},{1,13},{2,14},{3,15},{4,8},{5,9},{6,10},{7,11},{8,4},{9,5},... | collective-permute-start | bytes 6152 | tf_op jit(solution)/shard_map/ppermute | solution.py:461
  12.4 21.1 %copy-start.7 = (s32[4,16]{1,0:T(4,128)}, s32[4,16]{1,0:T(4,128)S(1)}, u32[]{:S(2)}) copy-start(s32[4,16]{1,0:T(4,128)S(1)} %get-tuple-element.139.jobs) | copy-start | bytes 772 | tf_op jit(solution)/shard_map/cond
  24.3 9.2 %copy-start.4 = (s32[2,64]{1,0:T(2,128)S(1)}, s32[2,64]{1,0:T(2,128)}, u32[]{:S(2)}) copy-start(s32[2,64]{1,0:T(2,128)} %get-tuple-element.140.slab) | copy-start | bytes 1540 | tf_op jit(solution)/shard_map/cond
  24.3 70.0 %all-to-all-start = ((bf16[16,64,1280]{2,1,0:T(8,128)(2,1)}), bf16[16,64,1280]{2,1,0:T(8,128)(2,1)S(1)}, u32[]{:S(2)}, u32[]{:S(2)}) async-start(bf16[16,64,1280]{2,1,0:T(8,128)(2,1)} %branch_1_fun.5), calls=%async_computation | async-start | bytes 5242880 | tf_op jit(solution)/shard_map/cond/branch_1_fun/all_to_all | solution.py:524
  39.7 0.7 copy-start
  40.4 13.4 %collective-permute-start = (bf16[64,1024]{1,0:T(8,128)(2,1)S(1)}, bf16[64,1024]{1,0:T(8,128)(2,1)S(1)}, u32[]{:S(2)}, u32[]{:S(2)}) collective-permute-start(bf16[64,1024]{1,0:T(8,128)(2,1)S(1)} %get-tuple-element.148), channel_id=1, source_target_pairs={{0,2},{2,0},{4,6},{6,4},{8,10},{10,8},{12,14},{14,12},{16,18},{18,... | collective-permute-start | bytes 393224 | tf_op jit(solution)/shard_map/cond/branch_1_fun/ppermute | solution.py:461
  41.0 57.9 %collective-permute-start.1 = (bf16[64,1024]{1,0:T(8,128)(2,1)S(1)}, bf16[64,1024]{1,0:T(8,128)(2,1)S(1)}, u32[]{:S(2)}, u32[]{:S(2)}) collective-permute-start(bf16[64,1024]{1,0:T(8,128)(2,1)S(1)} %get-tuple-element.149), channel_id=1, source_target_pairs={{0,4},{2,6},{4,0},{6,2},{8,12},{10,14},{12,8},{14,10},{16,20},{18,... | collective-permute-start | bytes 393224 | tf_op jit(solution)/shard_map/cond/branch_1_fun/ppermute | solution.py:461
  41.7 58.5 %collective-permute-start.10 = (bf16[64,1024]{1,0:T(8,128)(2,1)}, bf16[64,1024]{1,0:T(8,128)(2,1)S(1)}, u32[]{:S(2)}, u32[]{:S(2)}) collective-permute-start(bf16[64,1024]{1,0:T(8,128)(2,1)} %get-tuple-element.150), channel_id=1, source_target_pairs={{1,6},{3,4},{5,2},{7,0},{9,14},{11,12},{13,10},{15,8},{17,22},{19,... | collective-permute-start | bytes 393224 | tf_op jit(solution)/shard_map/cond/branch_1_fun/ppermute | solution.py:461
  49.6 56.4 %collective-permute-start.11 = (bf16[64,1024]{1,0:T(8,128)(2,1)}, bf16[64,1024]{1,0:T(8,128)(2,1)S(1)}, u32[]{:S(2)}, u32[]{:S(2)}) collective-permute-start(bf16[64,1024]{1,0:T(8,128)(2,1)} %get-tuple-element.151), channel_id=1, source_target_pairs={{1,8},{3,10},{5,12},{7,14},{9,0},{11,2},{13,4},{15,6},{17,24},{19,... | collective-permute-start | bytes 393224 | tf_op jit(solution)/shard_map/cond/branch_1_fun/ppermute | solution.py:461
  51.8 55.5 %collective-permute-start.12 = (bf16[64,1024]{1,0:T(8,128)(2,1)}, bf16[64,1024]{1,0:T(8,128)(2,1)}, u32[]{:S(2)}, u32[]{:S(2)}) collective-permute-start(bf16[64,1024]{1,0:T(8,128)(2,1)} %get-tuple-element.152), channel_id=1, source_target_pairs={{1,10},{3,8},{5,14},{7,12},{9,2},{11,0},{13,6},{15,4},{17,26},{19,... | collective-permute-start | bytes 393224 | tf_op jit(solution)/shard_map/cond/branch_1_fun/ppermute | solution.py:461
  53.8 81.6 %copy-start.8 = (s32[4,16]{1,0:T(4,128)S(1)}, s32[4,16]{1,0:T(4,128)}, u32[]{:S(2)}) copy-start(s32[4,16]{1,0:T(4,128)} %copy-done.7) | copy-start | bytes 772 | tf_op jit(solution)/shard_map/cond
  53.8 54.3 %collective-permute-start.13 = (bf16[64,1024]{1,0:T(8,128)(2,1)}, bf16[64,1024]{1,0:T(8,128)(2,1)}, u32[]{:S(2)}, u32[]{:S(2)}) collective-permute-start(bf16[64,1024]{1,0:T(8,128)(2,1)} %get-tuple-element.153), channel_id=1, source_target_pairs={{1,12},{3,14},{5,8},{7,10},{9,4},{11,6},{13,0},{15,2},{17,28},{19,... | collective-permute-start | bytes 393224 | tf_op jit(solution)/shard_map/cond/branch_1_fun/ppermute | solution.py:461
  94.3 11.7 %copy-start.1 = (bf16[64,1024]{1,0:T(8,128)(2,1)S(1)}, bf16[64,1024]{1,0:T(8,128)(2,1)}, u32[]{:S(2)}) copy-start(bf16[64,1024]{1,0:T(8,128)(2,1)} %copy-done) | copy-start | bytes 393220 | tf_op jit(solution)/shard_map/cond
  99.0 36.4 %collective-permute-start.15 = (bf16[1024,256]{1,0:T(8,128)(2,1)S(1)}, bf16[1024,256]{1,0:T(8,128)(2,1)S(1)}, u32[]{:S(2)}, u32[]{:S(2)}) collective-permute-start(bf16[1024,256]{1,0:T(8,128)(2,1)S(1)} %branch_1_fun.7.refs_16_), channel_id=1, source_target_pairs={{0,1},{2,3},{4,5},{6,7},{8,9},{10,11},{12,13},{14,15},{16,17},{18,... | collective-permute-start | bytes 1572872 | tf_op jit(solution)/shard_map/cond/branch_1_fun/ppermute | solution.py:461
  100.3 35.1 %collective-permute-start.16 = (bf16[1024,256]{1,0:T(8,128)(2,1)S(1)}, bf16[1024,256]{1,0:T(8,128)(2,1)S(1)}, u32[]{:S(2)}, u32[]{:S(2)}) collective-permute-start(bf16[1024,256]{1,0:T(8,128)(2,1)S(1)} %branch_1_fun.7.refs_16_), channel_id=1, source_target_pairs={{1,3},{5,7},{9,11},{13,15},{17,19},{21,23},{25,27},{29,31}} | collective-permute-start | bytes 1572872 | tf_op jit(solution)/shard_map/cond/branch_1_fun/ppermute | solution.py:461
  106.0 3.2 %collective-permute-start.14 = (bf16[64,1024]{1,0:T(8,128)(2,1)S(1)}, bf16[64,1024]{1,0:T(8,128)(2,1)S(1)}, u32[]{:S(2)}, u32[]{:S(2)}) collective-permute-start(bf16[64,1024]{1,0:T(8,128)(2,1)S(1)} %copy-done.1), channel_id=1, source_target_pairs={{1,14},{3,12},{5,10},{7,8},{9,6},{11,4},{13,2},{15,0},{17,30},{19,... | collective-permute-start | bytes 393224 | tf_op jit(solution)/shard_map/cond/branch_1_fun/ppermute | solution.py:461
  107.3 2.6 %collective-permute-start.2 = (bf16[64,1024]{1,0:T(8,128)(2,1)}, bf16[64,1024]{1,0:T(8,128)(2,1)S(1)}, u32[]{:S(2)}, u32[]{:S(2)}) collective-permute-start(bf16[64,1024]{1,0:T(8,128)(2,1)} %get-tuple-element.150), channel_id=1, source_target_pairs={{0,6},{2,4},{4,2},{6,0},{8,14},{10,12},{12,10},{14,8},{16,22},{18,... | collective-permute-start | bytes 393224 | tf_op jit(solution)/shard_map/cond/branch_1_fun/ppermute | solution.py:461
  108.0 2.6 %collective-permute-start.3 = (bf16[64,1024]{1,0:T(8,128)(2,1)}, bf16[64,1024]{1,0:T(8,128)(2,1)S(1)}, u32[]{:S(2)}, u32[]{:S(2)}) collective-permute-start(bf16[64,1024]{1,0:T(8,128)(2,1)} %get-tuple-element.151), channel_id=1, source_target_pairs={{0,8},{2,10},{4,12},{6,14},{8,0},{10,2},{12,4},{14,6},{16,24},{18,... | collective-permute-start | bytes 393224 | tf_op jit(solution)/shard_map/cond/branch_1_fun/ppermute | solution.py:461
  109.3 2.0 %collective-permute-start.4 = (bf16[64,1024]{1,0:T(8,128)(2,1)}, bf16[64,1024]{1,0:T(8,128)(2,1)S(1)}, u32[]{:S(2)}, u32[]{:S(2)}) collective-permute-start(bf16[64,1024]{1,0:T(8,128)(2,1)} %get-tuple-element.152), channel_id=1, source_target_pairs={{0,10},{2,8},{4,14},{6,12},{8,2},{10,0},{12,6},{14,4},{16,26},{18,... | collective-permute-start | bytes 393224 | tf_op jit(solution)/shard_map/cond/branch_1_fun/ppermute | solution.py:461
  109.9 17.2 %collective-permute-start.5 = (bf16[64,1024]{1,0:T(8,128)(2,1)}, bf16[64,1024]{1,0:T(8,128)(2,1)S(1)}, u32[]{:S(2)}, u32[]{:S(2)}) collective-permute-start(bf16[64,1024]{1,0:T(8,128)(2,1)} %get-tuple-element.153), channel_id=1, source_target_pairs={{0,12},{2,14},{4,8},{6,10},{8,4},{10,6},{12,0},{14,2},{16,28},{18,... | collective-permute-start | bytes 393224 | tf_op jit(solution)/shard_map/cond/branch_1_fun/ppermute | solution.py:461
  110.6 17.8 %collective-permute-start.6 = (bf16[64,1024]{1,0:T(8,128)(2,1)S(1)}, bf16[64,1024]{1,0:T(8,128)(2,1)S(1)}, u32[]{:S(2)}, u32[]{:S(2)}) collective-permute-start(bf16[64,1024]{1,0:T(8,128)(2,1)S(1)} %copy-done.1), channel_id=1, source_target_pairs={{0,14},{2,12},{4,10},{6,8},{8,6},{10,4},{12,2},{14,0},{16,30},{18,... | collective-permute-start | bytes 393224 | tf_op jit(solution)/shard_map/cond/branch_1_fun/ppermute | solution.py:461
  111.3 22.2 %collective-permute-start.8 = (bf16[64,1024]{1,0:T(8,128)(2,1)S(1)}, bf16[64,1024]{1,0:T(8,128)(2,1)S(1)}, u32[]{:S(2)}, u32[]{:S(2)}) collective-permute-start(bf16[64,1024]{1,0:T(8,128)(2,1)S(1)} %get-tuple-element.148), channel_id=1, source_target_pairs={{1,2},{3,0},{5,6},{7,4},{9,10},{11,8},{13,14},{15,12},{17,18},{19,... | collective-permute-start | bytes 393224 | tf_op jit(solution)/shard_map/cond/branch_1_fun/ppermute | solution.py:461
  127.1 35.1 %copy-start.9 = (s32[32]{0:T(128)S(1)}, s32[32]{0:T(128)}, u32[]{:S(2)}) copy-start(s32[32]{0:T(128)} %get-tuple-element.137.place) | copy-start | bytes 388 | tf_op jit(solution)/shard_map/cond
  127.1 6.3 %collective-permute-start.7 = (bf16[64,1024]{1,0:T(8,128)(2,1)S(1)}, bf16[64,1024]{1,0:T(8,128)(2,1)S(1)}, u32[]{:S(2)}, u32[]{:S(2)}) collective-permute-start(bf16[64,1024]{1,0:T(8,128)(2,1)S(1)} %get-tuple-element.147.refs_0_), channel_id=1, source_target_pairs={{1,0},{3,2},{5,4},{7,6},{9,8},{11,10},{13,12},{15,14},{17,16},{19,... | collective-permute-start | bytes 393224 | tf_op jit(solution)/shard_map/cond/branch_1_fun/ppermute | solution.py:461
  128.5 6.9 %collective-permute-start.9 = (bf16[64,1024]{1,0:T(8,128)(2,1)S(1)}, bf16[64,1024]{1,0:T(8,128)(2,1)S(1)}, u32[]{:S(2)}, u32[]{:S(2)}) collective-permute-start(bf16[64,1024]{1,0:T(8,128)(2,1)S(1)} %get-tuple-element.149), channel_id=1, source_target_pairs={{1,4},{3,6},{5,0},{7,2},{9,12},{11,14},{13,8},{15,10},{17,20},{19,... | collective-permute-start | bytes 393224 | tf_op jit(solution)/shard_map/cond/branch_1_fun/ppermute | solution.py:461

commit v4 on v3

--- a/solution.py
+++ b/solution.py
@@ -32,7 +32,7 @@
         lists[1, slot] = 0
         return carry
 
-    lax.fori_loop(0, slots, clear, 0)
+    lax.fori_loop(0, slots, clear, 0, unroll=8)
 
     def alive(slot):
         return slot % per_device < counts[slot // per_device]
@@ -44,7 +44,7 @@
 
         return carry
 
-    lax.fori_loop(0, slots, mark, 0)
+    lax.fori_loop(0, slots, mark, 0, unroll=8)
 
     def number(slot, found):
         count, twins = found
@@ -72,7 +72,9 @@
 
         return count + kept.astype(jnp.int32), twins + paired.astype(jnp.int32)
 
-    count, twins = lax.fori_loop(0, slots, number, (jnp.int32(0), jnp.int32(0)))
+    count, twins = lax.fori_loop(
+        0, slots, number, (jnp.int32(0), jnp.int32(0)), unroll=4
+    )
     total[0] = count
     leads, pair = count - twins, (twins + 1) // 2
     fits = leads - chips <= jnp.maximum(chips // 2 - pair, 0)
@@ -83,7 +85,7 @@
             jobs[row, device] = 0
         return carry
 
-    lax.fori_loop(0, devices, empty, 0)
+    lax.fori_loop(0, devices, empty, 0, unroll=8)
 
     @pl.when(fits)
     def _():
@@ -133,7 +135,7 @@
         )
         return carry
 
-    lax.fori_loop(0, slots, look, 0)
+    lax.fori_loop(0, slots, look, 0, unroll=8)
 
 
 def plan(counts, sources, per_device):
@@ -162,36 +164,38 @@
     blocks, left, held, semaphores = scratch[:4]
     picked = scratch[4] if walked else None
     outs = refs[: -4 - walked]
-    steps = (0, 1) if kind == "mixed" else (step,)
+    steps = (step,) if kind == "chips" else (0, 1)
     vectors = blocks.shape[1]
-    halves = semaphores.shape[0] - 1
-    half_rows = blocks.shape[2] // halves
+    quarters = semaphores.shape[0] - 1
+    part_rows = blocks.shape[2] // quarters
     orbitals = blocks.shape[3]
     devices = held.shape[0]
     block = pl.program_id(0)
 
     members = {0: range(devices), 1: range(1, devices, 2)}
-    if kind != "mixed":
-        members = {step: range(devices if kind == "all" else devices // 2)}
-
-    def slot_of(number):
+    if kind == "all":
+        members = {0: range(devices), 1: range(devices)}
+    if kind == "chips":
+        members = {step: range(devices // 2)}
+
+    def slot_of(number, now=0):
         if kind == "all":
-            return jobs[step, base[0] + number // 2 + number % 2 * (devices // 2)]
+            return jobs[now, base[0] + number // 2 + number % 2 * (devices // 2)]
         if kind == "mixed":
             return jobs[1, number]
         return jobs[2, (me[0] // 2) ^ number]
 
     @pl.when(block == 0)
     def _():
-        for half in range(halves):
-            rows = pl.ds(half * half_rows, half_rows)
+        for quarter in range(quarters):
+            rows = pl.ds(quarter * part_rows, part_rows)
             for which, step in enumerate(steps):
 
-                def one(vector, carry, rows=rows, half=half, which=which, step=step):
+                def one(vector, carry, rows=rows, quarter=quarter, which=which, step=step):
                     pltpu.make_async_copy(
                         cholesky.at[slab[step, vector], rows, :],
                         blocks.at[which, vector, rows, :],
-                        semaphores.at[half],
+                        semaphores.at[quarter],
                     ).start()
                     return carry
 
@@ -199,7 +203,7 @@
         if walked:
             for number in range(devices):
                 pltpu.make_async_copy(
-                    walkers.at[slot_of(number)], picked.at[number], semaphores.at[halves]
+                    walkers.at[slot_of(number)], picked.at[number], semaphores.at[quarters]
                 ).start()
         part = devices // pieces
         for piece in range(pieces):
@@ -216,7 +220,7 @@
             column = lax.broadcasted_iota(jnp.int32, shape, 1)
             wanted = jnp.zeros(shape, jnp.int32)
             for place, number in enumerate(members[now]):
-                slot = slot_of(number)
+                slot = slot_of(number, now)
                 there = ((slot // per_device) ^ me[0]) * per_device + slot % per_device
                 if kind == "mixed":
                     there = jnp.where(jobs[0, number] == now, there, -1)
@@ -240,14 +244,14 @@
             left[start : start + shape[0], :] = jnp.where(same, wide, 0.0).astype(jnp.bfloat16)
             start += shape[0]
         if walked:
-            pltpu.make_async_copy(picked, picked, semaphores.at[halves]).wait()
-
-    for half in range(halves):
-
-        @pl.when(block == half * (half_rows // ROWS))
-        def _():
-            view = blocks.at[:, :, pl.ds(half * half_rows, half_rows), :]
-            pltpu.make_async_copy(view, view, semaphores.at[half]).wait()
+            pltpu.make_async_copy(picked, picked, semaphores.at[quarters]).wait()
+
+    for quarter in range(quarters):
+
+        @pl.when(block == quarter * (part_rows // ROWS))
+        def _():
+            view = blocks.at[:, :, pl.ds(quarter * part_rows, part_rows), :]
+            pltpu.make_async_copy(view, view, semaphores.at[quarter]).wait()
 
     rows = pl.ds(block * ROWS, ROWS)
 
@@ -259,16 +263,20 @@
 
     count = len(members[steps[0]])
     made = product(0, 0, count)
-    if kind == "mixed":
+    if kind != "chips":
         second = product(1, count * ROWS, len(members[1]))
     for number in range(count):
         value = made[number * ROWS : (number + 1) * ROWS]
         if kind == "mixed" and number % 2:
             value = value + second[number // 2 * ROWS : (number // 2 + 1) * ROWS]
         out = outs[number] if kind == "chips" else outs[0].at[number]
+        width = out.shape[1]
         out[:, :orbitals] = value.astype(jnp.bfloat16)
+        if kind == "all":
+            value = second[number * ROWS : (number + 1) * ROWS]
+            out[:, orbitals : 2 * orbitals] = value.astype(jnp.bfloat16)
         if walked:
-            out[:, orbitals:] = picked[number, rows, :]
+            out[:, width - picked.shape[2] :] = picked[number, rows, :]
 
 
 def potential_rows(
@@ -276,17 +284,17 @@
 ):
     local_rows, orbitals = cholesky.shape[1:]
     vectors = slab.shape[1]
-    count = 2 if kind == "mixed" else 1
+    count = 1 if kind == "chips" else 2
     targets = devices // 2 if kind == "chips" else devices
-    made = targets + (devices // 2 if kind == "mixed" else 0)
+    made = targets + {"chips": 0, "mixed": devices // 2, "all": devices}[kind]
     walked = walkers is not None
-    width = orbitals + (walkers.shape[2] if walked else 0)
-    halves = 2 if local_rows % (2 * ROWS) == 0 else 1
+    width = orbitals * (1 + (kind == "all")) + (walkers.shape[2] if walked else 0)
+    quarters = next(n for n in (4, 2, 1) if local_rows % (n * ROWS) == 0)
     scratch = [
         pltpu.VMEM((count, vectors, local_rows, orbitals), jnp.bfloat16),
         pltpu.VMEM((made * ROWS, vectors * ROWS), jnp.bfloat16),
         pltpu.VMEM((devices, fields[0].shape[1]), jnp.float32),
-        pltpu.SemaphoreType.DMA((halves + 1,)),
+        pltpu.SemaphoreType.DMA((quarters + 1,)),
     ]
     if walked:
         scratch.append(pltpu.VMEM((targets,) + walkers.shape[1:], jnp.bfloat16))
@@ -331,7 +339,7 @@
     def copy_joint(number):
         for device in range(4):
             pltpu.make_async_copy(
-                joint.at[4 * number + device, :, pl.ds(0, rows)],
+                joint.at[4 * number + device, :, pl.ds(rows if mode == "large" else 0, rows)],
                 matrix.at[pl.ds(pl.multiple_of((4 * number + device) * local, local), local), :],
                 semaphores.at[number],
             ).start()
@@ -342,7 +350,7 @@
     if mode == "first":
         for device in range(devices):
             pltpu.make_async_copy(
-                joint.at[device, :, pl.ds(rows, columns)],
+                joint.at[device, :, pl.ds(joint.shape[2] - columns, columns)],
                 begun.at[pl.ds(device * local, local), :],
                 ready,
             ).start()
@@ -500,10 +508,8 @@
             starts = [current, twin, moved]
             advanced = taylor("small", me, jobs, joint, parts, across, starts, columns)
         else:
-            rows = rows_of("all", 1, None)
-            late = exchange(rows)
             current = taylor("first", me, jobs, joint, [], [], [], columns)
-            advanced = taylor("large", me, jobs, late, [], [], [current], columns)
+            advanced = taylor("large", me, jobs, joint, [], [], [current], columns)
         returned = exchange(advanced.reshape(devices, local_rows, columns))
         return select(owned if small else place, base, returned, before, small)
 
@@ -511,13 +517,17 @@
         return one_pass(True, jnp.zeros((1,), jnp.int32), None)
 
     def large():
+        return one_pass(False, jnp.zeros((1,), jnp.int32), None)
+
+    def huge():
         def another(turn, before):
             return one_pass(False, jnp.full((1,), turn * devices, jnp.int32), before)
 
         turns = (total[0] + devices - 1) // devices
         return lax.fori_loop(0, turns, another, jnp.zeros_like(walkers))
 
-    return lax.cond(total[1] == 1, small, large)
+    fitting = jnp.where(total[0] <= devices, 1, 2)
+    return lax.switch(jnp.where(total[1] == 1, 0, fitting), [small, large, huge])
 
 
 def exchange(array):

time: 166 us -> 165 us (level)
  starting transfers between devices: 62.9 us -> 57.8 us
  blocking collectives: 22.3 us -> 27.4 us
  waiting for transfers between devices: 43 us -> 41.1 us
    all_to_all x1, blocking collectives: 22.3 us -> 27.4 us  [exchange(): return lax.all_to_all(array, 'row', split_axis=0, concat_axis=0, tiled=True)]
    ppermute x22, starting transfers between devices: 53.8 us -> 51 us  [swap(): return lax.ppermute(array, 'row', pairs)]
    all_to_all x1, waiting for transfers between devices: 38.5 us -> 36 us  [exchange(): return lax.all_to_all(array, 'row', split_axis=0, concat_axis=0, tiled=True)]
    all_to_all x1, starting transfers between devices: 9.17 us -> 6.84 us  [exchange(): return lax.all_to_all(array, 'row', split_axis=0, concat_axis=0, tiled=True)]
  transfers between devices with their start and end apart: 23 -> 23, of which waited for: 5 -> 4; matrix products, arithmetic and copies ran while one was open for 0% -> 0% of each run, Pallas kernels for 9% -> 8%
where the time goes in v4:
time: 165 us; the launch traced here: 163 us
  starting transfers between devices  57.8 us (35%)
  waiting for transfers between devices  41.1 us (25%)
  Pallas kernels  31.7 us (19%)
  blocking collectives  27.4 us (17%)
  local copies, waits for them, and re-layouts  3.38 us (2%)
    ppermute x22, starting transfers between devices, swap(): return lax.ppermute(array, 'row', pairs)  51 us
    all_to_all x1, waiting for transfers between devices, exchange(): return lax.all_to_all(array, 'row', split_axis=0, concat_axis=0, tiled=True)  36 us
    all_to_all x1, blocking collectives, exchange(): return lax.all_to_all(array, 'row', split_axis=0, concat_axis=0, tiled=True)  27.4 us
    pallas_call x2, Pallas kernels, potential_rows(): pl.pallas_call(functools.partial(potential_kernel, kind, step, per_device...  17.5 us
    pallas_call x2, Pallas kernels, taylor(): pl.pallas_call(functools.partial(taylor_kernel, mode, chips), out_shape=j...  9.08 us
    all_to_all x1, starting transfers between devices, exchange(): return lax.all_to_all(array, 'row', split_axis=0, concat_axis=0, tiled=True)  6.84 us
    ppermute x22, waiting for transfers between devices, swap(): return lax.ppermute(array, 'row', pairs)  5.15 us
  transfers between devices with their start and end apart: 23, of which 4 were waited for; matrix products, arithmetic and copies ran while one was open for 0% of the time, Pallas kernels for 8%

profile of v4, /device:TPU:9, one launch (start us, length us, event | category | flops | bytes accessed | tf_op | source)
XLA Modules:
  0.0 163.3 jit_solution(7485261418214144584)
XLA Ops:
  0.0 0.8 reshape.30
  0.8 0.7 collective-permute-start.17
  1.4 0.8 collective-permute-done.17
  2.3 1.2 collective-permute-start.18
  3.5 3.0 %shard_map.67 = (s32[2,32]{1,0:T(2,128)}, s32[32]{0:T(128)}, s32[4,16]{1,0:T(4,128)S(1)}, s32[32]{0:T(128)}, s32[2]{0:T(128)S(1)}) custom-call(s32[16]{0:T(128)} %counts.1, s32[2,32]{1,0:T(2,128)} %sources.1), custom_call_target="tpu_custom_call" | custom-call | tf_op jit(solution)/shard_map/pallas_call | solution.py:144
  6.5 0.0 collective-permute-done.18
  6.5 1.4 collective-permute-start.21
  7.9 1.1 collective-permute-start.20
  9.0 1.1 collective-permute-start.19
  10.1 0.6 fusion
  12.0 0.0 collective-permute-done.21
  12.1 0.0 collective-permute-done.20
  12.1 0.0 collective-permute-done.19
  12.1 151.2 %conditional.1 = (bf16[32,64,256]{2,1,0:T(8,128)(2,1)}) conditional(s32[]{:T(128)} %bitcast.5, (s32[1]{0:T(128)}, s32[4,16]{1,0:T(4,128)S(1)}, s32[2,64]{1,0:T(2,128)}, bf16[4,256]{1,0:T(4,128)(2,1)S(1)}, bf16[4,256]{1,0:T(4,128)(2,1)S(1)}, /*index=5*/bf16[4,256]{1,0:T(4,128)(2,1)S(1)}, bf16[4,256]{1,0:T(4,128)(2,1)S(1)}, ...), branch_computations={%region_0.1_spmd, %region_1.2_spmd, %region_2.5_spmd} | conditional | flops 8589934592 | bytes 59774440 | solution.py:530
  12.1 0.0 copy-start.9
  12.1 11.9 %branch_0_fun.5 = bf16[16,64,1280]{2,1,0:T(8,128)(2,1)} custom-call(s32[1]{0:T(128)} %get-tuple-element.132.me, s32[4,16]{1,0:T(4,128)S(1)} %get-tuple-element.133.jobs, s32[1]{0:T(128)} %constant.35.clone.base, s32[2,64]{1,0:T(2,128)} %get-tuple-element.134.slab, bf16[4,256]{1,0:T(4,128)(2,1)S(1)} %get-tuple-element.135.refs_0_, ...), custom_call_target="tpu_custom_call" | custom-call | flops 3221225472 | bytes 18874368 | tf_op jit(solution)/shard_map/cond/branch_0_fun/pallas_call | solution.py:307
  24.0 0.0 copy-start.6
  24.0 6.8 %all-to-all-start = ((bf16[16,64,1280]{2,1,0:T(8,128)(2,1)}), bf16[16,64,1280]{2,1,0:T(8,128)(2,1)S(1)}, u32[]{:S(2)}, u32[]{:S(2)}) async-start(bf16[16,64,1280]{2,1,0:T(8,128)(2,1)} %branch_0_fun.5), calls=%async_computation | async-start | bytes 5242880 | tf_op jit(solution)/shard_map/cond/branch_0_fun/all_to_all | solution.py:534
  30.9 0.0 copy-done.9
  30.9 5.6 %branch_0_fun.6 = (bf16[64,1024]{1,0:T(8,128)(2,1)S(1)}, bf16[64,1024]{1,0:T(8,128)(2,1)}, bf16[64,1024]{1,0:T(8,128)(2,1)}, bf16[64,1024]{1,0:T(8,128)(2,1)}, b...) custom-call(s32[1]{0:T(128)} %get-tuple-element.132.me, ...), custom_call_target="tpu_custom_call" | custom-call | flops 1073741824 | bytes 9437184 | tf_op jit(solution)/shard_map/cond/branch_0_fun/pallas_call | solution.py:307
  36.5 0.0 copy-start
  36.5 0.6 copy-done
  37.2 0.6 copy-done.2
  37.8 0.7 copy-done.4
  38.5 2.4 %collective-permute-start.7 = (bf16[64,1024]{1,0:T(8,128)(2,1)S(1)}, bf16[64,1024]{1,0:T(8,128)(2,1)S(1)}, u32[]{:S(2)}, u32[]{:S(2)}) collective-permute-start(bf16[64,1024]{1,0:T(8,128)(2,1)S(1)} %get-tuple-element.141.refs_0_), channel_id=1, source_target_pairs={{1,0},{3,2},{5,4},{7,6},{9,8},{11,10},{13,12},{15,14},{17,16},{19,... | collective-permute-start | bytes 393224 | tf_op jit(solution)/shard_map/cond/branch_0_fun/ppermute | solution.py:469
  40.9 2.4 %collective-permute-start.8 = (bf16[64,1024]{1,0:T(8,128)(2,1)}, bf16[64,1024]{1,0:T(8,128)(2,1)S(1)}, u32[]{:S(2)}, u32[]{:S(2)}) collective-permute-start(bf16[64,1024]{1,0:T(8,128)(2,1)} %get-tuple-element.142), channel_id=1, source_target_pairs={{1,2},{3,0},{5,6},{7,4},{9,10},{11,8},{13,14},{15,12},{17,18},{19,... | collective-permute-start | bytes 393224 | tf_op jit(solution)/shard_map/cond/branch_0_fun/ppermute | solution.py:469
  43.3 0.7 collective-permute-start
  43.9 3.1 %collective-permute-start.9 = (bf16[64,1024]{1,0:T(8,128)(2,1)}, bf16[64,1024]{1,0:T(8,128)(2,1)S(1)}, u32[]{:S(2)}, u32[]{:S(2)}) collective-permute-start(bf16[64,1024]{1,0:T(8,128)(2,1)} %get-tuple-element.143), channel_id=1, source_target_pairs={{1,4},{3,6},{5,0},{7,2},{9,12},{11,14},{13,8},{15,10},{17,20},{19,... | collective-permute-start | bytes 393224 | tf_op jit(solution)/shard_map/cond/branch_0_fun/ppermute | solution.py:469
  47.0 0.7 collective-permute-start.1
  47.7 0.0 collective-permute-done.7.refs_8_
  47.7 4.7 %collective-permute-start.10 = (bf16[64,1024]{1,0:T(8,128)(2,1)}, bf16[64,1024]{1,0:T(8,128)(2,1)}, u32[]{:S(2)}, u32[]{:S(2)}) collective-permute-start(bf16[64,1024]{1,0:T(8,128)(2,1)} %get-tuple-element.144), channel_id=1, source_target_pairs={{1,6},{3,4},{5,2},{7,0},{9,14},{11,12},{13,10},{15,8},{17,22},{19,... | collective-permute-start | bytes 393224 | tf_op jit(solution)/shard_map/cond/branch_0_fun/ppermute | solution.py:469
  52.4 36.0 %all-to-all-done.joint = bf16[16,64,1280]{2,1,0:T(8,128)(2,1)S(1)} async-done(((bf16[16,64,1280]{2,1,0:T(8,128)(2,1)}), bf16[16,64,1280]{2,1,0:T(8,128)(2,1)S(1)}, u32[]{:S(2)}, u32[]{:S(2)}) %all-to-all-start) | async-done | bytes 2621472 | tf_op jit(solution)/shard_map/cond/branch_0_fun/all_to_all | solution.py:534
  88.4 4.6 %branch_0_fun.7.refs_16_ = bf16[1024,256]{1,0:T(8,128)(2,1)S(1)} custom-call(s32[1]{0:T(128)} %get-tuple-element.132.me, s32[4,16]{1,0:T(4,128)} %copy-done.9, bf16[16,64,1280]{2,1,0:T(8,128)(2,1)S(1)} %all-to-all-done.joint), custom_call_target="tpu_custom_call" | custom-call | flops 2147483648 | bytes 3670016 | tf_op jit(solution)/shard_map/cond/branch_0_fun/pallas_call | solution.py:409
  93.0 0.0 collective-permute-done.8.refs_9_
  93.0 4.3 %collective-permute-start.16 = (bf16[1024,256]{1,0:T(8,128)(2,1)S(1)}, bf16[1024,256]{1,0:T(8,128)(2,1)S(1)}, u32[]{:S(2)}, u32[]{:S(2)}) collective-permute-start(bf16[1024,256]{1,0:T(8,128)(2,1)S(1)} %branch_0_fun.7.refs_16_), channel_id=1, source_target_pairs={{1,3},{5,7},{9,11},{13,15},{17,19},{21,23},{25,27},{29,31}} | collective-permute-start | bytes 1572872 | tf_op jit(solution)/shard_map/cond/branch_0_fun/ppermute | solution.py:469
  97.3 0.0 collective-permute-done.refs_1_
  97.3 1.3 collective-permute-start.15
  98.6 0.0 collective-permute-done.9.refs_10_
  98.6 0.7 collective-permute-start.2
  99.3 0.0 collective-permute-done.1.refs_2_
  99.3 6.3 %collective-permute-start.11 = (bf16[64,1024]{1,0:T(8,128)(2,1)S(1)}, bf16[64,1024]{1,0:T(8,128)(2,1)S(1)}, u32[]{:S(2)}, u32[]{:S(2)}) collective-permute-start(bf16[64,1024]{1,0:T(8,128)(2,1)S(1)} %copy-done.5), channel_id=1, source_target_pairs={{1,8},{3,10},{5,12},{7,14},{9,0},{11,2},{13,4},{15,6},{17,24},{19,... | collective-permute-start | bytes 393224 | tf_op jit(solution)/shard_map/cond/branch_0_fun/ppermute | solution.py:469
  105.6 0.0 collective-permute-done.10.refs_11_
  105.6 0.7 collective-permute-start.3
  106.3 0.0 collective-permute-done.2.refs_3_
  106.3 0.0 copy-done.3
  106.3 4.5 %collective-permute-start.12 = (bf16[64,1024]{1,0:T(8,128)(2,1)S(1)}, bf16[64,1024]{1,0:T(8,128)(2,1)S(1)}, u32[]{:S(2)}, u32[]{:S(2)}) collective-permute-start(bf16[64,1024]{1,0:T(8,128)(2,1)S(1)} %copy-done.3), channel_id=1, source_target_pairs={{1,10},{3,8},{5,14},{7,12},{9,2},{11,0},{13,6},{15,4},{17,26},{19,... | collective-permute-start | bytes 393224 | tf_op jit(solution)/shard_map/cond/branch_0_fun/ppermute | solution.py:469
  110.8 0.3 collective-permute-done.11.refs_12_
  111.1 0.7 collective-permute-start.4
  111.8 0.0 collective-permute-done.3.refs_4_
  111.8 6.3 %collective-permute-start.13 = (bf16[64,1024]{1,0:T(8,128)(2,1)S(1)}, bf16[64,1024]{1,0:T(8,128)(2,1)S(1)}, u32[]{:S(2)}, u32[]{:S(2)}) collective-permute-start(bf16[64,1024]{1,0:T(8,128)(2,1)S(1)} %copy-done.1), channel_id=1, source_target_pairs={{1,12},{3,14},{5,8},{7,10},{9,4},{11,6},{13,0},{15,2},{17,28},{19,... | collective-permute-start | bytes 393224 | tf_op jit(solution)/shard_map/cond/branch_0_fun/ppermute | solution.py:469
  118.1 0.0 collective-permute-done.12.refs_13_
  118.1 0.7 collective-permute-start.5
  118.8 0.0 collective-permute-done.4.refs_5_
  118.8 5.7 %collective-permute-start.14 = (bf16[64,1024]{1,0:T(8,128)(2,1)S(1)}, bf16[64,1024]{1,0:T(8,128)(2,1)S(1)}, u32[]{:S(2)}, u32[]{:S(2)}) collective-permute-start(bf16[64,1024]{1,0:T(8,128)(2,1)S(1)} %get-tuple-element.148), channel_id=1, source_target_pairs={{1,14},{3,12},{5,10},{7,8},{9,6},{11,4},{13,2},{15,0},{17,30},{19,... | collective-permute-start | bytes 393224 | tf_op jit(solution)/shard_map/cond/branch_0_fun/ppermute | solution.py:469
  124.5 0.0 collective-permute-done.13.refs_14_
  124.5 0.7 collective-permute-start.6
  125.2 0.0 collective-permute-done.5.refs_6_
  125.2 4.0 %collective-permute-done.14.refs_15_ = bf16[64,1024]{1,0:T(8,128)(2,1)S(1)} collective-permute-done((bf16[64,1024]{1,0:T(8,128)(2,1)S(1)}, bf16[64,1024]{1,0:T(8,128)(2,1)S(1)}, u32[]{:S(2)}, u32[]{:S(2)}) %collective-permute-start.14) | collective-permute-done | bytes 131104 | tf_op jit(solution)/shard_map/cond/branch_0_fun/ppermute | solution.py:469
  129.2 0.0 collective-permute-done.6.refs_7_
  129.2 0.0 collective-permute-done.16.refs_18_
  129.2 0.0 collective-permute-done.15.refs_17_
  129.2 4.5 %branch_0_fun.8 = bf16[1024,256]{1,0:T(8,128)(2,1)S(1)} custom-call(s32[1]{0:T(128)} %get-tuple-element.132.me, s32[4,16]{1,0:T(4,128)S(1)} %copy-done.10, bf16[16,64,1280]{2,1,0:T(8,128)(2,1)S(1)} %all-to-all-done.joint, bf16[64,1024]{1,0:T(8,128)(2,1)S(1)} %get-tuple-element.141.refs_0_, bf16[64,1024]{1,0:T(8,128)(2,1)S(1)} %collective-permute-done.refs_1_, ...), custom_call_target="tpu_custom_call" | custom-call | flops 2147483648 | bytes 3670016 | tf_op jit(solution)/shard_map/cond/branch_0_fun/pallas_call | solution.py:409
  133.7 27.4 %all_to_all.28.returned = bf16[16,64,256]{2,1,0:T(8,128)(2,1)S(1)} all-to-all(bf16[16,64,256]{2,1,0:T(8,128)(2,1)S(1)} %bitcast.12), channel_id=1, replica_groups=mesh['groups'=2,'row'=16] {'row'}, dimensions={0} | all-to-all | bytes 1048576 | tf_op jit(solution)/shard_map/cond/branch_0_fun/all_to_all | solution.py:534
  161.1 2.2 %branch_0_fun.9 = bf16[32,64,256]{2,1,0:T(8,128)(2,1)} custom-call(s32[32]{0:T(128)S(1)} %copy-done.11, s32[1]{0:T(128)} %constant.35.clone.base, bf16[16,64,256]{2,1,0:T(8,128)(2,1)S(1)} %all_to_all.28.returned), custom_call_target="tpu_custom_call" | custom-call | tf_op jit(solution)/shard_map/cond/branch_0_fun/pallas_call | solution.py:458
  (14 shorter events, 0.0 us)
Async XLA Ops:
  0.8 1.5 collective-permute-start.17
  2.3 4.2 %collective-permute-start.18 = (bf16[2,256]{1,0:T(2,128)(2,1)S(1)}, bf16[2,256]{1,0:T(2,128)(2,1)S(1)}, u32[]{:S(2)}, u32[]{:S(2)}) collective-permute-start(bf16[2,256]{1,0:T(2,128)(2,1)S(1)} %pad_maximum_fusion.1), channel_id=1, source_target_pairs={{0,2},{1,3},{2,0},{3,1},{4,6},{5,7},{6,4},{7,5},{8,10},{9,11},{10,... | collective-permute-start | bytes 3080 | tf_op jit(solution)/shard_map/ppermute | solution.py:469
  6.5 5.5 %collective-permute-start.21 = (bf16[4,256]{1,0:T(4,128)(2,1)S(1)}, bf16[4,256]{1,0:T(4,128)(2,1)S(1)}, u32[]{:S(2)}, u32[]{:S(2)}) collective-permute-start(bf16[4,256]{1,0:T(4,128)(2,1)S(1)} %pad_maximum_fusion), channel_id=1, source_target_pairs={{0,12},{1,13},{2,14},{3,15},{4,8},{5,9},{6,10},{7,11},{8,4},{9,5},... | collective-permute-start | bytes 6152 | tf_op jit(solution)/shard_map/ppermute | solution.py:469
  7.9 4.2 %collective-permute-start.20 = (bf16[4,256]{1,0:T(4,128)(2,1)S(1)}, bf16[4,256]{1,0:T(4,128)(2,1)S(1)}, u32[]{:S(2)}, u32[]{:S(2)}) collective-permute-start(bf16[4,256]{1,0:T(4,128)(2,1)S(1)} %pad_maximum_fusion), channel_id=1, source_target_pairs={{0,8},{1,9},{2,10},{3,11},{4,12},{5,13},{6,14},{7,15},{8,0},{9,1},... | collective-permute-start | bytes 6152 | tf_op jit(solution)/shard_map/ppermute | solution.py:469
  9.0 3.1 %collective-permute-start.19 = (bf16[4,256]{1,0:T(4,128)(2,1)S(1)}, bf16[4,256]{1,0:T(4,128)(2,1)S(1)}, u32[]{:S(2)}, u32[]{:S(2)}) collective-permute-start(bf16[4,256]{1,0:T(4,128)(2,1)S(1)} %pad_maximum_fusion), channel_id=1, source_target_pairs={{0,4},{1,5},{2,6},{3,7},{4,0},{5,1},{6,2},{7,3},{8,12},{9,13},{10,... | collective-permute-start | bytes 6152 | tf_op jit(solution)/shard_map/ppermute | solution.py:469
  12.1 18.8 %copy-start.9 = (s32[4,16]{1,0:T(4,128)}, s32[4,16]{1,0:T(4,128)S(1)}, u32[]{:S(2)}) copy-start(s32[4,16]{1,0:T(4,128)S(1)} %get-tuple-element.133.jobs) | copy-start | bytes 772 | tf_op jit(solution)/shard_map/cond
  24.0 6.9 %copy-start.6 = (s32[2,64]{1,0:T(2,128)S(1)}, s32[2,64]{1,0:T(2,128)}, u32[]{:S(2)}) copy-start(s32[2,64]{1,0:T(2,128)} %get-tuple-element.134.slab) | copy-start | bytes 1540 | tf_op jit(solution)/shard_map/cond
  24.0 64.3 %all-to-all-start = ((bf16[16,64,1280]{2,1,0:T(8,128)(2,1)}), bf16[16,64,1280]{2,1,0:T(8,128)(2,1)S(1)}, u32[]{:S(2)}, u32[]{:S(2)}) async-start(bf16[16,64,1280]{2,1,0:T(8,128)(2,1)} %branch_0_fun.5), calls=%async_computation | async-start | bytes 5242880 | tf_op jit(solution)/shard_map/cond/branch_0_fun/all_to_all | solution.py:534
  36.5 0.6 copy-start
  37.2 0.6 copy-start.2
  37.8 0.7 copy-start.4
  38.5 90.7 %copy-start.10 = (s32[4,16]{1,0:T(4,128)S(1)}, s32[4,16]{1,0:T(4,128)}, u32[]{:S(2)}) copy-start(s32[4,16]{1,0:T(4,128)} %copy-done.9) | copy-start | bytes 772 | tf_op jit(solution)/shard_map/cond
  38.5 9.2 %collective-permute-start.7 = (bf16[64,1024]{1,0:T(8,128)(2,1)S(1)}, bf16[64,1024]{1,0:T(8,128)(2,1)S(1)}, u32[]{:S(2)}, u32[]{:S(2)}) collective-permute-start(bf16[64,1024]{1,0:T(8,128)(2,1)S(1)} %get-tuple-element.141.refs_0_), channel_id=1, source_target_pairs={{1,0},{3,2},{5,4},{7,6},{9,8},{11,10},{13,12},{15,14},{17,16},{19,... | collective-permute-start | bytes 393224 | tf_op jit(solution)/shard_map/cond/branch_0_fun/ppermute | solution.py:469
  40.9 52.1 %collective-permute-start.8 = (bf16[64,1024]{1,0:T(8,128)(2,1)}, bf16[64,1024]{1,0:T(8,128)(2,1)S(1)}, u32[]{:S(2)}, u32[]{:S(2)}) collective-permute-start(bf16[64,1024]{1,0:T(8,128)(2,1)} %get-tuple-element.142), channel_id=1, source_target_pairs={{1,2},{3,0},{5,6},{7,4},{9,10},{11,8},{13,14},{15,12},{17,18},{19,... | collective-permute-start | bytes 393224 | tf_op jit(solution)/shard_map/cond/branch_0_fun/ppermute | solution.py:469
  43.3 54.1 %collective-permute-start = (bf16[64,1024]{1,0:T(8,128)(2,1)}, bf16[64,1024]{1,0:T(8,128)(2,1)S(1)}, u32[]{:S(2)}, u32[]{:S(2)}) collective-permute-start(bf16[64,1024]{1,0:T(8,128)(2,1)} %get-tuple-element.142), channel_id=1, source_target_pairs={{0,2},{2,0},{4,6},{6,4},{8,10},{10,8},{12,14},{14,12},{16,18},{18,... | collective-permute-start | bytes 393224 | tf_op jit(solution)/shard_map/cond/branch_0_fun/ppermute | solution.py:469
  43.9 54.7 %collective-permute-start.9 = (bf16[64,1024]{1,0:T(8,128)(2,1)}, bf16[64,1024]{1,0:T(8,128)(2,1)S(1)}, u32[]{:S(2)}, u32[]{:S(2)}) collective-permute-start(bf16[64,1024]{1,0:T(8,128)(2,1)} %get-tuple-element.143), channel_id=1, source_target_pairs={{1,4},{3,6},{5,0},{7,2},{9,12},{11,14},{13,8},{15,10},{17,20},{19,... | collective-permute-start | bytes 393224 | tf_op jit(solution)/shard_map/cond/branch_0_fun/ppermute | solution.py:469
  47.0 52.3 %collective-permute-start.1 = (bf16[64,1024]{1,0:T(8,128)(2,1)}, bf16[64,1024]{1,0:T(8,128)(2,1)S(1)}, u32[]{:S(2)}, u32[]{:S(2)}) collective-permute-start(bf16[64,1024]{1,0:T(8,128)(2,1)} %get-tuple-element.143), channel_id=1, source_target_pairs={{0,4},{2,6},{4,0},{6,2},{8,12},{10,14},{12,8},{14,10},{16,20},{18,... | collective-permute-start | bytes 393224 | tf_op jit(solution)/shard_map/cond/branch_0_fun/ppermute | solution.py:469
  47.7 57.9 %collective-permute-start.10 = (bf16[64,1024]{1,0:T(8,128)(2,1)}, bf16[64,1024]{1,0:T(8,128)(2,1)}, u32[]{:S(2)}, u32[]{:S(2)}) collective-permute-start(bf16[64,1024]{1,0:T(8,128)(2,1)} %get-tuple-element.144), channel_id=1, source_target_pairs={{1,6},{3,4},{5,2},{7,0},{9,14},{11,12},{13,10},{15,8},{17,22},{19,... | collective-permute-start | bytes 393224 | tf_op jit(solution)/shard_map/cond/branch_0_fun/ppermute | solution.py:469
  88.3 11.0 %copy-start.5 = (bf16[64,1024]{1,0:T(8,128)(2,1)S(1)}, bf16[64,1024]{1,0:T(8,128)(2,1)}, u32[]{:S(2)}) copy-start(bf16[64,1024]{1,0:T(8,128)(2,1)} %copy-done.4) | copy-start | bytes 393220 | tf_op jit(solution)/shard_map/cond
  88.4 18.0 %copy-start.3 = (bf16[64,1024]{1,0:T(8,128)(2,1)S(1)}, bf16[64,1024]{1,0:T(8,128)(2,1)}, u32[]{:S(2)}) copy-start(bf16[64,1024]{1,0:T(8,128)(2,1)} %copy-done.2) | copy-start | bytes 393220 | tf_op jit(solution)/shard_map/cond
  88.4 23.4 %copy-start.1 = (bf16[64,1024]{1,0:T(8,128)(2,1)S(1)}, bf16[64,1024]{1,0:T(8,128)(2,1)}, u32[]{:S(2)}) copy-start(bf16[64,1024]{1,0:T(8,128)(2,1)} %copy-done) | copy-start | bytes 393220 | tf_op jit(solution)/shard_map/cond
  93.0 68.1 %copy-start.11 = (s32[32]{0:T(128)S(1)}, s32[32]{0:T(128)}, u32[]{:S(2)}) copy-start(s32[32]{0:T(128)} %get-tuple-element.130.place) | copy-start | bytes 388 | tf_op jit(solution)/shard_map/cond
  93.0 36.2 %collective-permute-start.16 = (bf16[1024,256]{1,0:T(8,128)(2,1)S(1)}, bf16[1024,256]{1,0:T(8,128)(2,1)S(1)}, u32[]{:S(2)}, u32[]{:S(2)}) collective-permute-start(bf16[1024,256]{1,0:T(8,128)(2,1)S(1)} %branch_0_fun.7.refs_16_), channel_id=1, source_target_pairs={{1,3},{5,7},{9,11},{13,15},{17,19},{21,23},{25,27},{29,31}} | collective-permute-start | bytes 1572872 | tf_op jit(solution)/shard_map/cond/branch_0_fun/ppermute | solution.py:469
  97.3 31.9 %collective-permute-start.15 = (bf16[1024,256]{1,0:T(8,128)(2,1)S(1)}, bf16[1024,256]{1,0:T(8,128)(2,1)S(1)}, u32[]{:S(2)}, u32[]{:S(2)}) collective-permute-start(bf16[1024,256]{1,0:T(8,128)(2,1)S(1)} %branch_0_fun.7.refs_16_), channel_id=1, source_target_pairs={{0,1},{2,3},{4,5},{6,7},{8,9},{10,11},{12,13},{14,15},{16,17},{18,... | collective-permute-start | bytes 1572872 | tf_op jit(solution)/shard_map/cond/branch_0_fun/ppermute | solution.py:469
  98.6 7.7 %collective-permute-start.2 = (bf16[64,1024]{1,0:T(8,128)(2,1)}, bf16[64,1024]{1,0:T(8,128)(2,1)S(1)}, u32[]{:S(2)}, u32[]{:S(2)}) collective-permute-start(bf16[64,1024]{1,0:T(8,128)(2,1)} %get-tuple-element.144), channel_id=1, source_target_pairs={{0,6},{2,4},{4,2},{6,0},{8,14},{10,12},{12,10},{14,8},{16,22},{18,... | collective-permute-start | bytes 393224 | tf_op jit(solution)/shard_map/cond/branch_0_fun/ppermute | solution.py:469
  99.3 11.8 %collective-permute-start.11 = (bf16[64,1024]{1,0:T(8,128)(2,1)S(1)}, bf16[64,1024]{1,0:T(8,128)(2,1)S(1)}, u32[]{:S(2)}, u32[]{:S(2)}) collective-permute-start(bf16[64,1024]{1,0:T(8,128)(2,1)S(1)} %copy-done.5), channel_id=1, source_target_pairs={{1,8},{3,10},{5,12},{7,14},{9,0},{11,2},{13,4},{15,6},{17,24},{19,... | collective-permute-start | bytes 393224 | tf_op jit(solution)/shard_map/cond/branch_0_fun/ppermute | solution.py:469
  105.6 6.1 %collective-permute-start.3 = (bf16[64,1024]{1,0:T(8,128)(2,1)S(1)}, bf16[64,1024]{1,0:T(8,128)(2,1)S(1)}, u32[]{:S(2)}, u32[]{:S(2)}) collective-permute-start(bf16[64,1024]{1,0:T(8,128)(2,1)S(1)} %copy-done.5), channel_id=1, source_target_pairs={{0,8},{2,10},{4,12},{6,14},{8,0},{10,2},{12,4},{14,6},{16,24},{18,... | collective-permute-start | bytes 393224 | tf_op jit(solution)/shard_map/cond/branch_0_fun/ppermute | solution.py:469
  106.3 11.8 %collective-permute-start.12 = (bf16[64,1024]{1,0:T(8,128)(2,1)S(1)}, bf16[64,1024]{1,0:T(8,128)(2,1)S(1)}, u32[]{:S(2)}, u32[]{:S(2)}) collective-permute-start(bf16[64,1024]{1,0:T(8,128)(2,1)S(1)} %copy-done.3), channel_id=1, source_target_pairs={{1,10},{3,8},{5,14},{7,12},{9,2},{11,0},{13,6},{15,4},{17,26},{19,... | collective-permute-start | bytes 393224 | tf_op jit(solution)/shard_map/cond/branch_0_fun/ppermute | solution.py:469
  111.1 7.7 %collective-permute-start.4 = (bf16[64,1024]{1,0:T(8,128)(2,1)S(1)}, bf16[64,1024]{1,0:T(8,128)(2,1)S(1)}, u32[]{:S(2)}, u32[]{:S(2)}) collective-permute-start(bf16[64,1024]{1,0:T(8,128)(2,1)S(1)} %copy-done.3), channel_id=1, source_target_pairs={{0,10},{2,8},{4,14},{6,12},{8,2},{10,0},{12,6},{14,4},{16,26},{18,... | collective-permute-start | bytes 393224 | tf_op jit(solution)/shard_map/cond/branch_0_fun/ppermute | solution.py:469
  111.8 12.7 %collective-permute-start.13 = (bf16[64,1024]{1,0:T(8,128)(2,1)S(1)}, bf16[64,1024]{1,0:T(8,128)(2,1)S(1)}, u32[]{:S(2)}, u32[]{:S(2)}) collective-permute-start(bf16[64,1024]{1,0:T(8,128)(2,1)S(1)} %copy-done.1), channel_id=1, source_target_pairs={{1,12},{3,14},{5,8},{7,10},{9,4},{11,6},{13,0},{15,2},{17,28},{19,... | collective-permute-start | bytes 393224 | tf_op jit(solution)/shard_map/cond/branch_0_fun/ppermute | solution.py:469
  118.1 7.1 %collective-permute-start.5 = (bf16[64,1024]{1,0:T(8,128)(2,1)S(1)}, bf16[64,1024]{1,0:T(8,128)(2,1)S(1)}, u32[]{:S(2)}, u32[]{:S(2)}) collective-permute-start(bf16[64,1024]{1,0:T(8,128)(2,1)S(1)} %copy-done.1), channel_id=1, source_target_pairs={{0,12},{2,14},{4,8},{6,10},{8,4},{10,6},{12,0},{14,2},{16,28},{18,... | collective-permute-start | bytes 393224 | tf_op jit(solution)/shard_map/cond/branch_0_fun/ppermute | solution.py:469
  118.8 10.4 %collective-permute-start.14 = (bf16[64,1024]{1,0:T(8,128)(2,1)S(1)}, bf16[64,1024]{1,0:T(8,128)(2,1)S(1)}, u32[]{:S(2)}, u32[]{:S(2)}) collective-permute-start(bf16[64,1024]{1,0:T(8,128)(2,1)S(1)} %get-tuple-element.148), channel_id=1, source_target_pairs={{1,14},{3,12},{5,10},{7,8},{9,6},{11,4},{13,2},{15,0},{17,30},{19,... | collective-permute-start | bytes 393224 | tf_op jit(solution)/shard_map/cond/branch_0_fun/ppermute | solution.py:469
  124.5 4.7 %collective-permute-start.6 = (bf16[64,1024]{1,0:T(8,128)(2,1)S(1)}, bf16[64,1024]{1,0:T(8,128)(2,1)S(1)}, u32[]{:S(2)}, u32[]{:S(2)}) collective-permute-start(bf16[64,1024]{1,0:T(8,128)(2,1)S(1)} %get-tuple-element.148), channel_id=1, source_target_pairs={{0,14},{2,12},{4,10},{6,8},{8,6},{10,4},{12,2},{14,0},{16,30},{18,... | collective-permute-start | bytes 393224 | tf_op jit(solution)/shard_map/cond/branch_0_fun/ppermute | solution.py:469

commit v5 on v4

--- a/solution.py
+++ b/solution.py
@@ -1,4 +1,5 @@
 import functools
+import itertools
 
 import jax
 import jax.numpy as jnp
@@ -325,37 +326,34 @@
 def taylor_kernel(mode, chips, me, jobs, joint, *refs):
     parts, refs = (refs[:chips], refs[chips:]) if mode == "small" else ((), refs)
     across, refs = (refs[: chips], refs[chips:]) if mode == "small" else ((), refs)
-    count = {"first": 0, "large": 1, "small": 3}[mode]
+    count = {"first": 0, "large": 0, "small": 3}[mode]
     starts, refs = refs[:count], refs[count:]
-    out, matrix, begun, summed, term, semaphores, ready = refs
+    out, matrices, begun, summed, term, semaphores, ready = refs
+    matrix = matrices.at[0]
     devices, local = joint.shape[:2]
     rows, columns = summed.shape
     tiles = devices // 4
     tile = rows // tiles
 
-    def view(number):
-        return matrix.at[pl.ds(pl.multiple_of(number * tile, tile), tile), :]
-
-    def copy_joint(number):
+    def copy_joint(number, step=0):
         for device in range(4):
+            here = pl.multiple_of((4 * number + device) * local, local)
             pltpu.make_async_copy(
-                joint.at[4 * number + device, :, pl.ds(rows if mode == "large" else 0, rows)],
-                matrix.at[pl.ds(pl.multiple_of((4 * number + device) * local, local), local), :],
-                semaphores.at[number],
+                joint.at[4 * number + device, :, pl.ds(step * rows, rows)],
+                matrices.at[step, pl.ds(here, local), :],
+                semaphores.at[step * tiles + number],
             ).start()
 
     def copy_begun(source):
         pltpu.make_async_copy(source, begun, ready).start()
 
-    if mode == "first":
+    if mode != "small":
         for device in range(devices):
             pltpu.make_async_copy(
                 joint.at[device, :, pl.ds(joint.shape[2] - columns, columns)],
                 begun.at[pl.ds(device * local, local), :],
                 ready,
             ).start()
-    if mode == "large":
-        copy_begun(starts[0])
     if mode == "small":
         own = me[0] % 2 == 0
 
@@ -377,16 +375,24 @@
             pl.when(twin)(lambda: copy_begun(starts[1]))
             pl.when(jnp.logical_not(twin))(lambda: copy_begun(starts[2]))
             for number in range(tiles):
-                copy_joint(number)
+                copy_joint((me[0] // 4) ^ number)
     else:
-        for number in range(tiles):
-            copy_joint(number)
+        for step in range(matrices.shape[0]):
+            for number in range(tiles):
+                copy_joint(number, step)
     pltpu.make_async_copy(begun, begun, ready).wait()
-    for degree in range(1, ORDER + 1):
+    for step, degree in itertools.product(range(matrices.shape[0]), range(1, ORDER + 1)):
+        matrix = matrices.at[step]
         for number in range(tiles):
             span = slice(number * tile, (number + 1) * tile)
             if degree == 1:
-                pltpu.make_async_copy(view(number), view(number), semaphores.at[number]).wait()
+                place = number
+                if mode == "small":
+                    place = (me[0] // 4) ^ number
+                    span = pl.ds(pl.multiple_of(place * tile, tile), tile)
+                rows_in = matrix.at[span, :]
+                arrived = semaphores.at[step * tiles + place]
+                pltpu.make_async_copy(rows_in, rows_in, arrived).wait()
                 source = begun[...]
                 before = begun[span, :].astype(jnp.float32)
             else:
@@ -399,7 +405,8 @@
                 summed[span, :] = before + product
                 term[(degree + 1) % 2, span, :] = product.astype(jnp.bfloat16)
             else:
-                out[span, :] = (before + product).astype(jnp.bfloat16)
+                done = out if step + 1 == matrices.shape[0] else begun
+                done[span, :] = (before + product).astype(jnp.bfloat16)
 
 
 def taylor(mode, me, jobs, joint, parts, across, starts, columns):
@@ -412,11 +419,11 @@
         in_specs=[SMEM] * 2 + [ANY] * (1 + len(parts) + len(across) + len(starts)),
         out_specs=VMEM,
         scratch_shapes=[
-            pltpu.VMEM((rows, rows), jnp.bfloat16),
+            pltpu.VMEM((1 + (mode == "large"), rows, rows), jnp.bfloat16),
             pltpu.VMEM((rows, columns), jnp.bfloat16),
             pltpu.VMEM((rows, columns), jnp.float32),
             pltpu.VMEM((2, rows, columns), jnp.bfloat16),
-            pltpu.SemaphoreType.DMA((devices // 4,)),
+            pltpu.SemaphoreType.DMA(((1 + (mode == "large")) * (devices // 4),)),
             pltpu.SemaphoreType.DMA,
         ],
         cost_estimate=pl.CostEstimate(
@@ -429,8 +436,10 @@
 
 
 def select_kernel(small, kept, place, base, returned, *refs):
-    out = refs[-1]
+    before, refs = (refs[0], refs[1:]) if kept else (None, refs)
+    out, blank, semaphore = refs
     devices = returned.shape[0]
+    blank[...] = jnp.zeros(blank.shape, blank.dtype)
 
     def one(slot, carry):
         chain = place[slot] - base[0]
@@ -441,15 +450,17 @@
 
         @pl.when(hit)
         def _():
-            out[slot] = returned[owner]
+            pltpu.make_async_copy(returned.at[owner], out.at[slot], semaphore).start()
 
         @pl.when(jnp.logical_not(hit))
         def _():
-            out[slot] = refs[0][slot] if kept else jnp.zeros(out.shape[1:], out.dtype)
+            source = before.at[slot] if kept else blank
+            pltpu.make_async_copy(source, out.at[slot], semaphore).start()
 
         return carry
 
     lax.fori_loop(0, out.shape[0], one, 0)
+    pltpu.make_async_copy(out, out, semaphore).wait()
 
 
 def select(place, base, returned, before, small):
@@ -459,7 +470,11 @@
         functools.partial(select_kernel, small, kept),
         out_shape=jax.ShapeDtypeStruct(shape, returned.dtype),
         in_specs=[SMEM] * 2 + [VMEM] * (1 + kept),
-        out_specs=VMEM,
+        out_specs=ANY,
+        scratch_shapes=[
+            pltpu.VMEM(returned.shape[1:], returned.dtype),
+            pltpu.SemaphoreType.DMA,
+        ],
         compiler_params=params(),
     )(place, base, returned, *((before,) if kept else ()))
 
@@ -508,8 +523,7 @@
             starts = [current, twin, moved]
             advanced = taylor("small", me, jobs, joint, parts, across, starts, columns)
         else:
-            current = taylor("first", me, jobs, joint, [], [], [], columns)
-            advanced = taylor("large", me, jobs, joint, [], [], [current], columns)
+            advanced = taylor("large", me, jobs, joint, [], [], [], columns)
         returned = exchange(advanced.reshape(devices, local_rows, columns))
         return select(owned if small else place, base, returned, before, small)
 

time: 165 us -> 165 us (level)
  no operation moved by 1% of the time
where the time goes in v5:
time: 165 us; the launch traced here: 163 us
  starting transfers between devices  57.8 us (35%)
  waiting for transfers between devices  41.1 us (25%)
  Pallas kernels  31.2 us (19%)
  blocking collectives  27.5 us (17%)
  local copies, waits for them, and re-layouts  3.38 us (2%)
    ppermute x22, starting transfers between devices, swap(): return lax.ppermute(array, 'row', pairs)  51 us
    all_to_all x1, waiting for transfers between devices, exchange(): return lax.all_to_all(array, 'row', split_axis=0, concat_axis=0, tiled=True)  36 us
    all_to_all x1, blocking collectives, exchange(): return lax.all_to_all(array, 'row', split_axis=0, concat_axis=0, tiled=True)  27.5 us
    pallas_call x2, Pallas kernels, potential_rows(): pl.pallas_call(functools.partial(potential_kernel, kind, step, per_device...  17.5 us
    pallas_call x2, Pallas kernels, taylor(): pl.pallas_call(functools.partial(taylor_kernel, mode, chips), out_shape=j...  9.2 us
    all_to_all x1, starting transfers between devices, exchange(): return lax.all_to_all(array, 'row', split_axis=0, concat_axis=0, tiled=True)  6.84 us
    ppermute x22, waiting for transfers between devices, swap(): return lax.ppermute(array, 'row', pairs)  5.15 us
  transfers between devices with their start and end apart: 23, of which 4 were waited for; matrix products, arithmetic and copies ran while one was open for 0% of the time, Pallas kernels for 8%

profile of v5, /device:TPU:9, one launch (start us, length us, event | category | flops | bytes accessed | tf_op | source)
XLA Modules:
  0.0 163.2 jit_solution(14342008485814048218)
XLA Ops:
  0.0 0.8 reshape.30
  0.8 0.7 collective-permute-start.17
  1.4 0.8 collective-permute-done.17
  2.3 1.2 collective-permute-start.18
  3.5 3.0 %shard_map.67 = (s32[2,32]{1,0:T(2,128)}, s32[32]{0:T(128)}, s32[4,16]{1,0:T(4,128)S(1)}, s32[32]{0:T(128)}, s32[2]{0:T(128)S(1)}) custom-call(s32[16]{0:T(128)} %counts.1, s32[2,32]{1,0:T(2,128)} %sources.1), custom_call_target="tpu_custom_call" | custom-call | tf_op jit(solution)/shard_map/pallas_call | solution.py:145
  6.5 0.0 collective-permute-done.18
  6.5 1.4 collective-permute-start.21
  7.9 1.1 collective-permute-start.20
  9.0 1.1 collective-permute-start.19
  10.1 0.6 fusion
  12.0 0.0 collective-permute-done.21
  12.1 0.0 collective-permute-done.20
  12.1 0.0 collective-permute-done.19
  12.1 150.9 %conditional.1 = (bf16[32,64,256]{2,1,0:T(8,128)(2,1)}) conditional(s32[]{:T(128)} %bitcast.5, (s32[1]{0:T(128)}, s32[4,16]{1,0:T(4,128)S(1)}, s32[2,64]{1,0:T(2,128)}, bf16[4,256]{1,0:T(4,128)(2,1)S(1)}, bf16[4,256]{1,0:T(4,128)(2,1)S(1)}, /*index=5*/bf16[4,256]{1,0:T(4,128)(2,1)S(1)}, bf16[4,256]{1,0:T(4,128)(2,1)S(1)}, ...), branch_computations={%region_0.1_spmd, %region_1.2_spmd, %region_2.5_spmd} | conditional | flops 8589934592 | bytes 59774440 | solution.py:544
  12.1 0.0 copy-start.9
  12.1 11.9 %branch_0_fun.5 = bf16[16,64,1280]{2,1,0:T(8,128)(2,1)} custom-call(s32[1]{0:T(128)} %get-tuple-element.132.me, s32[4,16]{1,0:T(4,128)S(1)} %get-tuple-element.133.jobs, s32[1]{0:T(128)} %constant.35.clone.base, s32[2,64]{1,0:T(2,128)} %get-tuple-element.134.slab, bf16[4,256]{1,0:T(4,128)(2,1)S(1)} %get-tuple-element.135.refs_0_, ...), custom_call_target="tpu_custom_call" | custom-call | flops 3221225472 | bytes 18874368 | tf_op jit(solution)/shard_map/cond/branch_0_fun/pallas_call | solution.py:308
  24.0 0.0 copy-start.6
  24.0 6.8 %all-to-all-start = ((bf16[16,64,1280]{2,1,0:T(8,128)(2,1)}), bf16[16,64,1280]{2,1,0:T(8,128)(2,1)S(1)}, u32[]{:S(2)}, u32[]{:S(2)}) async-start(bf16[16,64,1280]{2,1,0:T(8,128)(2,1)} %branch_0_fun.5), calls=%async_computation | async-start | bytes 5242880 | tf_op jit(solution)/shard_map/cond/branch_0_fun/all_to_all | solution.py:548
  30.9 5.6 %branch_0_fun.6 = (bf16[64,1024]{1,0:T(8,128)(2,1)S(1)}, bf16[64,1024]{1,0:T(8,128)(2,1)}, bf16[64,1024]{1,0:T(8,128)(2,1)}, bf16[64,1024]{1,0:T(8,128)(2,1)}, b...) custom-call(s32[1]{0:T(128)} %get-tuple-element.132.me, ...), custom_call_target="tpu_custom_call" | custom-call | flops 1073741824 | bytes 9437184 | tf_op jit(solution)/shard_map/cond/branch_0_fun/pallas_call | solution.py:308
  36.5 0.0 copy-start
  36.5 0.6 copy-done
  37.2 0.6 copy-done.2
  37.8 0.7 copy-done.4
  38.5 2.4 %collective-permute-start.7 = (bf16[64,1024]{1,0:T(8,128)(2,1)S(1)}, bf16[64,1024]{1,0:T(8,128)(2,1)S(1)}, u32[]{:S(2)}, u32[]{:S(2)}) collective-permute-start(bf16[64,1024]{1,0:T(8,128)(2,1)S(1)} %get-tuple-element.141.refs_0_), channel_id=1, source_target_pairs={{1,0},{3,2},{5,4},{7,6},{9,8},{11,10},{13,12},{15,14},{17,16},{19,... | collective-permute-start | bytes 393224 | tf_op jit(solution)/shard_map/cond/branch_0_fun/ppermute | solution.py:484
  40.9 2.4 %collective-permute-start.8 = (bf16[64,1024]{1,0:T(8,128)(2,1)}, bf16[64,1024]{1,0:T(8,128)(2,1)S(1)}, u32[]{:S(2)}, u32[]{:S(2)}) collective-permute-start(bf16[64,1024]{1,0:T(8,128)(2,1)} %get-tuple-element.142), channel_id=1, source_target_pairs={{1,2},{3,0},{5,6},{7,4},{9,10},{11,8},{13,14},{15,12},{17,18},{19,... | collective-permute-start | bytes 393224 | tf_op jit(solution)/shard_map/cond/branch_0_fun/ppermute | solution.py:484
  43.3 0.7 collective-permute-start
  43.9 3.1 %collective-permute-start.9 = (bf16[64,1024]{1,0:T(8,128)(2,1)}, bf16[64,1024]{1,0:T(8,128)(2,1)S(1)}, u32[]{:S(2)}, u32[]{:S(2)}) collective-permute-start(bf16[64,1024]{1,0:T(8,128)(2,1)} %get-tuple-element.143), channel_id=1, source_target_pairs={{1,4},{3,6},{5,0},{7,2},{9,12},{11,14},{13,8},{15,10},{17,20},{19,... | collective-permute-start | bytes 393224 | tf_op jit(solution)/shard_map/cond/branch_0_fun/ppermute | solution.py:484
  47.0 0.7 collective-permute-start.1
  47.7 0.0 collective-permute-done.7.refs_8_
  47.7 4.7 %collective-permute-start.10 = (bf16[64,1024]{1,0:T(8,128)(2,1)}, bf16[64,1024]{1,0:T(8,128)(2,1)}, u32[]{:S(2)}, u32[]{:S(2)}) collective-permute-start(bf16[64,1024]{1,0:T(8,128)(2,1)} %get-tuple-element.144), channel_id=1, source_target_pairs={{1,6},{3,4},{5,2},{7,0},{9,14},{11,12},{13,10},{15,8},{17,22},{19,... | collective-permute-start | bytes 393224 | tf_op jit(solution)/shard_map/cond/branch_0_fun/ppermute | solution.py:484
  52.4 36.0 %all-to-all-done.joint = bf16[16,64,1280]{2,1,0:T(8,128)(2,1)S(1)} async-done(((bf16[16,64,1280]{2,1,0:T(8,128)(2,1)}), bf16[16,64,1280]{2,1,0:T(8,128)(2,1)S(1)}, u32[]{:S(2)}, u32[]{:S(2)}) %all-to-all-start) | async-done | bytes 2621472 | tf_op jit(solution)/shard_map/cond/branch_0_fun/all_to_all | solution.py:548
  88.4 4.6 %branch_0_fun.7.refs_16_ = bf16[1024,256]{1,0:T(8,128)(2,1)S(1)} custom-call(s32[1]{0:T(128)} %get-tuple-element.132.me, s32[4,16]{1,0:T(4,128)} %copy-done.9, bf16[16,64,1280]{2,1,0:T(8,128)(2,1)S(1)} %all-to-all-done.joint), custom_call_target="tpu_custom_call" | custom-call | flops 2147483648 | bytes 3670016 | tf_op jit(solution)/shard_map/cond/branch_0_fun/pallas_call | solution.py:416
  93.0 0.0 collective-permute-done.8.refs_9_
  93.0 4.3 %collective-permute-start.16 = (bf16[1024,256]{1,0:T(8,128)(2,1)S(1)}, bf16[1024,256]{1,0:T(8,128)(2,1)S(1)}, u32[]{:S(2)}, u32[]{:S(2)}) collective-permute-start(bf16[1024,256]{1,0:T(8,128)(2,1)S(1)} %branch_0_fun.7.refs_16_), channel_id=1, source_target_pairs={{1,3},{5,7},{9,11},{13,15},{17,19},{21,23},{25,27},{29,31}} | collective-permute-start | bytes 1572872 | tf_op jit(solution)/shard_map/cond/branch_0_fun/ppermute | solution.py:484
  97.3 0.0 collective-permute-done.refs_1_
  97.3 1.3 collective-permute-start.15
  98.6 0.0 collective-permute-done.9.refs_10_
  98.6 0.7 collective-permute-start.2
  99.3 0.0 collective-permute-done.1.refs_2_
  99.3 6.3 %collective-permute-start.11 = (bf16[64,1024]{1,0:T(8,128)(2,1)S(1)}, bf16[64,1024]{1,0:T(8,128)(2,1)S(1)}, u32[]{:S(2)}, u32[]{:S(2)}) collective-permute-start(bf16[64,1024]{1,0:T(8,128)(2,1)S(1)} %copy-done.5), channel_id=1, source_target_pairs={{1,8},{3,10},{5,12},{7,14},{9,0},{11,2},{13,4},{15,6},{17,24},{19,... | collective-permute-start | bytes 393224 | tf_op jit(solution)/shard_map/cond/branch_0_fun/ppermute | solution.py:484
  105.6 0.0 collective-permute-done.10.refs_11_
  105.6 0.7 collective-permute-start.3
  106.3 0.0 collective-permute-done.2.refs_3_
  106.3 0.0 copy-done.3
  106.3 4.5 %collective-permute-start.12 = (bf16[64,1024]{1,0:T(8,128)(2,1)S(1)}, bf16[64,1024]{1,0:T(8,128)(2,1)S(1)}, u32[]{:S(2)}, u32[]{:S(2)}) collective-permute-start(bf16[64,1024]{1,0:T(8,128)(2,1)S(1)} %copy-done.3), channel_id=1, source_target_pairs={{1,10},{3,8},{5,14},{7,12},{9,2},{11,0},{13,6},{15,4},{17,26},{19,... | collective-permute-start | bytes 393224 | tf_op jit(solution)/shard_map/cond/branch_0_fun/ppermute | solution.py:484
  110.8 0.3 collective-permute-done.11.refs_12_
  111.1 0.7 collective-permute-start.4
  111.8 0.0 collective-permute-done.3.refs_4_
  111.8 6.3 %collective-permute-start.13 = (bf16[64,1024]{1,0:T(8,128)(2,1)S(1)}, bf16[64,1024]{1,0:T(8,128)(2,1)S(1)}, u32[]{:S(2)}, u32[]{:S(2)}) collective-permute-start(bf16[64,1024]{1,0:T(8,128)(2,1)S(1)} %copy-done.1), channel_id=1, source_target_pairs={{1,12},{3,14},{5,8},{7,10},{9,4},{11,6},{13,0},{15,2},{17,28},{19,... | collective-permute-start | bytes 393224 | tf_op jit(solution)/shard_map/cond/branch_0_fun/ppermute | solution.py:484
  118.1 0.0 collective-permute-done.12.refs_13_
  118.1 0.7 collective-permute-start.5
  118.8 0.0 collective-permute-done.4.refs_5_
  118.8 5.7 %collective-permute-start.14 = (bf16[64,1024]{1,0:T(8,128)(2,1)S(1)}, bf16[64,1024]{1,0:T(8,128)(2,1)S(1)}, u32[]{:S(2)}, u32[]{:S(2)}) collective-permute-start(bf16[64,1024]{1,0:T(8,128)(2,1)S(1)} %get-tuple-element.148), channel_id=1, source_target_pairs={{1,14},{3,12},{5,10},{7,8},{9,6},{11,4},{13,2},{15,0},{17,30},{19,... | collective-permute-start | bytes 393224 | tf_op jit(solution)/shard_map/cond/branch_0_fun/ppermute | solution.py:484
  124.5 0.0 collective-permute-done.13.refs_14_
  124.5 0.7 collective-permute-start.6
  125.2 0.0 collective-permute-done.5.refs_6_
  125.2 4.0 %collective-permute-done.14.refs_15_ = bf16[64,1024]{1,0:T(8,128)(2,1)S(1)} collective-permute-done((bf16[64,1024]{1,0:T(8,128)(2,1)S(1)}, bf16[64,1024]{1,0:T(8,128)(2,1)S(1)}, u32[]{:S(2)}, u32[]{:S(2)}) %collective-permute-start.14) | collective-permute-done | bytes 131104 | tf_op jit(solution)/shard_map/cond/branch_0_fun/ppermute | solution.py:484
  129.2 0.0 collective-permute-done.6.refs_7_
  129.2 0.0 collective-permute-done.16.refs_18_
  129.2 0.0 collective-permute-done.15.refs_17_
  129.2 4.6 %branch_0_fun.8 = bf16[1024,256]{1,0:T(8,128)(2,1)S(1)} custom-call(s32[1]{0:T(128)} %get-tuple-element.132.me, s32[4,16]{1,0:T(4,128)S(1)} %copy-done.10, bf16[16,64,1280]{2,1,0:T(8,128)(2,1)S(1)} %all-to-all-done.joint, bf16[64,1024]{1,0:T(8,128)(2,1)S(1)} %get-tuple-element.141.refs_0_, bf16[64,1024]{1,0:T(8,128)(2,1)S(1)} %collective-permute-done.refs_1_, ...), custom_call_target="tpu_custom_call" | custom-call | flops 2147483648 | bytes 3670016 | tf_op jit(solution)/shard_map/cond/branch_0_fun/pallas_call | solution.py:416
  133.8 27.5 %all_to_all.28.returned = bf16[16,64,256]{2,1,0:T(8,128)(2,1)S(1)} all-to-all(bf16[16,64,256]{2,1,0:T(8,128)(2,1)S(1)} %bitcast.12), channel_id=1, replica_groups=mesh['groups'=2,'row'=16] {'row'}, dimensions={0} | all-to-all | bytes 1048576 | tf_op jit(solution)/shard_map/cond/branch_0_fun/all_to_all | solution.py:548
  161.3 0.0 copy-done.11
  161.3 1.5 branch_0_fun.9
  (14 shorter events, 0.0 us)
Async XLA Ops:
  0.8 1.5 collective-permute-start.17
  2.3 4.2 %collective-permute-start.18 = (bf16[2,256]{1,0:T(2,128)(2,1)S(1)}, bf16[2,256]{1,0:T(2,128)(2,1)S(1)}, u32[]{:S(2)}, u32[]{:S(2)}) collective-permute-start(bf16[2,256]{1,0:T(2,128)(2,1)S(1)} %pad_maximum_fusion.1), channel_id=1, source_target_pairs={{0,2},{1,3},{2,0},{3,1},{4,6},{5,7},{6,4},{7,5},{8,10},{9,11},{10,... | collective-permute-start | bytes 3080 | tf_op jit(solution)/shard_map/ppermute | solution.py:484
  6.5 5.5 %collective-permute-start.21 = (bf16[4,256]{1,0:T(4,128)(2,1)S(1)}, bf16[4,256]{1,0:T(4,128)(2,1)S(1)}, u32[]{:S(2)}, u32[]{:S(2)}) collective-permute-start(bf16[4,256]{1,0:T(4,128)(2,1)S(1)} %pad_maximum_fusion), channel_id=1, source_target_pairs={{0,12},{1,13},{2,14},{3,15},{4,8},{5,9},{6,10},{7,11},{8,4},{9,5},... | collective-permute-start | bytes 6152 | tf_op jit(solution)/shard_map/ppermute | solution.py:484
  7.9 4.2 %collective-permute-start.20 = (bf16[4,256]{1,0:T(4,128)(2,1)S(1)}, bf16[4,256]{1,0:T(4,128)(2,1)S(1)}, u32[]{:S(2)}, u32[]{:S(2)}) collective-permute-start(bf16[4,256]{1,0:T(4,128)(2,1)S(1)} %pad_maximum_fusion), channel_id=1, source_target_pairs={{0,8},{1,9},{2,10},{3,11},{4,12},{5,13},{6,14},{7,15},{8,0},{9,1},... | collective-permute-start | bytes 6152 | tf_op jit(solution)/shard_map/ppermute | solution.py:484
  9.0 3.1 %collective-permute-start.19 = (bf16[4,256]{1,0:T(4,128)(2,1)S(1)}, bf16[4,256]{1,0:T(4,128)(2,1)S(1)}, u32[]{:S(2)}, u32[]{:S(2)}) collective-permute-start(bf16[4,256]{1,0:T(4,128)(2,1)S(1)} %pad_maximum_fusion), channel_id=1, source_target_pairs={{0,4},{1,5},{2,6},{3,7},{4,0},{5,1},{6,2},{7,3},{8,12},{9,13},{10,... | collective-permute-start | bytes 6152 | tf_op jit(solution)/shard_map/ppermute | solution.py:484
  12.1 18.8 %copy-start.9 = (s32[4,16]{1,0:T(4,128)}, s32[4,16]{1,0:T(4,128)S(1)}, u32[]{:S(2)}) copy-start(s32[4,16]{1,0:T(4,128)S(1)} %get-tuple-element.133.jobs) | copy-start | bytes 772 | tf_op jit(solution)/shard_map/cond
  24.0 6.9 %copy-start.6 = (s32[2,64]{1,0:T(2,128)S(1)}, s32[2,64]{1,0:T(2,128)}, u32[]{:S(2)}) copy-start(s32[2,64]{1,0:T(2,128)} %get-tuple-element.134.slab) | copy-start | bytes 1540 | tf_op jit(solution)/shard_map/cond
  24.0 64.3 %all-to-all-start = ((bf16[16,64,1280]{2,1,0:T(8,128)(2,1)}), bf16[16,64,1280]{2,1,0:T(8,128)(2,1)S(1)}, u32[]{:S(2)}, u32[]{:S(2)}) async-start(bf16[16,64,1280]{2,1,0:T(8,128)(2,1)} %branch_0_fun.5), calls=%async_computation | async-start | bytes 5242880 | tf_op jit(solution)/shard_map/cond/branch_0_fun/all_to_all | solution.py:548
  36.5 0.6 copy-start
  37.2 0.6 copy-start.2
  37.8 0.7 copy-start.4
  38.5 90.7 %copy-start.10 = (s32[4,16]{1,0:T(4,128)S(1)}, s32[4,16]{1,0:T(4,128)}, u32[]{:S(2)}) copy-start(s32[4,16]{1,0:T(4,128)} %copy-done.9) | copy-start | bytes 772 | tf_op jit(solution)/shard_map/cond
  38.5 9.2 %collective-permute-start.7 = (bf16[64,1024]{1,0:T(8,128)(2,1)S(1)}, bf16[64,1024]{1,0:T(8,128)(2,1)S(1)}, u32[]{:S(2)}, u32[]{:S(2)}) collective-permute-start(bf16[64,1024]{1,0:T(8,128)(2,1)S(1)} %get-tuple-element.141.refs_0_), channel_id=1, source_target_pairs={{1,0},{3,2},{5,4},{7,6},{9,8},{11,10},{13,12},{15,14},{17,16},{19,... | collective-permute-start | bytes 393224 | tf_op jit(solution)/shard_map/cond/branch_0_fun/ppermute | solution.py:484
  40.9 52.1 %collective-permute-start.8 = (bf16[64,1024]{1,0:T(8,128)(2,1)}, bf16[64,1024]{1,0:T(8,128)(2,1)S(1)}, u32[]{:S(2)}, u32[]{:S(2)}) collective-permute-start(bf16[64,1024]{1,0:T(8,128)(2,1)} %get-tuple-element.142), channel_id=1, source_target_pairs={{1,2},{3,0},{5,6},{7,4},{9,10},{11,8},{13,14},{15,12},{17,18},{19,... | collective-permute-start | bytes 393224 | tf_op jit(solution)/shard_map/cond/branch_0_fun/ppermute | solution.py:484
  43.3 54.1 %collective-permute-start = (bf16[64,1024]{1,0:T(8,128)(2,1)}, bf16[64,1024]{1,0:T(8,128)(2,1)S(1)}, u32[]{:S(2)}, u32[]{:S(2)}) collective-permute-start(bf16[64,1024]{1,0:T(8,128)(2,1)} %get-tuple-element.142), channel_id=1, source_target_pairs={{0,2},{2,0},{4,6},{6,4},{8,10},{10,8},{12,14},{14,12},{16,18},{18,... | collective-permute-start | bytes 393224 | tf_op jit(solution)/shard_map/cond/branch_0_fun/ppermute | solution.py:484
  43.9 54.7 %collective-permute-start.9 = (bf16[64,1024]{1,0:T(8,128)(2,1)}, bf16[64,1024]{1,0:T(8,128)(2,1)S(1)}, u32[]{:S(2)}, u32[]{:S(2)}) collective-permute-start(bf16[64,1024]{1,0:T(8,128)(2,1)} %get-tuple-element.143), channel_id=1, source_target_pairs={{1,4},{3,6},{5,0},{7,2},{9,12},{11,14},{13,8},{15,10},{17,20},{19,... | collective-permute-start | bytes 393224 | tf_op jit(solution)/shard_map/cond/branch_0_fun/ppermute | solution.py:484
  47.0 52.3 %collective-permute-start.1 = (bf16[64,1024]{1,0:T(8,128)(2,1)}, bf16[64,1024]{1,0:T(8,128)(2,1)S(1)}, u32[]{:S(2)}, u32[]{:S(2)}) collective-permute-start(bf16[64,1024]{1,0:T(8,128)(2,1)} %get-tuple-element.143), channel_id=1, source_target_pairs={{0,4},{2,6},{4,0},{6,2},{8,12},{10,14},{12,8},{14,10},{16,20},{18,... | collective-permute-start | bytes 393224 | tf_op jit(solution)/shard_map/cond/branch_0_fun/ppermute | solution.py:484
  47.7 57.9 %collective-permute-start.10 = (bf16[64,1024]{1,0:T(8,128)(2,1)}, bf16[64,1024]{1,0:T(8,128)(2,1)}, u32[]{:S(2)}, u32[]{:S(2)}) collective-permute-start(bf16[64,1024]{1,0:T(8,128)(2,1)} %get-tuple-element.144), channel_id=1, source_target_pairs={{1,6},{3,4},{5,2},{7,0},{9,14},{11,12},{13,10},{15,8},{17,22},{19,... | collective-permute-start | bytes 393224 | tf_op jit(solution)/shard_map/cond/branch_0_fun/ppermute | solution.py:484
  88.3 11.0 %copy-start.5 = (bf16[64,1024]{1,0:T(8,128)(2,1)S(1)}, bf16[64,1024]{1,0:T(8,128)(2,1)}, u32[]{:S(2)}) copy-start(bf16[64,1024]{1,0:T(8,128)(2,1)} %copy-done.4) | copy-start | bytes 393220 | tf_op jit(solution)/shard_map/cond
  88.4 18.0 %copy-start.3 = (bf16[64,1024]{1,0:T(8,128)(2,1)S(1)}, bf16[64,1024]{1,0:T(8,128)(2,1)}, u32[]{:S(2)}) copy-start(bf16[64,1024]{1,0:T(8,128)(2,1)} %copy-done.2) | copy-start | bytes 393220 | tf_op jit(solution)/shard_map/cond
  88.4 23.4 %copy-start.1 = (bf16[64,1024]{1,0:T(8,128)(2,1)S(1)}, bf16[64,1024]{1,0:T(8,128)(2,1)}, u32[]{:S(2)}) copy-start(bf16[64,1024]{1,0:T(8,128)(2,1)} %copy-done) | copy-start | bytes 393220 | tf_op jit(solution)/shard_map/cond
  93.0 68.3 %copy-start.11 = (s32[32]{0:T(128)S(1)}, s32[32]{0:T(128)}, u32[]{:S(2)}) copy-start(s32[32]{0:T(128)} %get-tuple-element.130.place) | copy-start | bytes 388 | tf_op jit(solution)/shard_map/cond
  93.0 36.2 %collective-permute-start.16 = (bf16[1024,256]{1,0:T(8,128)(2,1)S(1)}, bf16[1024,256]{1,0:T(8,128)(2,1)S(1)}, u32[]{:S(2)}, u32[]{:S(2)}) collective-permute-start(bf16[1024,256]{1,0:T(8,128)(2,1)S(1)} %branch_0_fun.7.refs_16_), channel_id=1, source_target_pairs={{1,3},{5,7},{9,11},{13,15},{17,19},{21,23},{25,27},{29,31}} | collective-permute-start | bytes 1572872 | tf_op jit(solution)/shard_map/cond/branch_0_fun/ppermute | solution.py:484
  97.3 31.9 %collective-permute-start.15 = (bf16[1024,256]{1,0:T(8,128)(2,1)S(1)}, bf16[1024,256]{1,0:T(8,128)(2,1)S(1)}, u32[]{:S(2)}, u32[]{:S(2)}) collective-permute-start(bf16[1024,256]{1,0:T(8,128)(2,1)S(1)} %branch_0_fun.7.refs_16_), channel_id=1, source_target_pairs={{0,1},{2,3},{4,5},{6,7},{8,9},{10,11},{12,13},{14,15},{16,17},{18,... | collective-permute-start | bytes 1572872 | tf_op jit(solution)/shard_map/cond/branch_0_fun/ppermute | solution.py:484
  98.6 7.7 %collective-permute-start.2 = (bf16[64,1024]{1,0:T(8,128)(2,1)}, bf16[64,1024]{1,0:T(8,128)(2,1)S(1)}, u32[]{:S(2)}, u32[]{:S(2)}) collective-permute-start(bf16[64,1024]{1,0:T(8,128)(2,1)} %get-tuple-element.144), channel_id=1, source_target_pairs={{0,6},{2,4},{4,2},{6,0},{8,14},{10,12},{12,10},{14,8},{16,22},{18,... | collective-permute-start | bytes 393224 | tf_op jit(solution)/shard_map/cond/branch_0_fun/ppermute | solution.py:484
  99.3 11.8 %collective-permute-start.11 = (bf16[64,1024]{1,0:T(8,128)(2,1)S(1)}, bf16[64,1024]{1,0:T(8,128)(2,1)S(1)}, u32[]{:S(2)}, u32[]{:S(2)}) collective-permute-start(bf16[64,1024]{1,0:T(8,128)(2,1)S(1)} %copy-done.5), channel_id=1, source_target_pairs={{1,8},{3,10},{5,12},{7,14},{9,0},{11,2},{13,4},{15,6},{17,24},{19,... | collective-permute-start | bytes 393224 | tf_op jit(solution)/shard_map/cond/branch_0_fun/ppermute | solution.py:484
  105.6 6.1 %collective-permute-start.3 = (bf16[64,1024]{1,0:T(8,128)(2,1)S(1)}, bf16[64,1024]{1,0:T(8,128)(2,1)S(1)}, u32[]{:S(2)}, u32[]{:S(2)}) collective-permute-start(bf16[64,1024]{1,0:T(8,128)(2,1)S(1)} %copy-done.5), channel_id=1, source_target_pairs={{0,8},{2,10},{4,12},{6,14},{8,0},{10,2},{12,4},{14,6},{16,24},{18,... | collective-permute-start | bytes 393224 | tf_op jit(solution)/shard_map/cond/branch_0_fun/ppermute | solution.py:484
  106.3 11.8 %collective-permute-start.12 = (bf16[64,1024]{1,0:T(8,128)(2,1)S(1)}, bf16[64,1024]{1,0:T(8,128)(2,1)S(1)}, u32[]{:S(2)}, u32[]{:S(2)}) collective-permute-start(bf16[64,1024]{1,0:T(8,128)(2,1)S(1)} %copy-done.3), channel_id=1, source_target_pairs={{1,10},{3,8},{5,14},{7,12},{9,2},{11,0},{13,6},{15,4},{17,26},{19,... | collective-permute-start | bytes 393224 | tf_op jit(solution)/shard_map/cond/branch_0_fun/ppermute | solution.py:484
  111.1 7.7 %collective-permute-start.4 = (bf16[64,1024]{1,0:T(8,128)(2,1)S(1)}, bf16[64,1024]{1,0:T(8,128)(2,1)S(1)}, u32[]{:S(2)}, u32[]{:S(2)}) collective-permute-start(bf16[64,1024]{1,0:T(8,128)(2,1)S(1)} %copy-done.3), channel_id=1, source_target_pairs={{0,10},{2,8},{4,14},{6,12},{8,2},{10,0},{12,6},{14,4},{16,26},{18,... | collective-permute-start | bytes 393224 | tf_op jit(solution)/shard_map/cond/branch_0_fun/ppermute | solution.py:484
  111.8 12.7 %collective-permute-start.13 = (bf16[64,1024]{1,0:T(8,128)(2,1)S(1)}, bf16[64,1024]{1,0:T(8,128)(2,1)S(1)}, u32[]{:S(2)}, u32[]{:S(2)}) collective-permute-start(bf16[64,1024]{1,0:T(8,128)(2,1)S(1)} %copy-done.1), channel_id=1, source_target_pairs={{1,12},{3,14},{5,8},{7,10},{9,4},{11,6},{13,0},{15,2},{17,28},{19,... | collective-permute-start | bytes 393224 | tf_op jit(solution)/shard_map/cond/branch_0_fun/ppermute | solution.py:484
  118.1 7.1 %collective-permute-start.5 = (bf16[64,1024]{1,0:T(8,128)(2,1)S(1)}, bf16[64,1024]{1,0:T(8,128)(2,1)S(1)}, u32[]{:S(2)}, u32[]{:S(2)}) collective-permute-start(bf16[64,1024]{1,0:T(8,128)(2,1)S(1)} %copy-done.1), channel_id=1, source_target_pairs={{0,12},{2,14},{4,8},{6,10},{8,4},{10,6},{12,0},{14,2},{16,28},{18,... | collective-permute-start | bytes 393224 | tf_op jit(solution)/shard_map/cond/branch_0_fun/ppermute | solution.py:484
  118.8 10.4 %collective-permute-start.14 = (bf16[64,1024]{1,0:T(8,128)(2,1)S(1)}, bf16[64,1024]{1,0:T(8,128)(2,1)S(1)}, u32[]{:S(2)}, u32[]{:S(2)}) collective-permute-start(bf16[64,1024]{1,0:T(8,128)(2,1)S(1)} %get-tuple-element.148), channel_id=1, source_target_pairs={{1,14},{3,12},{5,10},{7,8},{9,6},{11,4},{13,2},{15,0},{17,30},{19,... | collective-permute-start | bytes 393224 | tf_op jit(solution)/shard_map/cond/branch_0_fun/ppermute | solution.py:484
  124.5 4.7 %collective-permute-start.6 = (bf16[64,1024]{1,0:T(8,128)(2,1)S(1)}, bf16[64,1024]{1,0:T(8,128)(2,1)S(1)}, u32[]{:S(2)}, u32[]{:S(2)}) collective-permute-start(bf16[64,1024]{1,0:T(8,128)(2,1)S(1)} %get-tuple-element.148), channel_id=1, source_target_pairs={{0,14},{2,12},{4,10},{6,8},{8,6},{10,4},{12,2},{14,0},{16,30},{18,... | collective-permute-start | bytes 393224 | tf_op jit(solution)/shard_map/cond/branch_0_fun/ppermute | solution.py:484
